TPU v7x, 32 devices: a whole 2x2x4 slice. The times are simulated.
32 devices in a mesh: seq: 8 (over y, x, core), head: 4 (over z).
Axes of the slice: x: 2, y: 2, z: 4, core: 2. Of those that a mesh axis runs over, the one named last changes fastest.
Arguments:
- block_in: bfloat16 [4096, 2048], P('seq'), may hold values from -6 to 6
- pre_gain: float32 [2048], replicated, may hold values from 0.1 to 1.9
- gate_proj: bfloat16 [2048, 2560], P(None, 'head'), may hold values from -0.125 to 0.125
- input_proj: bfloat16 [2048, 2560], P(None, 'head'), may hold values from -0.125 to 0.125
- conv_taps: float32 [4, 2560], P(None, 'head'), may hold values from -3 to 3
- recur_gate: bfloat16 [16, 160, 160], P('head'), may hold values from -0.5 to 0.5
- input_gate: bfloat16 [16, 160, 160], P('head'), may hold values from -0.5 to 0.5
- decay_param: float32 [2560], P('head'), may hold values from 5 to 13
- out_proj: bfloat16 [2560, 2048], P('head'), may hold values from -0.3125 to 0.3125
- post_gain: float32 [2048], replicated, may hold values from 0.1 to 1.9
- ffn_gate: bfloat16 [2048, 6144], P(None, 'head'), may hold values from -0.125 to 0.125
- ffn_up: bfloat16 [2048, 6144], P(None, 'head'), may hold values from -0.125 to 0.125
- ffn_down: bfloat16 [6144, 2048], P('head'), may hold values from -0.109375 to 0.109375
- cotangent: bfloat16 [4096, 2048], P('seq'), may hold values from -6 to 6
Outputs:
- block_out: bfloat16 [4096, 2048], P('seq')
- grad_input: float32 [4096, 2048], P('seq')
- grad_pregain: float32 [2048], P('seq')
- grad_gateproj: float32 [2048, 2560], P('seq', 'head')
- grad_inproj: float32 [2048, 2560], P('seq', 'head')
- grad_convtaps: float32 [4, 2560], P(None, ('head', 'seq'))
- grad_recur: float32 [16, 160, 160], P('head', 'seq')
- grad_ingate: float32 [16, 160, 160], P('head', 'seq')
- grad_decay: float32 [2560], P(('head', 'seq'))
- grad_outproj: float32 [2560, 2048], P('head', 'seq')
- grad_postgain: float32 [2048], P('seq')
- grad_ffngate: float32 [2048, 6144], P('seq', 'head')
- grad_ffnup: float32 [2048, 6144], P('seq', 'head')
- grad_ffndown: float32 [6144, 2048], P('head', 'seq')
All inputs are finite; a program needn't handle non-finite values.
Results may differ from a plain program's by a relative error of at most 0.02.
Values may be sent and summed in bfloat16 or wider, within the bound.
No kernel may reach another device: no remote copies, remote signals or barrier semaphores. Data moves between devices by JAX's collectives and lax.ppermute only.
A program may use at most 256 MiB of HBM per device.

v0:
```python
import jax
import jax.numpy as jnp
from jax import lax
from jax.sharding import PartitionSpec as P

epsilon = 1e-06
sharpness = 8.0


def passed_along(value, axis, by):
    peers = lax.axis_size(axis)
    pairs = [(i, i + by) for i in range(peers) if 0 <= i + by < peers]
    return lax.ppermute(value, axis, pairs)


def entering(value, axis, combine, identity, reverse):
    peers, index = (lax.axis_size(axis), lax.axis_index(axis))
    everything = jax.tree.map(lambda part: lax.all_gather(part, axis), value)
    start = jax.tree.map(
        lambda part, zero: jnp.broadcast_to(jnp.asarray(zero, part.dtype), part.shape),
        value,
        identity,
    )

    def lap(k, before):
        at = peers - 1 - k if reverse else k
        reached = at > index if reverse else at < index
        new = combine(before, jax.tree.map(lambda part: part[at], everything))
        return jax.tree.map(lambda a, b: jnp.where(reached, a, b), new, before)

    return lax.fori_loop(0, peers, lap, start)


def rms_norm(values, scales):
    return values * lax.rsqrt(jnp.mean(values * values, axis=-1, keepdims=True) + epsilon) * scales


def gelu_tanh(values):
    return jax.nn.gelu(values, approximate=True)


def gated_product(gate_vals, other_vals):
    return gelu_tanh(gate_vals) * other_vals


def combine_pairs(former, latter):
    return (former[0] * latter[0], latter[0] * former[1] + latter[1])


def decay_terms(recur_pre, input_pre, conv_vals, decay_param):
    recur_rate = jax.nn.sigmoid(recur_pre)
    log_decay = -sharpness * recur_rate * jax.nn.softplus(-decay_param)
    decays = jnp.exp(log_decay)
    drives = jnp.sqrt(-jnp.expm1(2.0 * log_decay)) * jax.nn.sigmoid(input_pre) * conv_vals
    return (decays, drives)


def local(
    block_in,
    pre_gain,
    gate_proj,
    input_proj,
    conv_taps,
    recur_gate,
    input_gate,
    decay_param,
    out_proj,
    post_gain,
    ffn_gate,
    ffn_up,
    ffn_down,
    cotangent,
):
    tokens = block_in.shape[0]
    channels = gate_proj.shape[1]
    blocks = recur_gate.shape[0]
    block_width = recur_gate.shape[1]
    tap_count = conv_taps.shape[0]
    inputs = block_in.astype(jnp.float32)
    normed = rms_norm(inputs, pre_gain).astype(jnp.bfloat16)
    gate_pre = jnp.dot(normed, gate_proj, preferred_element_type=jnp.float32)
    branch_in = jnp.dot(normed, input_proj, preferred_element_type=jnp.float32).astype(jnp.bfloat16)
    earlier_rows = passed_along(branch_in[tokens - tap_count + 1 :], "seq", 1)
    padded = jnp.concatenate([earlier_rows, branch_in], axis=0).astype(jnp.float32)
    conv_sum = conv_taps[0] * padded[tap_count - 1 :]
    for offset in range(1, tap_count):
        conv_sum = (
            conv_sum
            + conv_taps[offset] * padded[tap_count - 1 - offset : tap_count - 1 - offset + tokens]
        )
    conv_low = conv_sum.astype(jnp.bfloat16)
    conv_vals = conv_low.astype(jnp.float32)
    grouped = conv_low.reshape(tokens, blocks, block_width)
    recur_pre = jnp.einsum(
        "tbi,bij->tbj", grouped, recur_gate, preferred_element_type=jnp.float32
    ).reshape(tokens, channels)
    input_pre = jnp.einsum(
        "tbi,bij->tbj", grouped, input_gate, preferred_element_type=jnp.float32
    ).reshape(tokens, channels)
    decays, drives = decay_terms(recur_pre, input_pre, conv_vals, decay_param)
    decay_prods, local_states = lax.associative_scan(combine_pairs, (decays, drives), axis=0)
    identity_pair = (jnp.ones((channels,), jnp.float32), jnp.zeros((channels,), jnp.float32))
    _, carry_in = entering(
        (decay_prods[-1], local_states[-1]), "seq", combine_pairs, identity_pair, False
    )
    states = local_states + decay_prods * carry_in
    mixed_low = gated_product(gate_pre, states).astype(jnp.bfloat16)
    branch_out = lax.psum(jnp.dot(mixed_low, out_proj, preferred_element_type=jnp.float32), "head")
    residual = inputs + branch_out
    normed_two = rms_norm(residual, post_gain).astype(jnp.bfloat16)
    ffn_gpre = jnp.dot(normed_two, ffn_gate, preferred_element_type=jnp.float32)
    ffn_upre = jnp.dot(normed_two, ffn_up, preferred_element_type=jnp.float32)
    hidden = gated_product(ffn_gpre, ffn_upre).astype(jnp.bfloat16)
    ffn_out = lax.psum(
        jnp.dot(hidden, ffn_down, preferred_element_type=jnp.float32).astype(jnp.bfloat16), "head"
    ).astype(jnp.float32)
    block_out = (residual + ffn_out).astype(jnp.bfloat16)
    upstream = cotangent.astype(jnp.float32)
    grad_ffndown = jnp.einsum("tf,td->fd", hidden, cotangent, preferred_element_type=jnp.float32)
    d_hidden = jnp.einsum("td,fd->tf", cotangent, ffn_down, preferred_element_type=jnp.float32)
    _, hidden_pull = jax.vjp(gated_product, ffn_gpre, ffn_upre)
    d_gpre, d_upre = hidden_pull(d_hidden)
    d_gpre = d_gpre.astype(jnp.bfloat16)
    d_upre = d_upre.astype(jnp.bfloat16)
    grad_ffngate = jnp.einsum("td,tf->df", normed_two, d_gpre, preferred_element_type=jnp.float32)
    grad_ffnup = jnp.einsum("td,tf->df", normed_two, d_upre, preferred_element_type=jnp.float32)
    d_normed_two = jnp.einsum(
        "tf,df->td", d_gpre, ffn_gate, preferred_element_type=jnp.float32
    ) + jnp.einsum("tf,df->td", d_upre, ffn_up, preferred_element_type=jnp.float32)
    d_normed_two = lax.psum(d_normed_two.astype(jnp.bfloat16), "head").astype(jnp.float32)
    _, second_pull = jax.vjp(rms_norm, residual, post_gain)
    d_resid_norm, grad_postgain = second_pull(d_normed_two)
    d_resid = upstream + d_resid_norm
    d_out_low = d_resid.astype(jnp.bfloat16)
    grad_outproj = jnp.einsum("tc,td->cd", mixed_low, d_out_low, preferred_element_type=jnp.float32)
    d_mixed = jnp.einsum("td,cd->tc", d_out_low, out_proj, preferred_element_type=jnp.float32)
    _, mixed_pull = jax.vjp(gated_product, gate_pre, states)
    d_gate_pre, d_states = mixed_pull(d_mixed)
    d_gate_low = d_gate_pre.astype(jnp.bfloat16)
    next_decays = jnp.concatenate([decays[1:], jnp.ones((1, channels), jnp.float32)], axis=0)
    suffix_prods, suffix_local = lax.associative_scan(
        combine_pairs, (next_decays, d_states), axis=0, reverse=True
    )
    _, carry_back = entering(
        (decays[0] * suffix_prods[0], decays[0] * suffix_local[0]),
        "seq",
        combine_pairs,
        identity_pair,
        True,
    )
    state_grad = suffix_local + suffix_prods * carry_back
    prev_states = jnp.concatenate([carry_in[None, :], states[:-1]], axis=0)
    _, decay_pull = jax.vjp(decay_terms, recur_pre, input_pre, conv_vals, decay_param)
    d_recur, d_input, d_conv, grad_decay = decay_pull((state_grad * prev_states, state_grad))
    d_recur_low = d_recur.astype(jnp.bfloat16).reshape(tokens, blocks, block_width)
    d_input_low = d_input.astype(jnp.bfloat16).reshape(tokens, blocks, block_width)
    grad_recur = jnp.einsum(
        "tbi,tbj->bij", grouped, d_recur_low, preferred_element_type=jnp.float32
    )
    grad_ingate = jnp.einsum(
        "tbi,tbj->bij", grouped, d_input_low, preferred_element_type=jnp.float32
    )
    gate_back = jnp.einsum(
        "tbj,bij->tbi", d_recur_low, recur_gate, preferred_element_type=jnp.float32
    ) + jnp.einsum("tbj,bij->tbi", d_input_low, input_gate, preferred_element_type=jnp.float32)
    d_conv = d_conv + gate_back.reshape(tokens, channels)
    grad_convtaps = jnp.stack(
        [
            jnp.sum(
                d_conv * padded[tap_count - 1 - offset : tap_count - 1 - offset + tokens], axis=0
            )
            for offset in range(tap_count)
        ],
        axis=0,
    )
    d_padded = jnp.pad(conv_taps[0] * d_conv, ((tap_count - 1, 0), (0, 0)))
    for offset in range(1, tap_count):
        d_padded = d_padded + jnp.pad(
            conv_taps[offset] * d_conv, ((tap_count - 1 - offset, offset), (0, 0))
        )
    later_rows = passed_along(d_padded[: tap_count - 1], "seq", -1)
    d_branch = d_padded[tap_count - 1 :] + jnp.concatenate(
        [jnp.zeros((tokens - tap_count + 1, channels), jnp.float32), later_rows], axis=0
    )
    d_branch_low = d_branch.astype(jnp.bfloat16)
    grad_gateproj = jnp.einsum("td,tc->dc", normed, d_gate_low, preferred_element_type=jnp.float32)
    grad_inproj = jnp.einsum("td,tc->dc", normed, d_branch_low, preferred_element_type=jnp.float32)
    d_normed = jnp.einsum(
        "tc,dc->td", d_gate_low, gate_proj, preferred_element_type=jnp.float32
    ) + jnp.einsum("tc,dc->td", d_branch_low, input_proj, preferred_element_type=jnp.float32)
    d_normed = lax.psum(d_normed.astype(jnp.bfloat16), "head").astype(jnp.float32)
    _, first_pull = jax.vjp(rms_norm, inputs, pre_gain)
    d_inputs_norm, grad_pregain = first_pull(d_normed)
    grad_input = d_resid + d_inputs_norm
    summed = (
        lax.psum_scatter(
            grad_pregain.astype(jnp.bfloat16), "seq", scatter_dimension=0, tiled=True
        ).astype(jnp.float32),
        lax.psum_scatter(
            grad_gateproj.astype(jnp.bfloat16), "seq", scatter_dimension=0, tiled=True
        ).astype(jnp.float32),
        lax.psum_scatter(
            grad_inproj.astype(jnp.bfloat16), "seq", scatter_dimension=0, tiled=True
        ).astype(jnp.float32),
        lax.psum_scatter(
            grad_convtaps.astype(jnp.bfloat16), "seq", scatter_dimension=1, tiled=True
        ).astype(jnp.float32),
        lax.psum_scatter(
            grad_recur.astype(jnp.bfloat16), "seq", scatter_dimension=1, tiled=True
        ).astype(jnp.float32),
        lax.psum_scatter(
            grad_ingate.astype(jnp.bfloat16), "seq", scatter_dimension=1, tiled=True
        ).astype(jnp.float32),
        lax.psum_scatter(
            grad_decay.astype(jnp.bfloat16), "seq", scatter_dimension=0, tiled=True
        ).astype(jnp.float32),
        lax.psum_scatter(
            grad_outproj.astype(jnp.bfloat16), "seq", scatter_dimension=1, tiled=True
        ).astype(jnp.float32),
        lax.psum_scatter(
            grad_postgain.astype(jnp.bfloat16), "seq", scatter_dimension=0, tiled=True
        ).astype(jnp.float32),
        lax.psum_scatter(
            grad_ffngate.astype(jnp.bfloat16), "seq", scatter_dimension=0, tiled=True
        ).astype(jnp.float32),
        lax.psum_scatter(
            grad_ffnup.astype(jnp.bfloat16), "seq", scatter_dimension=0, tiled=True
        ).astype(jnp.float32),
        lax.psum_scatter(
            grad_ffndown.astype(jnp.bfloat16), "seq", scatter_dimension=1, tiled=True
        ).astype(jnp.float32),
    )
    return (
        block_out,
        grad_input,
        summed[0],
        summed[1],
        summed[2],
        summed[3],
        summed[4],
        summed[5],
        summed[6],
        summed[7],
        summed[8],
        summed[9],
        summed[10],
        summed[11],
    )


def solution(mesh):
    placed = (
        P("seq", None),
        P(),
        P(None, "head"),
        P(None, "head"),
        P(None, "head"),
        P("head", None, None),
        P("head", None, None),
        P("head"),
        P("head", None),
        P(),
        P(None, "head"),
        P(None, "head"),
        P("head", None),
        P("seq", None),
    )
    return jax.shard_map(
        local,
        mesh=mesh,
        in_specs=placed,
        out_specs=(
            P("seq", None),
            P("seq", None),
            P("seq"),
            P("seq", "head"),
            P("seq", "head"),
            P(None, ("head", "seq")),
            P("head", "seq", None),
            P("head", "seq", None),
            P(("head", "seq")),
            P("head", "seq"),
            P("seq"),
            P("seq", "head"),
            P("seq", "head"),
            P("head", "seq"),
        ),
        check_vma=False,
    )
```

profile of v0, /device:TPU:0, one launch (start us, length us, event | category | flops | bytes accessed | tf_op | source)
XLA Modules:
  0.0 1369.6 jit_solution(15695485699709563004)
XLA Ops:
  31.7 6.1 convert_multiply_fusion.9
  182.1 4.8 pad.274
  189.1 4.8 pad.256
  197.9 4.8 pad.273
  203.5 13.5 all-gather
  219.0 4.8 pad.255
  224.6 8.1 all-gather.1
  233.2 6.9 multiply_convert_fusion.3
  244.9 155.4 %all-reduce.92.cloned.1.call-done = f32[512,2048]{1,0:T(8,128)} async-done(((f32[512,2048]{1,0:T(8,128)}), f32[512,2048]{1,0:T(8,128)}) %all-reduce.92.cloned.1.call-update) | async-done | bytes 4194320 | tf_op jit(solution)/shard_map/psum | solution.py:108
  405.9 9.3 fusion.98
  415.2 5.0 fusion.97
  420.2 10.8 multiply_convert_fusion.1
  434.5 4.6 add_convert_fusion.1
  442.6 4.3 slice.707
  455.4 5.9 slice.708
  461.3 6.0 slice.699
  467.3 5.9 slice.701
  473.2 51.7 %all-reduce.94.cloned.1.call-done = bf16[512,2048]{1,0:T(8,128)(2,1)} async-done(((bf16[512,2048]{1,0:T(8,128)(2,1)}), bf16[512,2048]{1,0:T(8,128)(2,1)}) %all-reduce.94.cloned.1.call-update) | async-done | bytes 2097168 | tf_op jit(solution)/shard_map/psum | solution.py:130
  524.9 4.9 fusion.6
  550.7 6.0 slice.703
  556.6 5.9 slice.705
  615.1 6.1 slice.769
  683.2 4.8 pad.291
  688.0 4.9 pad.309
  692.9 4.9 pad.310
  697.9 4.9 pad.292
  707.8 10.7 rev.8
  718.5 10.7 rev.9
  729.1 9.0 all-gather.3
  738.1 9.2 all-gather.2
  747.9 6.9 multiply_reduce_fusion.1
  770.1 6.9 multiply_reduce_fusion.5
  781.5 5.3 convolution_convert_fusion.3
  787.9 5.1 convolution_convert_fusion.5
  801.6 8.0 convolution_convert_fusion.6
  815.2 8.2 convolution_convert_fusion.1
  823.6 8.2 convolution_convert_fusion.2
  832.0 8.1 convolution_convert_fusion
  844.8 22.3 %all-reduce.96.cloned.1.call-done = (bf16[4,160,160]{2,0,1:T(4,128)(2,1)}, bf16[4,160,160]{2,0,1:T(4,128)(2,1)}) async-done(((bf16[4,160,160]{2,0,1:T(4,128)(2,1)}, bf16[4,160,160]{2,0,1:T(4,128)(2,1)}), (bf16[4,160,160]{2,0,1:T(4,128)(2,1)}, bf16[4,160,160]{2,0,1:T(4,128)(2,1)})) %all-reduce.96.cloned.1.call-update) | async-done | bytes 409616
  869.9 43.3 %reduce-scatter.14.cloned.1.call-done = bf16[640,256]{1,0:T(8,128)(2,1)} async-done(((bf16[640,2048]{1,0:T(8,128)(2,1)}), bf16[640,256]{1,0:T(8,128)(2,1)}) %reduce-scatter.14.cloned.1.call-update) | async-done | bytes 327696 | tf_op jit(solution)/shard_map/reduce_scatter | solution.py:217
  915.0 45.0 %reduce-scatter.10.cloned.1.call-done = bf16[256,640]{1,0:T(8,128)(2,1)} async-done(((bf16[2048,640]{1,0:T(8,128)(2,1)}), bf16[256,640]{1,0:T(8,128)(2,1)}) %reduce-scatter.10.cloned.1.call-update) | async-done | bytes 327696 | tf_op jit(solution)/shard_map/reduce_scatter | solution.py:199
  961.8 45.2 %reduce-scatter.12.cloned.1.call-done = bf16[256,640]{1,0:T(8,128)(2,1)} async-done(((bf16[2048,640]{1,0:T(8,128)(2,1)}), bf16[256,640]{1,0:T(8,128)(2,1)}) %reduce-scatter.12.cloned.1.call-update) | async-done | bytes 327696 | tf_op jit(solution)/shard_map/reduce_scatter | solution.py:202
  1008.8 156.5 %all-reduce.98.cloned.1.call-done = (bf16[512,2048]{1,0:T(8,128)(2,1)}, bf16[512,2048]{1,0:T(8,128)(2,1)}) async-done(((bf16[512,2048]{1,0:T(8,128)(2,1)}, bf16[512,2048]{1,0:T(8,128)(2,1)}), (bf16[512,2048]{1,0:T(8,128)(2,1)}, bf16[512,2048]{1,0:T(8,128)(2,1)})) %all-reduce.98.cloned.1.call-update) | async-done | bytes 4194320 | tf_op jit(solution)/shard_map/psum | solution.py:114
  1169.3 24.0 %all-reduce.84 = (bf16[2048]{0:T(1024)(128)(2,1)S(1)}, bf16[640]{0:T(1024)(128)(2,1)S(1)}, bf16[2048]{0:T(1024)(128)(2,1)S(1)}) all-reduce(bf16[2048]{0:T(1024)(128)(2,1)S(1)} %get-tuple-element.308, bf16[640]{0:T(1024)(128)(2,1)S(1)} %get-tuple-element.448, ...), channel_id=2, replica_groups=mesh['seq'=8,'head'=4] {'seq'}, use_global_device_ids=true, to_apply=%region_13.14.clone | all-reduce | flops 4736 | bytes 18944
  1195.2 5.0 add_convert_fusion.2
  1204.5 25.4 %reduce-scatter.18.cloned.1.call-done = bf16[256,1536]{1,0:T(8,128)(2,1)} async-done(((bf16[2048,1536]{1,0:T(8,128)(2,1)}), bf16[256,1536]{1,0:T(8,128)(2,1)}) %reduce-scatter.18.cloned.1.call-update) | async-done | bytes 786448 | tf_op jit(solution)/shard_map/reduce_scatter | solution.py:226
  1232.4 62.5 %reduce-scatter.16.cloned.1.call-done = bf16[256,1536]{1,0:T(8,128)(2,1)} async-done(((bf16[2048,1536]{1,0:T(8,128)(2,1)}), bf16[256,1536]{1,0:T(8,128)(2,1)}) %reduce-scatter.16.cloned.1.call-update) | async-done | bytes 786448 | tf_op jit(solution)/shard_map/reduce_scatter | solution.py:223
  1297.3 63.1 %reduce-scatter.20.cloned.1.call-done = bf16[1536,256]{1,0:T(8,128)(2,1)} async-done(((bf16[1536,2048]{1,0:T(8,128)(2,1)}), bf16[1536,256]{1,0:T(8,128)(2,1)}) %reduce-scatter.20.cloned.1.call-update) | async-done | bytes 786448 | tf_op jit(solution)/shard_map/reduce_scatter | solution.py:229
  (592 shorter events, 409.0 us)
Async XLA Ops:
  7.2 226.0 %copy-start = (bf16[2048,640]{1,0:T(8,128)(2,1)S(1)}, bf16[2048,640]{1,0:T(8,128)(2,1)}, u32[]{:S(2)}) copy-start(bf16[2048,640]{1,0:T(8,128)(2,1)} %param.20) | copy-start | bytes 7864324
  7.2 393.0 %all-reduce.92.cloned.1.call-start = ((), (), s32[]{:S(2)}) async-start(), calls=%async_computation.7 | async-start | bytes 8388608 | tf_op jit(solution)/shard_map/psum | solution.py:108
  10.1 6.1 copy-start.57
  10.1 6.1 copy-start.67
  13.8 3.2 collective-permute-start
  119.1 6.3 copy-start.70
  119.1 9.0 copy-start.68
  130.9 10.2 copy-start.72
  145.6 7.5 copy-start.65
  149.5 5.1 copy-start.63
  161.8 3.8 copy-start.42
  197.9 19.1 %copy-start.60 = (f32[1,640]{1,0:T(1,128)S(1)}, f32[1,640]{1,0:T(1,128)}, u32[]{:S(2)}) copy-start(f32[1,640]{1,0:T(1,128)} %slice.796) | copy-start | bytes 7684
  219.0 14.2 %copy-start.52 = (f32[2048]{0:T(1024)S(1)}, f32[2048]{0:T(1024)}, u32[]{:S(2)}) copy-start(f32[2048]{0:T(1024)} %param.19) | copy-start | bytes 24580
  233.2 7.8 copy-start.78
  244.8 158.9 %copy-start.51 = (f32[2048]{0:T(1024)S(1)}, f32[2048]{0:T(1024)}, u32[]{:S(2)}) copy-start(f32[2048]{0:T(1024)} %param.27) | copy-start | bytes 24580
  244.8 280.0 %all-reduce.94.cloned.1.call-start = ((), (), s32[]{:S(2)}) async-start(), calls=%async_computation.8 | async-start | bytes 4194304 | tf_op jit(solution)/shard_map/psum | solution.py:130
  403.7 11.4 slice-start
  405.8 9.3 copy-start.37
  405.9 9.3 slice-start.1
  415.2 5.1 copy-start.36
  420.2 14.3 %slice-start.2 = ((s8[6291456]{0:T(1024)(128)(4,1)}), s8[4194304]{0:T(1024)(128)(4,1)S(1)}, s32[]{:S(2)}) async-start(s8[6291456]{0:T(1024)(128)(4,1)} %bitcast.96), calls=%async_computation.20 | async-start | bytes 8388608
  439.2 404.2 %reduce-scatter.22.cloned.1.call-start = ((), (), s32[]{:S(2)}) async-start(), calls=%async_computation.15 | async-start | bytes 184320
  524.9 4.9 copy-start.4
  524.9 4.9 copy-start.13
  615.0 7.5 copy-start.71
  615.1 10.2 copy-start.69
  628.1 10.1 copy-start.73
  642.7 7.4 copy-start.66
  646.6 5.2 copy-start.64
  718.5 29.4 %copy-start.59 = (f32[1,640]{1,0:T(1,128)S(1)}, f32[1,640]{1,0:T(1,128)}, u32[]{:S(2)}) copy-start(f32[1,640]{1,0:T(1,128)} %broadcast_in_dim.7) | copy-start | bytes 7684
  747.9 7.0 copy-start.58
  747.9 7.0 copy-start.2
  747.9 7.0 copy-start.8
  747.9 7.0 copy-start.9
  777.9 89.2 %all-reduce.96.cloned.1.call-start = ((), (), s32[]{:S(2)}) async-start(), calls=%async_computation.16 | async-start | bytes 1310720
  781.4 131.7 %reduce-scatter.14.cloned.1.call-start = ((), (), s32[]{:S(2)}) async-start(), calls=%async_computation.11 | async-start | bytes 2949120 | tf_op jit(solution)/shard_map/reduce_scatter | solution.py:217
  786.8 173.2 %reduce-scatter.10.cloned.1.call-start = ((), (), s32[]{:S(2)}) async-start(), calls=%async_computation.9 | async-start | bytes 2949120 | tf_op jit(solution)/shard_map/reduce_scatter | solution.py:199
  793.0 214.0 %reduce-scatter.12.cloned.1.call-start = ((), (), s32[]{:S(2)}) async-start(), calls=%async_computation.10 | async-start | bytes 2949120 | tf_op jit(solution)/shard_map/reduce_scatter | solution.py:202
  794.8 3.2 collective-permute-start.1
  801.6 363.8 %all-reduce.98.cloned.1.call-start = ((), (), s32[]{:S(2)}) async-start(), calls=%async_computation.17 | async-start | bytes 8388608 | tf_op jit(solution)/shard_map/psum | solution.py:114
  815.0 414.9 %reduce-scatter.18.cloned.1.call-start = ((), (), s32[]{:S(2)}) async-start(), calls=%async_computation.13 | async-start | bytes 7077888 | tf_op jit(solution)/shard_map/reduce_scatter | solution.py:226
  823.5 471.4 %reduce-scatter.16.cloned.1.call-start = ((), (), s32[]{:S(2)}) async-start(), calls=%async_computation.12 | async-start | bytes 7077888 | tf_op jit(solution)/shard_map/reduce_scatter | solution.py:223
  831.8 528.7 %reduce-scatter.20.cloned.1.call-start = ((), (), s32[]{:S(2)}) async-start(), calls=%async_computation.14 | async-start | bytes 7077888 | tf_op jit(solution)/shard_map/reduce_scatter | solution.py:229
  1165.3 4.0 copy-start.56
  1165.3 29.9 %copy-start.55 = (f32[512]{0:T(512)S(1)}, f32[512]{0:T(512)}, u32[]{:S(2)}) copy-start(f32[512]{0:T(512)} %copy-done.54) | copy-start | bytes 6148
  1195.2 5.1 copy-start.7
  1195.2 5.1 copy-start.11
  1195.2 6.1 copy-start.14
  (57 other events, 131.6 us)
Sparse Core Ops, SparseCore 0:
  244.9 155.2 all-reduce.91
  439.3 85.5 all-reduce.93
  778.0 29.8 reduce-scatter.21
  811.8 55.1 all-reduce.95
  870.2 42.9 reduce-scatter.13
  916.3 43.6 reduce-scatter.9
  963.3 43.6 reduce-scatter.11
  1010.0 155.3 all-reduce.97
  1169.1 60.7 reduce-scatter.17
  1233.1 61.7 reduce-scatter.15
  1298.6 61.7 reduce-scatter.19
where the time goes:
time: 1390 us; the launch traced here: 1370 us
  waiting for transfers between devices  673 us (48%)
  local copies, waits for them, and re-layouts  335 us (24%)
  other arithmetic  161 us (12%)
  matrix products  114 us (8%)
  blocking collectives  63.7 us (5%)
  between operations  17.4 us (1%)
    psum x1, waiting for transfers between devices, local(): lax.psum(jnp.dot(hidden, ffn_down, preferred_element_type=jnp.float32).as...  156 us
    psum x1, waiting for transfers between devices, local(): lax.psum(jnp.dot(mixed_low, out_proj, preferred_element_type=jnp.float32)...  155 us
    slice x65, local copies, waits for them, and re-layouts, local(): lax.associative_scan(combine_pairs, (next_decays, d_states), axis=0, reve...  104 us
    slice x60, local copies, waits for them, and re-layouts, local(): lax.associative_scan(combine_pairs, (decays, drives), axis=0)  72.9 us
    reduce_scatter x1, waiting for transfers between devices, local(): lax.psum_scatter(grad_ffndown.astype(jnp.bfloat16), 'seq', scatter_dimens...  63.1 us
    reduce_scatter x1, waiting for transfers between devices, local(): lax.psum_scatter(grad_ffngate.astype(jnp.bfloat16), 'seq', scatter_dimens...  62.5 us
    psum x1, waiting for transfers between devices, local(): lax.psum(d_normed_two.astype(jnp.bfloat16), 'head').astype(jnp.float32)  51.7 us
    pad x32, local copies, waits for them, and re-layouts, local(): lax.associative_scan(combine_pairs, (next_decays, d_states), axis=0, reve...  50.2 us
  transfers between devices with their start and end apart: 13, of which 12 were waited for; matrix products, arithmetic and copies ran while one was open for 9% of the time, Pallas kernels for 0%

commit v1 on v0

v1 whole, which is shorter than its diff:
```python
import jax
import jax.numpy as jnp
from jax import lax
from jax.experimental import pallas as pl
from jax.experimental.pallas import tpu as pltpu
from jax.sharding import PartitionSpec as P

epsilon = 1e-06
sharpness = 8.0
segments = 8
rows_at_once = 32
root_two_over_pi = 0.7978845608028654
cubic = 0.044715
f32 = jnp.float32
bf16 = jnp.bfloat16


def call(body, out_shape, scratch, *operands, scalars=0, flops=0):
    vectors = len(operands) - scalars
    moved = sum(x.size * x.dtype.itemsize for x in (*operands, *out_shape))
    return pl.pallas_call(
        body,
        out_shape=out_shape,
        in_specs=[pl.BlockSpec(memory_space=pltpu.VMEM)] * vectors
        + [pl.BlockSpec(memory_space=pltpu.SMEM)] * scalars,
        out_specs=[pl.BlockSpec(memory_space=pltpu.VMEM)] * len(out_shape),
        scratch_shapes=scratch,
        compiler_params=pltpu.CompilerParams(vmem_limit_bytes=48 << 20),
        cost_estimate=pl.CostEstimate(flops=1000, bytes_accessed=1000, transcendentals=0),
    )(*operands)


def split(ref, at, value):
    for j in range(ref.shape[0]):
        ref[j, at, :] = value[:, 128 * j : 128 * (j + 1)]


def joined(ref, at):
    return jnp.concatenate([ref[j, at, :] for j in range(ref.shape[0])], axis=1)


def over_rows(tokens, body):
    @pl.loop(0, tokens // rows_at_once)
    def _(step):
        body(pl.multiple_of(step * rows_at_once, rows_at_once))


def minus_expm1(v):
    series = 1.0 / 5040.0
    for term in (720.0, 120.0, 24.0, 6.0, 2.0, 1.0):
        series = series * v + 1.0 / term
    return jnp.where(v > -0.25, -v * series, 1.0 - jnp.exp(v))


def gelu_parts(v):
    bent = jnp.tanh(root_two_over_pi * (v + cubic * v * v * v))
    half = 0.5 * (1.0 + bent)
    slope = half + 0.5 * v * (1.0 - bent * bent) * root_two_over_pi * (1.0 + 3.0 * cubic * v * v)
    return v * half, slope


def forward_scan(
    branch_ref, halo_ref, taps_ref, soft_ref, recur_gate_ref, input_gate_ref,
    conv_ref, recur_ref, input_ref, local_ref, prod_ref, seg_ref, end_ref, gates_ref,
    padded, pre, decay, drive,
):
    tokens, channels = branch_ref.shape
    taps = taps_ref.shape[0]
    steps = tokens // segments
    blocks, width, _ = recur_gate_ref.shape
    gates_ref[...] = jnp.zeros((channels, 2 * channels), bf16)
    for b in range(blocks):
        rows = pl.ds(b * width, width)
        gates_ref[rows, b * width : (b + 1) * width] = recur_gate_ref[b]
        gates_ref[rows, channels + b * width : channels + (b + 1) * width] = input_gate_ref[b]
    padded[0:8, :] = halo_ref[...].astype(f32)

    def fill(row):
        padded[pl.ds(row + 8, rows_at_once), :] = branch_ref[pl.ds(row, rows_at_once), :].astype(f32)

    over_rows(tokens, fill)

    def convolve(row):
        window = padded[pl.ds(row, rows_at_once + 8), :]
        total = taps_ref[0:1, :] * window[8:, :]
        for k in range(1, taps):
            total = total + taps_ref[k : k + 1, :] * window[8 - k : 8 - k + rows_at_once, :]
        conv_ref[pl.ds(row, rows_at_once), :] = total.astype(bf16)

    over_rows(tokens, convolve)
    pre[...] = jnp.dot(conv_ref[...], gates_ref[...], preferred_element_type=f32)

    def terms(row):
        at = pl.ds(row, rows_at_once)
        recur = jax.nn.sigmoid(pre[at, 0:channels])
        inward = jax.nn.sigmoid(pre[at, channels : 2 * channels])
        log_decay = -sharpness * recur * soft_ref[...]
        recur_ref[at, :] = recur
        input_ref[at, :] = inward
        split(decay, at, jnp.exp(log_decay))
        split(drive, at, jnp.sqrt(minus_expm1(2.0 * log_decay)) * inward * conv_ref[at, :].astype(f32))

    over_rows(tokens, terms)

    slabs = channels // 128

    def step(i, carried):
        at = pl.ds(i, segments, stride=steps)
        new = []
        for j in range(slabs):
            state, product = carried[j]
            a = decay[j, at, :]
            state = a * state + drive[j, at, :]
            product = a * product
            local_ref[j, at, :] = state
            prod_ref[j, at, :] = product
            new.append((state, product))
        return tuple(new)

    start = ((jnp.zeros((segments, 128), f32), jnp.ones((segments, 128), f32)),) * slabs
    last = lax.fori_loop(0, steps, step, start, unroll=4)
    state = jnp.concatenate([pair[0] for pair in last], axis=1)
    product = jnp.concatenate([pair[1] for pair in last], axis=1)
    seg_ref[0:segments, :] = product
    seg_ref[segments : 2 * segments, :] = state
    whole = jnp.ones((1, channels), f32)
    end = jnp.zeros((1, channels), f32)
    for s in range(segments):
        end = product[s : s + 1, :] * end + state[s : s + 1, :]
        whole = product[s : s + 1, :] * whole
    end_ref[0:1, :] = whole
    end_ref[1:2, :] = end


def mix(gate_ref, local_ref, prod_ref, seg_ref, ends_ref, index_ref, states_ref, mixed_ref, entry_ref):
    tokens, channels = gate_ref.shape
    steps = tokens // segments
    index = index_ref[0]
    carry = jnp.zeros((1, channels), f32)
    for j in range(ends_ref.shape[0]):
        new = ends_ref[j, 0:1, :] * carry + ends_ref[j, 1:2, :]
        carry = jnp.where(j < index, new, carry)
    entry_ref[...] = carry
    for s in range(segments):
        held = carry

        @pl.loop(0, steps // rows_at_once)
        def _(i):
            at = pl.ds(pl.multiple_of(s * steps + i * rows_at_once, rows_at_once), rows_at_once)
            states = joined(local_ref, at) + joined(prod_ref, at) * held
            states_ref[at, :] = states
            gate, _ = gelu_parts(gate_ref[at, :])
            mixed_ref[at, :] = (gate * states).astype(bf16)

        carry = seg_ref[s : s + 1, :] * carry + seg_ref[segments + s : segments + s + 1, :]


def backward_scan(
    d_mixed_ref, gate_ref, states_ref, recur_ref, soft_ref,
    d_gate_ref, local_ref, prod_ref, seg_ref, end_ref,
    decay, d_state,
):
    tokens, channels = gate_ref.shape
    steps = tokens // segments

    def terms(row):
        at = pl.ds(row, rows_at_once)
        d_mixed = d_mixed_ref[at, :].astype(f32)
        value, slope = gelu_parts(gate_ref[at, :])
        d_gate_ref[at, :] = (d_mixed * states_ref[at, :] * slope).astype(bf16)
        split(d_state, at, d_mixed * value)
        split(decay, at, jnp.exp(-sharpness * recur_ref[at, :] * soft_ref[...]))

    over_rows(tokens, terms)

    slabs = channels // 128

    def step(k, carried):
        at = pl.ds(steps - 1 - k, segments, stride=steps)
        new = []
        for j in range(slabs):
            into, reach = carried[j]
            a = decay[j, at, :]
            grad = d_state[j, at, :] + into
            local_ref[j, at, :] = grad
            prod_ref[j, at, :] = reach
            new.append((a * grad, a * reach))
        return tuple(new)

    start = ((jnp.zeros((segments, 128), f32), jnp.ones((segments, 128), f32)),) * slabs
    last = lax.fori_loop(0, steps, step, start, unroll=4)
    into = jnp.concatenate([pair[0] for pair in last], axis=1)
    reach = jnp.concatenate([pair[1] for pair in last], axis=1)
    seg_ref[0:segments, :] = reach
    seg_ref[segments : 2 * segments, :] = into
    end = jnp.zeros((1, channels), f32)
    for s in reversed(range(segments)):
        end = reach[s : s + 1, :] * end + into[s : s + 1, :]
    end_ref[...] = end


def backward_terms(
    local_ref, prod_ref, seg_ref, ends_ref, backs_ref, recur_ref, input_ref, conv_ref, states_ref, entry_ref,
    soft_ref, slide_ref, taps_ref, branch_ref, halo_ref, gates_ref, index_ref,
    d_both_ref, d_branch_ref, head_ref, decay_sum_ref, taps_sum_ref,
    before, d_conv, padded,
):
    tokens, channels = states_ref.shape
    taps = taps_ref.shape[0]
    steps = tokens // segments
    index = index_ref[0]
    padded[0:8, :] = halo_ref[...].astype(f32)
    before[0:8, :] = jnp.broadcast_to(entry_ref[...], (8, channels))
    carry = jnp.zeros((1, channels), f32)
    for j in reversed(range(ends_ref.shape[0])):
        new = ends_ref[j, 0:1, :] * carry + backs_ref[j, 0:1, :]
        carry = jnp.where(j > index, new, carry)
    decay_sum_ref[...] = jnp.zeros((8, channels), f32)
    taps_sum_ref[...] = jnp.zeros((8 * taps, channels), f32)

    def fill(row):
        padded[pl.ds(row + 8, rows_at_once), :] = branch_ref[pl.ds(row, rows_at_once), :].astype(f32)
        before[pl.ds(row + 8, rows_at_once), :] = states_ref[pl.ds(row, rows_at_once), :]

    over_rows(tokens, fill)
    for s in reversed(range(segments)):
        held = carry

        @pl.loop(0, steps // rows_at_once)
        def _(i):
            row = pl.multiple_of(s * steps + i * rows_at_once, rows_at_once)
            at = pl.ds(row, rows_at_once)
            grad = joined(local_ref, at) + joined(prod_ref, at) * held
            recur = recur_ref[at, :]
            inward = input_ref[at, :]
            conv = conv_ref[at, :].astype(f32)
            log_decay = -sharpness * recur * soft_ref[...]
            decay = jnp.exp(log_decay)
            root = jnp.sqrt(minus_expm1(2.0 * log_decay))
            previous = before[pl.ds(row, rows_at_once + 8), :][7 : 7 + rows_at_once, :]
            push = grad * inward
            total = decay * (grad * previous - push * decay * conv / root)
            rate = recur * total
            d_both_ref[at, 0:channels] = (-sharpness * soft_ref[...] * (1.0 - recur) * rate).astype(bf16)
            d_both_ref[at, channels : 2 * channels] = (push * root * conv * (1.0 - inward)).astype(bf16)
            d_conv[at, :] = push * root
            decay_sum_ref[...] += jnp.sum(rate.reshape(rows_at_once // 8, 8, channels), axis=0)

        carry = seg_ref[s : s + 1, :] * carry + seg_ref[segments + s : segments + s + 1, :]
    decay_sum_ref[...] = decay_sum_ref[...] * slide_ref[...]
    d_conv[0:tokens, :] += lax.dot_general(
        d_both_ref[...], gates_ref[...], (((1,), (1,)), ((), ())), preferred_element_type=f32
    )
    d_conv[tokens : tokens + 8, :] = jnp.zeros((8, channels), f32)
    first = jnp.concatenate([jnp.zeros((8, channels), f32), d_conv[0:8, :]], axis=0)
    head = taps_ref[0:1, :] * first[0:8, :]
    for k in range(1, taps):
        head = head + taps_ref[k : k + 1, :] * first[k : k + 8, :]
    head_ref[...] = head

    def finish(row):
        window = d_conv[pl.ds(row, rows_at_once + 8), :]
        now = window[0:rows_at_once, :]
        total = taps_ref[0:1, :] * now
        for k in range(1, taps):
            total = total + taps_ref[k : k + 1, :] * window[k : k + rows_at_once, :]
        d_branch_ref[pl.ds(row, rows_at_once), :] = total
        earlier = padded[pl.ds(row, rows_at_once + 8), :]
        for k in range(taps):
            product = now * earlier[8 - k : 8 - k + rows_at_once, :]
            taps_sum_ref[8 * k : 8 * k + 8, :] += jnp.sum(
                product.reshape(rows_at_once // 8, 8, channels), axis=0
            )

    over_rows(tokens, finish)


def place(me, own_ref, arrived, store):
    from_left, from_right, over, back, far = arrived
    for m, parts in enumerate(
        (
            (own_ref, from_right, back, far),
            (from_left, own_ref, from_right, over),
            (over, from_left, own_ref, from_right),
            (far, back, from_left, own_ref),
        )
    ):

        @pl.when(me == m)
        def _():
            for source, ref in enumerate(parts):
                store(source, ref)


def add_projection(
    own_ref, left_ref, right_ref, over_ref, back_ref, far_ref, weight_ref, inputs_ref, gain_ref, index_ref,
    residual_ref, normed_ref, inverse_ref,
    mixed, rows,
):
    tokens, channels = own_ref.shape
    columns = weight_ref.shape[2]
    step = pl.program_id(0)

    def store(source, ref):
        mixed[:, source * channels : (source + 1) * channels] = ref[...]

    @pl.when(step == 0)
    def _():
        place(index_ref[0], own_ref, (left_ref, right_ref, over_ref, back_ref, far_ref), store)

    total = inputs_ref[...].astype(f32) + jnp.dot(mixed[...], weight_ref[0], preferred_element_type=f32)
    residual_ref[...] = total
    rows[:, pl.ds(pl.multiple_of(step * columns, columns), columns)] = total

    @pl.when(step == pl.num_programs(0) - 1)
    def _():
        def normalise(row):
            at = pl.ds(row, rows_at_once)
            values = rows[at, :]
            inverse = inverse_rms(values)
            inverse_ref[at, :] = inverse
            normed_ref[at, :] = (values * inverse * gain_ref[...]).astype(bf16)

        over_rows(tokens, normalise)


def residual_norm(own, arrived, weight, inputs, gain, index):
    tokens, channels = own.shape
    blocks, depth, columns = weight.shape
    width = inputs.shape[1]

    def whole(*dims):
        return pl.BlockSpec(dims, lambda j: (0,) * len(dims))

    return pl.pallas_call(
        add_projection,
        grid=(blocks,),
        in_specs=[whole(tokens, channels)] * 6
        + [
            pl.BlockSpec((1, depth, columns), lambda j: (j, 0, 0)),
            pl.BlockSpec((tokens, columns), lambda j: (0, j)),
            whole(1, width),
            pl.BlockSpec(memory_space=pltpu.SMEM),
        ],
        out_specs=[pl.BlockSpec((tokens, columns), lambda j: (0, j)), whole(tokens, width), whole(tokens, 1)],
        out_shape=[
            jax.ShapeDtypeStruct((tokens, width), f32),
            jax.ShapeDtypeStruct((tokens, width), bf16),
            jax.ShapeDtypeStruct((tokens, 1), f32),
        ],
        scratch_shapes=[pltpu.VMEM((tokens, depth), bf16), pltpu.VMEM((tokens, width), f32)],
        compiler_params=pltpu.CompilerParams(vmem_limit_bytes=48 << 20),
        cost_estimate=pl.CostEstimate(
            flops=2 * tokens * depth * width,
            bytes_accessed=2 * (depth * width + 5 * tokens * width),
            transcendentals=0,
        ),
    )(own, *arrived, weight, inputs, gain, index)


def rotated(own, arrived, index):
    size, width = own.shape
    peers = len(arrived) + 1

    def body(*refs):
        *part_refs, index_ref, out_ref = refs
        for k, ref in enumerate(part_refs):
            source = lax.rem(index_ref[0] + (peers - k), peers)
            out_ref[pl.ds(pl.multiple_of(source * size, size), size), :] = ref[...]

    whole = jax.ShapeDtypeStruct((peers * size, width), own.dtype)
    return call(body, [whole], [], own, *arrived, index, scalars=1)[0]


def assembled(own, first, second, index, kind):
    size, width = own.shape
    peers = lax.axis_size("head")

    def body(own_ref, left_ref, right_ref, over_ref, back_ref, far_ref, index_ref, out_ref):
        def store(source, ref):
            out_ref[source * size : (source + 1) * size, :] = ref[...].astype(kind)

        place(index_ref[0], own_ref, (left_ref, right_ref, over_ref, back_ref, far_ref), store)

    return call(
        body,
        [jax.ShapeDtypeStruct((peers * size, width), kind)],
        [],
        own,
        *first,
        *second,
        index,
        scalars=1,
    )[0]


def weight_grads(products, extra=None):
    lefts = [left for left, _ in products]
    rights = [right for _, right in products]
    tokens, width = lefts[0].shape
    count = len(products)
    spans = [right.shape[1] for right in rights]
    total = sum(spans) + (0 if extra is None else extra.shape[1])
    block = 256

    def body(*refs):
        left_refs, right_refs, out_ref = refs[:count], refs[count : 2 * count], refs[-1]
        place = 0
        for left_ref, right_ref in zip(left_refs, right_refs, strict=True):
            span = right_ref.shape[1]
            out_ref[:, place : place + span] = lax.dot_general(
                left_ref[...], right_ref[...], (((0,), (0,)), ((), ())), preferred_element_type=f32
            ).astype(bf16)
            place += span
        if extra is not None:
            out_ref[:, place:] = refs[2 * count][...]

    extras = [] if extra is None else [extra]
    return pl.pallas_call(
        body,
        grid=(width // block,),
        in_specs=[pl.BlockSpec((tokens, block), lambda i: (0, i))] * count
        + [pl.BlockSpec((tokens, span), lambda i: (0, 0)) for span in spans]
        + [pl.BlockSpec((block, e.shape[1]), lambda i: (i, 0)) for e in extras],
        out_specs=pl.BlockSpec((block, total), lambda i: (i, 0)),
        out_shape=jax.ShapeDtypeStruct((width, total), bf16),
        compiler_params=pltpu.CompilerParams(vmem_limit_bytes=48 << 20),
        cost_estimate=pl.CostEstimate(
            flops=2 * tokens * width * total, bytes_accessed=2 * width * total, transcendentals=0
        ),
    )(*lefts, *rights, *extras)


def gate_grads(conv_low, d_both, taps_sums, decay_sums, blocks, owners, rows):
    channels = conv_low.shape[1]
    taps = taps_sums.shape[0] // 8
    width = channels // blocks
    patch, kept, span = width // owners, channels // owners, rows // owners
    columns = -(-2 * width // 128) * 128

    def body(conv_ref, both_ref, taps_ref, decay_ref, out_ref):
        out_ref[...] = jnp.zeros((rows, columns), bf16)
        dense = lax.dot_general(
            conv_ref[...], both_ref[...], (((0,), (0,)), ((), ())), preferred_element_type=f32
        )
        sums = [jnp.sum(taps_ref[8 * k : 8 * k + 8, :], axis=0, keepdims=True) for k in range(taps)]
        sums.append(jnp.sum(decay_ref[...], axis=0, keepdims=True))
        sums = jnp.concatenate(sums, axis=0).astype(bf16)
        for b in range(blocks):
            at = slice(b * width, (b + 1) * width)
            recur = dense[at, b * width : (b + 1) * width].astype(bf16)
            inward = dense[at, channels + b * width : channels + (b + 1) * width].astype(bf16)
            for s in range(owners):
                row = s * span + b * patch
                out_ref[row : row + patch, 0:width] = recur[s * patch : (s + 1) * patch, :]
                out_ref[row : row + patch, width : 2 * width] = inward[s * patch : (s + 1) * patch, :]
        for s in range(owners):
            row = s * span + blocks * patch
            out_ref[row : row + taps + 1, 0:kept] = sums[:, s * kept : (s + 1) * kept]

    return call(
        body,
        [jax.ShapeDtypeStruct((rows, columns), bf16)],
        [],
        conv_low,
        d_both,
        taps_sums,
        decay_sums,
        flops=4 * conv_low.shape[0] * channels * channels,
    )[0]


def shifted(count, by):
    return [(i, (i + by) % count) for i in range(count)]


def exchanged(blocks):
    peers = lax.axis_size("head")
    return [lax.ppermute(blocks(k), "head", shifted(peers, k)) for k in range(1, peers)]


def block_of(array, where, dim):
    peers = lax.axis_size("head")
    size = array.shape[dim] // peers
    return lax.dynamic_slice_in_dim(array, (where % peers) * size, size, dim)


def shard(array, where):
    return block_of(array, where, 0)


def added(first, *others):
    total = first.astype(f32)
    for part in others:
        total = total + part.astype(f32)
    return total


def line_pairs(by):
    peers = lax.axis_size("head")
    return [(i, i + by) for i in range(peers) if 0 <= i + by < peers]


def scatter_first(low):
    me = lax.axis_index("head")
    across = shard(low, me + 2)
    return (
        lax.ppermute(across, "head", [(0, 1), (1, 2)]),
        lax.ppermute(across, "head", [(3, 2), (2, 1)]),
        lax.ppermute(shard(low, 3 - me), "head", [(0, 2), (3, 1)]),
    )


def scatter_second(low, first):
    me = lax.axis_index("head")
    from_left, from_right, far = first
    none = jnp.zeros_like(far)
    to_right = added(shard(low, me + 1), from_left, jnp.where(me == 2, far, none)).astype(bf16)
    to_left = added(shard(low, me - 1), from_right, jnp.where(me == 1, far, none)).astype(bf16)
    return lax.ppermute(to_right, "head", line_pairs(1)), lax.ppermute(to_left, "head", line_pairs(-1))


def gather_first(own):
    return lax.ppermute(own, "head", line_pairs(1)), lax.ppermute(own, "head", line_pairs(-1))


def gather_second(first):
    me = lax.axis_index("head")
    from_left, from_right = first
    over = jnp.where(me == 1, from_left, from_right)
    back = jnp.where(me == 1, from_right, from_left)
    return (
        lax.ppermute(over, "head", [(1, 2), (2, 1)]),
        lax.ppermute(back, "head", [(1, 0), (2, 3)]),
        lax.ppermute(over, "head", [(1, 3), (2, 0)]),
    )


def line_turn(turn, sent):
    peers = lax.axis_size("head")
    return lax.ppermute(sent, "head", [(turn - 1, turn), (peers - turn, peers - turn - 1)])


together = lax.optimization_barrier


def inverse_rms(values):
    return lax.rsqrt(jnp.mean(values * values, axis=-1, keepdims=True) + epsilon)


def norm_back(values, inverse, scales, grad):
    unit = values * inverse
    scaled = grad * scales
    inner = jnp.mean(scaled * unit, axis=-1, keepdims=True)
    return inverse * (scaled - unit * inner), jnp.sum(grad * unit, axis=0)


def local(
    block_in,
    pre_gain,
    gate_proj,
    input_proj,
    conv_taps,
    recur_gate,
    input_gate,
    decay_param,
    out_proj,
    post_gain,
    ffn_gate,
    ffn_up,
    ffn_down,
    cotangent,
):
    tokens, width = block_in.shape
    channels = gate_proj.shape[1]
    blocks, block_width, _ = recur_gate.shape
    tap_count = conv_taps.shape[0]
    hidden_units = ffn_gate.shape[1]
    seq_count, seq_index = lax.axis_size("seq"), lax.axis_index("seq")
    head_count, head_index = lax.axis_size("head"), lax.axis_index("head")
    share = tokens // head_count
    slabs = (channels // 128, tokens, 128)
    here = seq_index.astype(jnp.int32).reshape(1)
    place_index = head_index.astype(jnp.int32).reshape(1)
    forward_pairs = [(i, i + 1) for i in range(seq_count - 1)]
    backward_pairs = [(i + 1, i) for i in range(seq_count - 1)]

    def mine(rows):
        return lax.dynamic_slice_in_dim(rows, head_index * share, share, 0)

    def struct(*dims, kind=f32):
        return jax.ShapeDtypeStruct(dims, kind)

    halo_in = lax.ppermute(block_in[tokens - 8 :], "seq", forward_pairs)
    columns = width // seq_count
    column_block = lax.dynamic_slice_in_dim(out_proj, seq_index * columns, columns, 1)
    column_pieces = exchanged(lambda k: column_block)
    soft = jax.nn.softplus(-decay_param)[None, :]
    slide = sharpness * jax.nn.sigmoid(-decay_param)[None, :]

    def normalise(rows):
        values = rows.astype(f32)
        return (values * inverse_rms(values) * pre_gain).astype(bf16)

    normed = normalise(block_in)
    branch_in = jnp.dot(normed, input_proj, preferred_element_type=f32).astype(bf16)
    halo = jnp.dot(normalise(halo_in), input_proj, preferred_element_type=f32).astype(bf16)
    conv_low, recur_rate, input_rate, local_states, products, seg_ends, end, gates = call(
        forward_scan,
        [
            struct(tokens, channels, kind=bf16),
            struct(tokens, channels),
            struct(tokens, channels),
            struct(*slabs),
            struct(*slabs),
            struct(2 * segments, channels),
            struct(2, channels),
            struct(channels, 2 * channels, kind=bf16),
        ],
        [
            pltpu.VMEM((tokens + 8, channels), f32),
            pltpu.VMEM((tokens, 2 * channels), f32),
            pltpu.VMEM(slabs, f32),
            pltpu.VMEM(slabs, f32),
        ],
        branch_in,
        halo,
        conv_taps,
        soft,
        recur_gate,
        input_gate,
        flops=4 * tokens * channels * channels,
    )
    ends = lax.all_gather(end, "seq")
    column_pieces, ends = together((column_pieces, ends))
    projection = lax.all_gather(rotated(column_block, column_pieces, place_index), "seq")
    if columns % 128:
        projection = jnp.moveaxis(projection, 0, 1).reshape(1, head_count * channels, width)
    gate_pre = jnp.dot(normed, gate_proj, preferred_element_type=f32)
    states, mixed_low, entry = call(
        mix,
        [struct(tokens, channels), struct(tokens, channels, kind=bf16), struct(1, channels)],
        [],
        gate_pre,
        local_states,
        products,
        seg_ends,
        ends,
        here,
        scalars=1,
    )
    first = gather_first(mixed_low)
    second = gather_second(first)
    d_hidden = jnp.einsum("td,fd->tf", cotangent, ffn_down, preferred_element_type=f32)
    second, d_hidden = together((second, d_hidden))
    residual, normed_two, inverse_two = residual_norm(
        mixed_low,
        (*first, *second),
        projection,
        block_in,
        post_gain[None, :],
        place_index,
    )
    ffn_gpre = jnp.dot(normed_two, ffn_gate, preferred_element_type=f32)
    ffn_upre = jnp.dot(normed_two, ffn_up, preferred_element_type=f32)
    value, slope = gelu_parts(ffn_gpre)
    hidden = (value * ffn_upre).astype(bf16)
    d_gpre = (d_hidden * ffn_upre * slope).astype(bf16)
    d_upre = (d_hidden * value).astype(bf16)
    d_normed_two = jnp.einsum(
        "tf,df->td", d_gpre, ffn_gate, preferred_element_type=f32
    ) + jnp.einsum("tf,df->td", d_upre, ffn_up, preferred_element_type=f32)
    d_normed_two = d_normed_two.astype(bf16)
    d_normed_two, hidden, d_gpre, d_upre = together((d_normed_two, hidden, d_gpre, d_upre))
    first = scatter_first(d_normed_two)
    grad_ffn = weight_grads([(normed_two, d_gpre), (normed_two, d_upre), (cotangent, hidden)])
    first, grad_ffn = together((first, grad_ffn))
    grad_ffn = lax.psum_scatter(grad_ffn, "seq", scatter_dimension=0, tiled=True)
    second = scatter_second(d_normed_two, first)
    ffn_out = jnp.dot(hidden, ffn_down, preferred_element_type=f32).astype(bf16)
    second, ffn_out = together((second, ffn_out))
    d_normed_two = added(mine(d_normed_two), *second)
    d_norm_part, grad_postgain = norm_back(mine(residual), mine(inverse_two), post_gain, d_normed_two)
    d_resid = mine(cotangent).astype(f32) + d_norm_part
    d_out_share = d_resid.astype(bf16)
    first = gather_first(d_out_share)
    first, ffn_out = together((first, ffn_out))
    second = gather_second(first)
    half = tokens // 2
    ffn_halves = [ffn_out[:half], ffn_out[half:]]
    turn_one = [line_turn(1, ffn_halves[0])]
    d_out_low = assembled(d_out_share, first, second, place_index, bf16)
    d_out_low, ffn_halves[1] = together((d_out_low, ffn_halves[1]))
    turn_one.append(line_turn(1, ffn_halves[1]))
    d_mixed = jnp.einsum("td,cd->tc", d_out_low, out_proj, preferred_element_type=f32)
    sent = added(ffn_halves[0], turn_one[0]).astype(bf16)
    d_mixed, sent = together((d_mixed, sent))
    turn_two = [line_turn(2, sent)]
    d_gate_low, grad_local, grad_prod, grad_segs, grad_end = call(
        backward_scan,
        [
            struct(tokens, channels, kind=bf16),
            struct(*slabs),
            struct(*slabs),
            struct(2 * segments, channels),
            struct(1, channels),
        ],
        [pltpu.VMEM(slabs, f32), pltpu.VMEM(slabs, f32)],
        d_mixed,
        gate_pre,
        states,
        recur_rate,
        soft,
    )
    backs = lax.all_gather(grad_end, "seq")
    sent = added(ffn_halves[1], turn_one[1]).astype(bf16)
    backs, sent = together((backs, sent))
    turn_two.append(line_turn(2, sent))
    d_both, d_branch, head_rows, decay_sums, taps_sums = call(
        backward_terms,
        [
            struct(tokens, 2 * channels, kind=bf16),
            struct(tokens, channels),
            struct(8, channels),
            struct(8, channels),
            struct(8 * tap_count, channels),
        ],
        [
            pltpu.VMEM((tokens + 8, channels), f32),
            pltpu.VMEM((tokens + 8, channels), f32),
            pltpu.VMEM((tokens + 8, channels), f32),
        ],
        grad_local,
        grad_prod,
        grad_segs,
        ends,
        backs,
        recur_rate,
        input_rate,
        conv_low,
        states,
        entry,
        soft,
        slide,
        conv_taps,
        branch_in,
        halo,
        gates,
        here,
        scalars=1,
        flops=4 * tokens * channels * channels,
    )
    sent = added(ffn_halves[0], turn_two[0]).astype(bf16)
    head_rows, d_branch, d_both, sent = together((head_rows, d_branch, d_both, sent))
    later_rows = lax.ppermute(head_rows, "seq", backward_pairs)
    turn_three = [line_turn(3, sent)]
    d_branch_low = (d_branch + jnp.pad(later_rows, ((tokens - 8, 0), (0, 0)))).astype(bf16)
    d_normed = jnp.einsum("tc,dc->td", d_gate_low, gate_proj, preferred_element_type=f32) + jnp.einsum(
        "tc,dc->td", d_branch_low, input_proj, preferred_element_type=f32
    )
    d_normed = d_normed.astype(bf16)
    d_normed, conv_low, d_both = together((d_normed, conv_low, d_both))
    first = scatter_first(d_normed)
    packed = gate_grads(conv_low, d_both, taps_sums, decay_sums, blocks, seq_count, width)
    grad_rest = weight_grads([(normed, d_gate_low), (normed, d_branch_low), (d_out_low, mixed_low)], packed)
    first, grad_rest, turn_three, turn_two = together((first, grad_rest, turn_three, turn_two))
    second = scatter_second(d_normed, first)
    sent = added(ffn_halves[1], turn_two[1]).astype(bf16)
    second, sent = together((second, sent))
    turn_three.append(line_turn(3, sent))
    grad_rest = lax.psum_scatter(grad_rest, "seq", scatter_dimension=0, tiled=True)
    d_normed = added(mine(d_normed), *second)
    inputs = mine(block_in).astype(f32)
    inverse_one = inverse_rms(inputs)
    d_inputs, grad_pregain = norm_back(inputs, inverse_one, pre_gain, d_normed)
    grad_input = d_resid + d_inputs
    first = gather_first(grad_input.astype(bf16))
    gains = jnp.stack([grad_pregain, grad_postgain])
    gain_pieces = exchanged(lambda k: gains)
    second = gather_second(first)
    block_out = jnp.concatenate(
        [
            residual[half * h : half * (h + 1)] + added(ffn_halves[h], turn_one[h], turn_two[h], turn_three[h])
            for h in range(2)
        ],
        axis=0,
    ).astype(bf16)
    second, block_out = together((second, block_out))
    gains = jnp.sum(lax.all_gather(sum(gain_pieces, gains), "seq"), axis=0)
    gain_share = width // seq_count
    gains = lax.dynamic_slice_in_dim(gains, seq_index * gain_share, gain_share, 1)
    grad_ffn = grad_ffn.astype(f32)
    grad_ffn = (
        grad_ffn[:, :hidden_units],
        grad_ffn[:, hidden_units : 2 * hidden_units],
        grad_ffn[:, 2 * hidden_units :].T,
    )
    second, grad_rest, grad_ffn = together((second, grad_rest, grad_ffn))
    grad_input = assembled(grad_input, first, second, place_index, f32)
    grad_rest = grad_rest.astype(f32)
    packed = grad_rest[:, 3 * channels :]
    patch = block_width // seq_count
    kept = channels // seq_count
    small = packed[: blocks * patch, : 2 * block_width].reshape(blocks, patch, 2 * block_width)
    return (
        block_out,
        grad_input,
        gains[0],
        grad_rest[:, :channels],
        grad_rest[:, channels : 2 * channels],
        packed[blocks * patch : blocks * patch + tap_count, :kept],
        small[:, :, :block_width],
        small[:, :, block_width:],
        packed[blocks * patch + tap_count, :kept],
        grad_rest[:, 2 * channels : 3 * channels].T,
        gains[1],
        *grad_ffn,
    )


def solution(mesh):
    placed = (
        P("seq", None),
        P(),
        P(None, "head"),
        P(None, "head"),
        P(None, "head"),
        P("head", None, None),
        P("head", None, None),
        P("head"),
        P("head", None),
        P(),
        P(None, "head"),
        P(None, "head"),
        P("head", None),
        P("seq", None),
    )
    return jax.shard_map(
        local,
        mesh=mesh,
        in_specs=placed,
        out_specs=(
            P("seq", None),
            P("seq", None),
            P("seq"),
            P("seq", "head"),
            P("seq", "head"),
            P(None, ("head", "seq")),
            P("head", "seq", None),
            P("head", "seq", None),
            P(("head", "seq")),
            P("head", "seq"),
            P("seq"),
            P("seq", "head"),
            P("seq", "head"),
            P("head", "seq"),
        ),
        check_vma=False,
    )
```

time: 1390 us -> 483 us (0.35)
  waiting for transfers between devices: 673 us -> 119 us
  local copies, waits for them, and re-layouts: 335 us -> 46 us
  other arithmetic: 161 us -> 34.8 us
  starting transfers between devices: 5.2 us -> 106 us
  Pallas kernels: 0 us -> 74.4 us
  matrix products: 114 us -> 51.7 us
  blocking collectives: 63.7 us -> 27.2 us
    psum x3 -> x0, waiting for transfers between devices: 363 us -> none  [the longest x1 156 us: local(): lax.psum(jnp.dot(hidden, ffn_down, preferred_element_type=jnp.float32).as...]
    reduce_scatter x6 -> x2, waiting for transfers between devices: 284 us -> 0.01 us  [the longest x1 0.01 us: local(): lax.psum_scatter(grad_ffn, 'seq', scatter_dimension=0, tiled=True)]
    slice x128 -> x8, local copies, waits for them, and re-layouts: 178 us -> 9.01 us  [the longest x1 2.22 us: local(): grad_rest[:, channels:2 * channels]]
    ppermute x2 -> x39, waiting for transfers between devices: 2.07 us -> 119 us  [the longest x3 43.3 us: gather_second(): lax.ppermute(back, 'head', [(1, 0), (2, 3)])]
    ppermute x2 -> x39, starting transfers between devices: 3.78 us -> 106 us  [the longest x2 24.3 us: scatter_second(): lax.ppermute(to_right, 'head', line_pairs(1))]
    pad x64 -> x0, local copies, waits for them, and re-layouts: 100 us -> none  [the longest x32 50.2 us: local(): lax.associative_scan(combine_pairs, (next_decays, d_states), axis=0, reve...]
    pallas_call x0 -> x11, Pallas kernels: none -> 74.4 us  [the longest x8 33.8 us: call(): pl.pallas_call(body, out_shape=out_shape, in_specs=[pl.BlockSpec(memory_s...]
    add x51 -> x0, other arithmetic: 61.7 us -> none  [the longest x18 20.4 us: local(): lax.associative_scan(combine_pairs, (next_decays, d_states), axis=0, reve...]
  transfers between devices with their start and end apart: 13 -> 42, of which waited for: 12 -> 15; matrix products, arithmetic and copies ran while one was open for 9% -> 15% of each run, Pallas kernels for 0% -> 11%
where the time goes in v1:
time: 483 us; the launch traced here: 474 us
  waiting for transfers between devices  119 us (25%)
  starting transfers between devices  106 us (22%)
  Pallas kernels  74.4 us (15%)
  matrix products  51.7 us (11%)
  local copies, waits for them, and re-layouts  46 us (10%)
  other arithmetic  34.8 us (7%)
  blocking collectives  27.2 us (6%)
  between operations  15 us (3%)
    ppermute x3, waiting for transfers between devices, gather_second(): lax.ppermute(back, 'head', [(1, 0), (2, 3)])  43.3 us
    pallas_call x8, Pallas kernels, call(): pl.pallas_call(body, out_shape=out_shape, in_specs=[pl.BlockSpec(memory_s...  33.8 us
    ppermute x6, waiting for transfers between devices, line_turn(): lax.ppermute(sent, 'head', [(turn - 1, turn), (peers - turn, peers - turn...  29.2 us
    unnamed x130, local copies, waits for them, and re-layouts  29.1 us
    pallas_call x2, Pallas kernels, weight_grads(): pl.pallas_call(body, grid=(width // block,), in_specs=[pl.BlockSpec((toke...  25.4 us
    ppermute x2, starting transfers between devices, scatter_second(): lax.ppermute(to_right, 'head', line_pairs(1))  24.3 us
    ppermute x3, waiting for transfers between devices, gather_first(): lax.ppermute(own, 'head', line_pairs(-1))  21.3 us
    ppermute x3, starting transfers between devices, gather_first(): lax.ppermute(own, 'head', line_pairs(1))  16.3 us
  transfers between devices with their start and end apart: 42, of which 15 were waited for; matrix products, arithmetic and copies ran while one was open for 15% of the time, Pallas kernels for 11%

profile of v1, /device:TPU:0, one launch (start us, length us, event | category | flops | bytes accessed | tf_op | source)
XLA Modules:
  0.0 474.2 jit_solution(10170261663542697728)
XLA Ops:
  9.1 5.0 %collective-permute-start.3 = (bf16[640,256]{1,0:T(8,128)(2,1)}, bf16[640,256]{1,0:T(8,128)(2,1)}, u32[]{:S(2)}, u32[]{:S(2)}) collective-permute-start(bf16[640,256]{1,0:T(8,128)(2,1)} %constant_dynamic-slice_fusion.5.refs_0_), channel_id=1, source_target_pairs={{0,3},{1,0},{2,1},{3,2},{4,7},{5,4},{6,5},{7,6},{8,11},{9,8},{10,9... | collective-permute-start | bytes 983048 | tf_op jit(solution)/shard_map/ppermute | solution.py:479
  22.9 9.8 %shard_map.245 = (bf16[512,640]{1,0:T(8,128)(2,1)S(1)}, f32[512,640]{1,0:T(8,128)S(1)}, f32[512,640]{1,0:T(8,128)S(1)}, f32[5,512,128]{2,1,0:T(8,128)S(1)}, f32[...) custom-call(bf16[512,640]{1,0:T(8,128)(2,1)S(1)} %convolution_convert_fusion.1.bra, ...), custom_call_target="tpu_custom_call" | custom-call | flops 1000 | bytes 1000 | tf_op jit(solution)/shard_map/pallas_call | solution.py:21
  36.7 9.8 %all-gather.4.ends_ref = f32[8,2,640]{2,1,0:T(2,128)S(1)} all-gather(f32[1,2,640]{2,1,0:T(2,128)S(1)} %bitcast.42), channel_id=2, replica_groups=mesh['seq'=8,'head'=4] {'seq'}, dimensions={0}, use_global_device_ids=true | all-gather | bytes 46080 | tf_op jit(solution)/shard_map/all_gather | solution.py:634
  49.1 4.3 fusion.41.gate_ref
  57.4 5.9 %collective-permute-start.4 = (bf16[512,640]{1,0:T(8,128)(2,1)}, bf16[512,640]{1,0:T(8,128)(2,1)}, u32[]{:S(2)}, u32[]{:S(2)}) collective-permute-start(bf16[512,640]{1,0:T(8,128)(2,1)} %get-tuple-element.99.own_ref.refs_5_), channel_id=1, source_target_pairs={{0,1},{1,2},{2,3},{4,5},{5,6},{6,7},{8,9},{9,10},{10,11},{12,13},{... | collective-permute-start | bytes 1966088 | tf_op jit(solution)/shard_map/ppermute | solution.py:524
  63.3 12.7 %collective-permute-done.5.right_ref = bf16[512,640]{1,0:T(8,128)(2,1)} collective-permute-done((bf16[512,640]{1,0:T(8,128)(2,1)}, bf16[512,640]{1,0:T(8,128)(2,1)}, u32[]{:S(2)}, u32[]{:S(2)}) %collective-permute-start.5) | collective-permute-done | bytes 655392 | tf_op jit(solution)/shard_map/ppermute | solution.py:524
  82.1 7.9 %fusion.42 = f32[512,1536]{1,0:T(8,128)} fusion(bf16[512,2048]{1,0:T(8,128)(2,1)S(1)} %copy-done.54, bf16[1536,2048]{1,0:T(8,128)(2,1)} %param.26), kind=kOutput, calls=%fused_computation.99 | convolution fusion | flops 3221225472 | bytes 11534336 | tf_op jit(solution)/shard_map/td,fd->tf/dot_general | solution.py:654
  90.0 21.6 %collective-permute-done.7.back_ref = bf16[512,640]{1,0:T(8,128)(2,1)S(1)} collective-permute-done((bf16[512,640]{1,0:T(8,128)(2,1)S(1)}, bf16[512,640]{1,0:T(8,128)(2,1)S(1)}, u32[]{:S(2)}, u32[]{:S(2)}) %collective-permute-start.7) | collective-permute-done | bytes 655392 | tf_op jit(solution)/shard_map/ppermute | solution.py:534
  117.5 15.2 %shard_map.248 = (f32[512,2048]{1,0:T(8,128)}, bf16[512,2048]{1,0:T(8,128)(2,1)}, f32[512,1]{1,0:T(8,128)S(1)}) custom-call(bf16[512,640]{1,0:T(8,128)(2,1)} %get-tuple-element.99.own_ref.refs_5_, bf16[512,640]{1,0:T(8,128)(2,1)} %collective-permute-done.4.left_ref, bf16[512,640]{1,0:T(8,128)(2,1)} %collective-permute-done.5.right_ref, ...), custom_call_target="tpu_custom_call" | custom-call | flops 5368709120 | bytes 20971520 | tf_op jit(solution)/shard_map/pallas_call | solution.py:335
  132.7 6.3 %fusion.43 = f32[512,1536]{1,0:T(8,128)S(1)} fusion(bf16[512,2048]{1,0:T(8,128)(2,1)} %get-tuple-element.108.refs_0_.refs_1_, bf16[2048,1536]{1,0:T(8,128)(2,1)} %param.24), kind=kOutput, calls=%fused_computation.100 | convolution fusion | flops 3221225472 | bytes 11534336 | tf_op jit(solution)/shard_map/dot_general | solution.py:664
  139.1 5.4 %multiply_convert_fusion = (bf16[512,1536]{1,0:T(8,128)(2,1)S(1)}, bf16[512,1536]{1,0:T(8,128)(2,1)S(1)}, bf16[512,1536]{1,0:T(8,128)(2,1)S(1)}) fusion(f32[512,1536]{1,0:T(8,128)S(1)} %fusion.43, f32[512,1536]{1,0:T(8,128)S(1)} %copy-done.58, bf16[512,2048]{1,0:T(8,128)(2,1)S(1)} %copy-done.57, bf16[2048,1536]{1,0:T(8,128)(2,1)S(1)} %bitcast.52), kind=kOutput, calls=%fused_computation.16 | convolution fusion | flops 3240886272 | bytes 19398656 | tf_op jit(solution)/shard_map/dot_general | solution.py:665
  144.6 5.0 %fusion.44 = f32[512,2048]{1,0:T(8,128)} fusion(bf16[512,1536]{1,0:T(8,128)(2,1)S(1)} %get-tuple-element.111.refs_4_, bf16[2048,1536]{1,0:T(8,128)(2,1)S(1)} %bitcast.52), kind=kOutput, calls=%fused_computation.101 | convolution fusion | flops 3221225472 | bytes 12058624 | tf_op jit(solution)/shard_map/tf,df->td/dot_general | solution.py:672
  149.6 5.3 %add_convert_fusion.1 = bf16[512,2048]{1,0:T(8,128)(2,1)S(1)} fusion(f32[512,2048]{1,0:T(8,128)} %fusion.44, bf16[512,1536]{1,0:T(8,128)(2,1)S(1)} %get-tuple-element.110.refs_3_, bf16[2048,1536]{1,0:T(8,128)(2,1)S(1)} %bitcast.54), kind=kOutput, calls=%fused_computation.8 | convolution fusion | flops 3223322624 | bytes 14155776 | tf_op jit(solution)/shard_map/tf,df->td/dot_general | solution.py:670
  158.8 2.1 collective-permute-start.9
  160.9 4.0 collective-permute-start.11
  164.9 14.9 %shard_map.249 = bf16[2048,4608]{1,0:T(8,128)(2,1)} custom-call(bf16[512,2048]{1,0:T(8,128)(2,1)} %get-tuple-element.108.refs_0_.refs_1_, bf16[512,2048]{1,0:T(8,128)(2,1)} %get-tuple-element.108.refs_0_.refs_1_, bf16[512,2048]{1,0:T(8,128)(2,1)} %refs_2_.1, bf16[512,1536]{1,0:T(8,128)(2,1)S(1)} %get-tuple-element.110.refs_3_, ...), custom_call_target="tpu_custom_call" | custom-call | flops 9663676416 | bytes 18874368 | tf_op jit(solution)/shard_map/pallas_call | solution.py:419
  179.8 3.5 collective-permute-done.11
  184.7 2.2 add_convert_fusion.6
  188.2 5.9 %collective-permute-start.12 = (bf16[128,2048]{1,0:T(8,128)(2,1)S(1)}, bf16[128,2048]{1,0:T(8,128)(2,1)S(1)}, u32[]{:S(2)}, u32[]{:S(2)}) collective-permute-start(bf16[128,2048]{1,0:T(8,128)(2,1)S(1)} %get-tuple-element.232), channel_id=1, source_target_pairs={{0,1},{1,2},{2,3},{4,5},{5,6},{6,7},{8,9},{9,10},{10,11},{12,13},{... | collective-permute-start | bytes 1572872 | tf_op jit(solution)/shard_map/ppermute | solution.py:520
  194.1 7.8 %convolution_convert_fusion = bf16[512,2048]{1,0:T(8,128)(2,1)S(1)} fusion(bf16[512,1536]{1,0:T(8,128)(2,1)S(1)} %copy-done.35, bf16[1536,2048]{1,0:T(8,128)(2,1)} %param.26), kind=kOutput, calls=%fused_computation.20 | convolution fusion | flops 3222274048 | bytes 9961472 | tf_op jit(solution)/shard_map/dot_general | solution.py:680
  205.2 2.8 fusion.35
  209.3 5.1 %collective-permute-start.14 = (bf16[128,2048]{1,0:T(8,128)(2,1)S(1)}, bf16[128,2048]{1,0:T(8,128)(2,1)S(1)}, u32[]{:S(2)}, u32[]{:S(2)}) collective-permute-start(bf16[128,2048]{1,0:T(8,128)(2,1)S(1)} %get-tuple-element.222.own_ref), channel_id=1, source_target_pairs={{0,1},{1,2},{2,3},{4,5},{5,6},{6,7},{8,9},{9,10},{10,11},{12,13},{... | collective-permute-start | bytes 1572872 | tf_op jit(solution)/shard_map/ppermute | solution.py:524
  214.3 8.4 %collective-permute-done.15.right_ref = bf16[128,2048]{1,0:T(8,128)(2,1)S(1)} collective-permute-done((bf16[128,2048]{1,0:T(8,128)(2,1)S(1)}, bf16[128,2048]{1,0:T(8,128)(2,1)S(1)}, u32[]{:S(2)}, u32[]{:S(2)}) %collective-permute-start.15) | collective-permute-done | bytes 524320 | tf_op jit(solution)/shard_map/ppermute | solution.py:524
  225.0 4.4 collective-permute-start.19
  232.8 20.7 %collective-permute-done.17.back_ref = bf16[128,2048]{1,0:T(8,128)(2,1)S(1)} collective-permute-done((bf16[128,2048]{1,0:T(8,128)(2,1)S(1)}, bf16[128,2048]{1,0:T(8,128)(2,1)S(1)}, u32[]{:S(2)}, u32[]{:S(2)}) %collective-permute-start.17) | collective-permute-done | bytes 524320 | tf_op jit(solution)/shard_map/ppermute | solution.py:534
  253.7 5.3 %collective-permute-start.20 = (bf16[256,2048]{1,0:T(8,128)(2,1)S(1)}, bf16[256,2048]{1,0:T(8,128)(2,1)S(1)}, u32[]{:S(2)}, u32[]{:S(2)}) collective-permute-start(bf16[256,2048]{1,0:T(8,128)(2,1)S(1)} %get-tuple-element.132), channel_id=1, source_target_pairs={{0,1},{3,2},{4,5},{7,6},{8,9},{11,10},{12,13},{15,14},{16,17},{19,... | collective-permute-start | bytes 3145736 | tf_op jit(solution)/shard_map/ppermute | solution.py:541
  259.0 3.6 fusion.45.d_mixed_ref
  265.7 7.3 %shard_map.251 = (bf16[512,640]{1,0:T(8,128)(2,1)S(1)}, f32[5,512,128]{2,1,0:T(8,128)S(1)}, f32[5,512,128]{2,1,0:T(8,128)S(1)}, f32[16,640]{1,0:T(8,128)S(1)}, f32[1,640]{1,0:T(1,128)S(1)}) custom-call(f32[512,640]{1,0:T(8,128)S(1)} %fusion.45.d_mixed_ref, f32[512,640]{1,0:T(8,128)S(1)} %copy-done.7, f32[512,640]{1,0:T(8,128)} %copy-done.5, ...), custom_call_target="tpu_custom_call" | custom-call | flops 1000 | bytes 1000 | tf_op jit(solution)/shard_map/pallas_call | solution.py:21
  274.1 9.3 %all-gather.5.backs_ref = f32[8,1,640]{2,1,0:T(1,128)S(1)} all-gather(f32[1,1,640]{2,1,0:T(1,128)S(1)} %bitcast.43), channel_id=4, replica_groups=mesh['seq'=8,'head'=4] {'seq'}, dimensions={0}, use_global_device_ids=true | all-gather | bytes 23040 | tf_op jit(solution)/shard_map/all_gather | solution.py:715
  284.8 8.9 %shard_map.252 = (bf16[512,1280]{1,0:T(8,128)(2,1)S(1)}, f32[512,640]{1,0:T(8,128)S(1)}, f32[8,640]{1,0:T(8,128)S(1)}, f32[8,640]{1,0:T(8,128)S(1)}, f32[32,640]{1,0:T(8,128)S(1)}) custom-call(f32[5,512,128]{2,1,0:T(8,128)S(1)} %get-tuple-element.128.local_ref, f32[5,512,128]{2,1,0:T(8,128)} %copy-done.13, f32[16,640]{1,0:T(8,128)S(1)} %get-tuple-element.130.seg_ref, ...), custom_call_target="tpu_custom_call" | custom-call | flops 1000 | bytes 1000 | tf_op jit(solution)/shard_map/pallas_call | solution.py:21
  293.7 2.7 fusion.11
  306.0 7.3 %collective-permute-start.25 = (bf16[128,2048]{1,0:T(8,128)(2,1)}, bf16[128,2048]{1,0:T(8,128)(2,1)}, u32[]{:S(2)}, u32[]{:S(2)}) collective-permute-start(bf16[128,2048]{1,0:T(8,128)(2,1)} %get-tuple-element.235), channel_id=1, source_target_pairs={{0,2},{3,1},{4,6},{7,5},{8,10},{11,9},{12,14},{15,13},{16,18},{19,... | collective-permute-start | bytes 1572872 | tf_op jit(solution)/shard_map/ppermute | solution.py:510
  318.2 10.4 %shard_map.254 = bf16[2048,2304]{1,0:T(8,128)(2,1)} custom-call(bf16[512,2048]{1,0:T(8,128)(2,1)S(1)} %copy-done.2, bf16[512,2048]{1,0:T(8,128)(2,1)S(1)} %copy-done.2, bf16[512,2048]{1,0:T(8,128)(2,1)} %copy-done.3, bf16[512,640]{1,0:T(8,128)(2,1)S(1)} %get-tuple-element.127.refs_3_, bf16[512,640]{1,0:T(8,128)(2,1)S(1)} %add_convert_fusion.3.refs_4_, ...), custom_call_target="tpu_custom_call" | custom-call | flops 4831838208 | bytes 9437184 | tf_op jit(solution)/shard_map/pallas_call | solution.py:419
  328.6 7.7 %collective-permute-done.23 = bf16[128,2048]{1,0:T(8,128)(2,1)} collective-permute-done((bf16[128,2048]{1,0:T(8,128)(2,1)}, bf16[128,2048]{1,0:T(8,128)(2,1)}, u32[]{:S(2)}, u32[]{:S(2)}) %collective-permute-start.23) | collective-permute-done | bytes 524320 | tf_op jit(solution)/shard_map/ppermute | solution.py:508
  337.7 2.3 add_convert_fusion.4
  341.4 18.4 %collective-permute-start.28 = (bf16[128,2048]{1,0:T(8,128)(2,1)S(1)}, bf16[128,2048]{1,0:T(8,128)(2,1)S(1)}, u32[]{:S(2)}, u32[]{:S(2)}) collective-permute-start(bf16[128,2048]{1,0:T(8,128)(2,1)S(1)} %get-tuple-element.230), channel_id=1, source_target_pairs={{0,1},{1,2},{2,3},{4,5},{5,6},{6,7},{8,9},{9,10},{10,11},{12,13},{... | collective-permute-start | bytes 1572872 | tf_op jit(solution)/shard_map/ppermute | solution.py:520
  359.9 2.7 fusion.12
  362.6 7.3 %collective-permute-done.29 = bf16[128,2048]{1,0:T(8,128)(2,1)S(1)} collective-permute-done((bf16[128,2048]{1,0:T(8,128)(2,1)S(1)}, bf16[128,2048]{1,0:T(8,128)(2,1)S(1)}, u32[]{:S(2)}, u32[]{:S(2)}) %collective-permute-start.29) | collective-permute-done | bytes 524320 | tf_op jit(solution)/shard_map/ppermute | solution.py:520
  371.8 3.7 collective-permute-start.37
  380.5 5.3 %collective-permute-start.30 = (bf16[128,2048]{1,0:T(8,128)(2,1)}, bf16[128,2048]{1,0:T(8,128)(2,1)}, u32[]{:S(2)}, u32[]{:S(2)}) collective-permute-start(bf16[128,2048]{1,0:T(8,128)(2,1)} %get-tuple-element.220), channel_id=1, source_target_pairs={{0,1},{1,2},{2,3},{4,5},{5,6},{6,7},{8,9},{9,10},{10,11},{12,13},{... | collective-permute-start | bytes 1572872 | tf_op jit(solution)/shard_map/ppermute | solution.py:524
  387.2 8.1 %all-gather.6 = f32[8,2,2048]{2,1,0:T(2,128)S(1)} all-gather(f32[1,2,2048]{2,1,0:T(2,128)S(1)} %add_bitcast_fusion), channel_id=5, replica_groups=mesh['seq'=8,'head'=4] {'seq'}, dimensions={0}, use_global_device_ids=true | all-gather | bytes 147456 | tf_op jit(solution)/shard_map/all_gather | solution.py:789
  400.7 29.2 %collective-permute-done.35 = bf16[256,2048]{1,0:T(8,128)(2,1)} collective-permute-done((bf16[256,2048]{1,0:T(8,128)(2,1)}, bf16[256,2048]{1,0:T(8,128)(2,1)}, u32[]{:S(2)}, u32[]{:S(2)}) %collective-permute-start.35) | collective-permute-done | bytes 1048608 | tf_op jit(solution)/shard_map/ppermute | solution.py:541
  430.0 6.0 %add_convert_fusion.2 = (bf16[256,2048]{1,0:T(8,128)(2,1)S(1)}, bf16[256,2048]{1,0:T(8,128)(2,1)S(1)}) fusion(bf16[256,2048]{1,0:T(8,128)(2,1)} %collective-permute-done.26, bf16[256,2048]{1,0:T(8,128)(2,1)} %collective-permute-done.21, f32[512,2048]{1,0:T(8,128)} %get-tuple-element.118, bf16[256,2048]{1,0:T(8,128)(2,1)S(1)} %copy-done.50, ...), kind=kLoop, calls=%fused_computation.32 | loop fusion | flops 9437184 | bytes 14680064 | tf_op jit(solution)/shard_map/convert
  440.8 2.2 convert_element_type.224
  449.4 2.2 fusion.38
  454.7 2.2 copy.38
  456.8 3.0 copy.39
  464.2 3.3 shard_map.255
  (246 shorter events, 104.5 us)
Async XLA Ops:
  7.2 107.0 %all-gather.9.cloned.1.call-start = ((), (), s32[]{:S(2)}) async-start(), calls=%async_computation.4 | async-start | bytes 11796480 | tf_op jit(solution)/shard_map/all_gather | solution.py:636
  9.1 37.4 %collective-permute-start.3 = (bf16[640,256]{1,0:T(8,128)(2,1)}, bf16[640,256]{1,0:T(8,128)(2,1)}, u32[]{:S(2)}, u32[]{:S(2)}) collective-permute-start(bf16[640,256]{1,0:T(8,128)(2,1)} %constant_dynamic-slice_fusion.5.refs_0_), channel_id=1, source_target_pairs={{0,3},{1,0},{2,1},{3,2},{4,7},{5,4},{6,5},{7,6},{8,11},{9,8},{10,9... | collective-permute-start | bytes 983048 | tf_op jit(solution)/shard_map/ppermute | solution.py:479
  14.2 32.3 %collective-permute-start.2 = (bf16[640,256]{1,0:T(8,128)(2,1)}, bf16[640,256]{1,0:T(8,128)(2,1)}, u32[]{:S(2)}, u32[]{:S(2)}) collective-permute-start(bf16[640,256]{1,0:T(8,128)(2,1)} %constant_dynamic-slice_fusion.5.refs_0_), channel_id=1, source_target_pairs={{0,2},{1,3},{2,0},{3,1},{4,6},{5,7},{6,4},{7,5},{8,10},{9,11},{10,... | collective-permute-start | bytes 983048 | tf_op jit(solution)/shard_map/ppermute | solution.py:479
  14.2 32.3 %collective-permute-start.1 = (bf16[640,256]{1,0:T(8,128)(2,1)}, bf16[640,256]{1,0:T(8,128)(2,1)}, u32[]{:S(2)}, u32[]{:S(2)}) collective-permute-start(bf16[640,256]{1,0:T(8,128)(2,1)} %constant_dynamic-slice_fusion.5.refs_0_), channel_id=1, source_target_pairs={{0,1},{1,2},{2,3},{3,0},{4,5},{5,6},{6,7},{7,4},{8,9},{9,10},{10,1... | collective-permute-start | bytes 983048 | tf_op jit(solution)/shard_map/ppermute | solution.py:479
  16.0 5.9 %collective-permute-start = (bf16[8,2048]{1,0:T(8,128)(2,1)S(1)}, bf16[8,2048]{1,0:T(8,128)(2,1)S(1)}, u32[]{:S(2)}, u32[]{:S(2)}) collective-permute-start(bf16[8,2048]{1,0:T(8,128)(2,1)S(1)} %slice.58), channel_id=1, source_target_pairs={{0,4},{4,8},{8,12},{12,16},{16,20},{20,24},{24,28},{1,5},{5,9},{9,... | collective-permute-start | bytes 98312 | tf_op jit(solution)/shard_map/ppermute | solution.py:594
  49.0 391.8 %reduce-scatter.5.cloned.1.call-start = ((), (), s32[]{:S(2)}) async-start(), calls=%async_computation.3 | async-start | bytes 21233664 | tf_op jit(solution)/shard_map/reduce_scatter | solution.py:678
  56.1 19.9 %collective-permute-start.5 = (bf16[512,640]{1,0:T(8,128)(2,1)}, bf16[512,640]{1,0:T(8,128)(2,1)}, u32[]{:S(2)}, u32[]{:S(2)}) collective-permute-start(bf16[512,640]{1,0:T(8,128)(2,1)} %get-tuple-element.99.own_ref.refs_5_), channel_id=1, source_target_pairs={{1,0},{2,1},{3,2},{5,4},{6,5},{7,6},{9,8},{10,9},{11,10},{13,12},{... | collective-permute-start | bytes 1966088 | tf_op jit(solution)/shard_map/ppermute | solution.py:524
  57.4 19.8 %collective-permute-start.4 = (bf16[512,640]{1,0:T(8,128)(2,1)}, bf16[512,640]{1,0:T(8,128)(2,1)}, u32[]{:S(2)}, u32[]{:S(2)}) collective-permute-start(bf16[512,640]{1,0:T(8,128)(2,1)} %get-tuple-element.99.own_ref.refs_5_), channel_id=1, source_target_pairs={{0,1},{1,2},{2,3},{4,5},{5,6},{6,7},{8,9},{9,10},{10,11},{12,13},{... | collective-permute-start | bytes 1966088 | tf_op jit(solution)/shard_map/ppermute | solution.py:524
  78.6 33.9 %collective-permute-start.8 = (bf16[512,640]{1,0:T(8,128)(2,1)S(1)}, bf16[512,640]{1,0:T(8,128)(2,1)S(1)}, u32[]{:S(2)}, u32[]{:S(2)}) collective-permute-start(bf16[512,640]{1,0:T(8,128)(2,1)S(1)} %get-tuple-element.242), channel_id=1, source_target_pairs={{1,3},{2,0},{5,7},{6,4},{9,11},{10,8},{13,15},{14,12},{17,19},{18,... | collective-permute-start | bytes 1966088 | tf_op jit(solution)/shard_map/ppermute | solution.py:535
  79.9 33.5 %collective-permute-start.6 = (bf16[512,640]{1,0:T(8,128)(2,1)S(1)}, bf16[512,640]{1,0:T(8,128)(2,1)S(1)}, u32[]{:S(2)}, u32[]{:S(2)}) collective-permute-start(bf16[512,640]{1,0:T(8,128)(2,1)S(1)} %get-tuple-element.242), channel_id=1, source_target_pairs={{1,2},{2,1},{5,6},{6,5},{9,10},{10,9},{13,14},{14,13},{17,18},{18,... | collective-permute-start | bytes 1966088 | tf_op jit(solution)/shard_map/ppermute | solution.py:533
  80.6 31.0 %collective-permute-start.7 = (bf16[512,640]{1,0:T(8,128)(2,1)S(1)}, bf16[512,640]{1,0:T(8,128)(2,1)S(1)}, u32[]{:S(2)}, u32[]{:S(2)}) collective-permute-start(bf16[512,640]{1,0:T(8,128)(2,1)S(1)} %get-tuple-element.241), channel_id=1, source_target_pairs={{1,0},{2,3},{5,4},{6,7},{9,8},{10,11},{13,12},{14,15},{17,16},{18,... | collective-permute-start | bytes 1966088 | tf_op jit(solution)/shard_map/ppermute | solution.py:534
  157.3 26.0 %collective-permute-start.10 = (bf16[128,2048]{1,0:T(8,128)(2,1)}, bf16[128,2048]{1,0:T(8,128)(2,1)}, u32[]{:S(2)}, u32[]{:S(2)}) collective-permute-start(bf16[128,2048]{1,0:T(8,128)(2,1)} %get-tuple-element.240), channel_id=1, source_target_pairs={{3,2},{2,1},{7,6},{6,5},{11,10},{10,9},{15,14},{14,13},{19,18},{18... | collective-permute-start | bytes 1572872 | tf_op jit(solution)/shard_map/ppermute | solution.py:509
  158.8 24.5 %collective-permute-start.9 = (bf16[128,2048]{1,0:T(8,128)(2,1)}, bf16[128,2048]{1,0:T(8,128)(2,1)}, u32[]{:S(2)}, u32[]{:S(2)}) collective-permute-start(bf16[128,2048]{1,0:T(8,128)(2,1)} %get-tuple-element.240), channel_id=1, source_target_pairs={{0,1},{1,2},{4,5},{5,6},{8,9},{9,10},{12,13},{13,14},{16,17},{17,1... | collective-permute-start | bytes 1572872 | tf_op jit(solution)/shard_map/ppermute | solution.py:508
  160.9 22.4 %collective-permute-start.11 = (bf16[128,2048]{1,0:T(8,128)(2,1)}, bf16[128,2048]{1,0:T(8,128)(2,1)}, u32[]{:S(2)}, u32[]{:S(2)}) collective-permute-start(bf16[128,2048]{1,0:T(8,128)(2,1)} %get-tuple-element.239), channel_id=1, source_target_pairs={{0,2},{3,1},{4,6},{7,5},{8,10},{11,9},{12,14},{15,13},{16,18},{19,... | collective-permute-start | bytes 1572872 | tf_op jit(solution)/shard_map/ppermute | solution.py:510
  183.3 264.0 %reduce-scatter.3.cloned.1.call-start = ((), (), s32[]{:S(2)}) async-start(), calls=%async_computation.2 | async-start | bytes 10616832 | tf_op jit(solution)/shard_map/reduce_scatter | solution.py:771
  186.9 16.3 %collective-permute-start.13 = (bf16[128,2048]{1,0:T(8,128)(2,1)S(1)}, bf16[128,2048]{1,0:T(8,128)(2,1)S(1)}, u32[]{:S(2)}, u32[]{:S(2)}) collective-permute-start(bf16[128,2048]{1,0:T(8,128)(2,1)S(1)} %get-tuple-element.231), channel_id=1, source_target_pairs={{1,0},{2,1},{3,2},{5,4},{6,5},{7,6},{9,8},{10,9},{11,10},{13,12},{... | collective-permute-start | bytes 1572872 | tf_op jit(solution)/shard_map/ppermute | solution.py:520
  188.2 16.5 %collective-permute-start.12 = (bf16[128,2048]{1,0:T(8,128)(2,1)S(1)}, bf16[128,2048]{1,0:T(8,128)(2,1)S(1)}, u32[]{:S(2)}, u32[]{:S(2)}) collective-permute-start(bf16[128,2048]{1,0:T(8,128)(2,1)S(1)} %get-tuple-element.232), channel_id=1, source_target_pairs={{0,1},{1,2},{2,3},{4,5},{5,6},{6,7},{8,9},{9,10},{10,11},{12,13},{... | collective-permute-start | bytes 1572872 | tf_op jit(solution)/shard_map/ppermute | solution.py:520
  202.0 91.8 %copy-start.41 = (bf16[512,2048]{1,0:T(8,128)(2,1)}, bf16[512,2048]{1,0:T(8,128)(2,1)S(1)}, u32[]{:S(2)}) copy-start(bf16[512,2048]{1,0:T(8,128)(2,1)S(1)} %convolution_convert_fusion) | copy-start | bytes 6291460
  208.0 14.7 %collective-permute-start.15 = (bf16[128,2048]{1,0:T(8,128)(2,1)S(1)}, bf16[128,2048]{1,0:T(8,128)(2,1)S(1)}, u32[]{:S(2)}, u32[]{:S(2)}) collective-permute-start(bf16[128,2048]{1,0:T(8,128)(2,1)S(1)} %get-tuple-element.222.own_ref), channel_id=1, source_target_pairs={{1,0},{2,1},{3,2},{5,4},{6,5},{7,6},{9,8},{10,9},{11,10},{13,12},{... | collective-permute-start | bytes 1572872 | tf_op jit(solution)/shard_map/ppermute | solution.py:524
  209.3 14.6 %collective-permute-start.14 = (bf16[128,2048]{1,0:T(8,128)(2,1)S(1)}, bf16[128,2048]{1,0:T(8,128)(2,1)S(1)}, u32[]{:S(2)}, u32[]{:S(2)}) collective-permute-start(bf16[128,2048]{1,0:T(8,128)(2,1)S(1)} %get-tuple-element.222.own_ref), channel_id=1, source_target_pairs={{0,1},{1,2},{2,3},{4,5},{5,6},{6,7},{8,9},{9,10},{10,11},{12,13},{... | collective-permute-start | bytes 1572872 | tf_op jit(solution)/shard_map/ppermute | solution.py:524
  225.0 58.4 %copy-start.36 = (bf16[256,2048]{1,0:T(8,128)(2,1)}, bf16[256,2048]{1,0:T(8,128)(2,1)S(1)}, u32[]{:S(2)}) copy-start(bf16[256,2048]{1,0:T(8,128)(2,1)S(1)} %get-tuple-element.132) | copy-start | bytes 3145732
  225.0 37.6 %collective-permute-start.19 = (bf16[256,2048]{1,0:T(8,128)(2,1)}, bf16[256,2048]{1,0:T(8,128)(2,1)S(1)}, u32[]{:S(2)}, u32[]{:S(2)}) collective-permute-start(bf16[256,2048]{1,0:T(8,128)(2,1)} %get-tuple-element.237), channel_id=1, source_target_pairs={{0,1},{3,2},{4,5},{7,6},{8,9},{11,10},{12,13},{15,14},{16,17},{19,... | collective-permute-start | bytes 3145736 | tf_op jit(solution)/shard_map/ppermute | solution.py:541
  229.5 24.0 %collective-permute-start.17 = (bf16[128,2048]{1,0:T(8,128)(2,1)S(1)}, bf16[128,2048]{1,0:T(8,128)(2,1)S(1)}, u32[]{:S(2)}, u32[]{:S(2)}) collective-permute-start(bf16[128,2048]{1,0:T(8,128)(2,1)S(1)} %get-tuple-element.247), channel_id=1, source_target_pairs={{1,0},{2,3},{5,4},{6,7},{9,8},{10,11},{13,12},{14,15},{17,16},{18,... | collective-permute-start | bytes 1572872 | tf_op jit(solution)/shard_map/ppermute | solution.py:534
  230.8 22.7 %collective-permute-start.18 = (bf16[128,2048]{1,0:T(8,128)(2,1)S(1)}, bf16[128,2048]{1,0:T(8,128)(2,1)S(1)}, u32[]{:S(2)}, u32[]{:S(2)}) collective-permute-start(bf16[128,2048]{1,0:T(8,128)(2,1)S(1)} %get-tuple-element.248), channel_id=1, source_target_pairs={{1,3},{2,0},{5,7},{6,4},{9,11},{10,8},{13,15},{14,12},{17,19},{18,... | collective-permute-start | bytes 1572872 | tf_op jit(solution)/shard_map/ppermute | solution.py:535
  232.1 21.4 %collective-permute-start.16 = (bf16[128,2048]{1,0:T(8,128)(2,1)S(1)}, bf16[128,2048]{1,0:T(8,128)(2,1)S(1)}, u32[]{:S(2)}, u32[]{:S(2)}) collective-permute-start(bf16[128,2048]{1,0:T(8,128)(2,1)S(1)} %get-tuple-element.248), channel_id=1, source_target_pairs={{1,2},{2,1},{5,6},{6,5},{9,10},{10,9},{13,14},{14,13},{17,18},{18,... | collective-permute-start | bytes 1572872 | tf_op jit(solution)/shard_map/ppermute | solution.py:533
  253.7 29.7 %collective-permute-start.20 = (bf16[256,2048]{1,0:T(8,128)(2,1)S(1)}, bf16[256,2048]{1,0:T(8,128)(2,1)S(1)}, u32[]{:S(2)}, u32[]{:S(2)}) collective-permute-start(bf16[256,2048]{1,0:T(8,128)(2,1)S(1)} %get-tuple-element.132), channel_id=1, source_target_pairs={{0,1},{3,2},{4,5},{7,6},{8,9},{11,10},{12,13},{15,14},{16,17},{19,... | collective-permute-start | bytes 3145736 | tf_op jit(solution)/shard_map/ppermute | solution.py:541
  264.0 29.7 %collective-permute-start.21 = (bf16[256,2048]{1,0:T(8,128)(2,1)}, bf16[256,2048]{1,0:T(8,128)(2,1)}, u32[]{:S(2)}, u32[]{:S(2)}) collective-permute-start(bf16[256,2048]{1,0:T(8,128)(2,1)} %fusion.16), channel_id=1, source_target_pairs={{1,2},{2,1},{5,6},{6,5},{9,10},{10,9},{13,14},{14,13},{17,18},{18,... | collective-permute-start | bytes 3145736 | tf_op jit(solution)/shard_map/ppermute | solution.py:541
  296.5 6.5 %collective-permute-start.22 = (f32[8,640]{1,0:T(8,128)S(1)}, f32[8,640]{1,0:T(8,128)S(1)}, u32[]{:S(2)}, u32[]{:S(2)}) collective-permute-start(f32[8,640]{1,0:T(8,128)S(1)} %get-tuple-element.143), channel_id=1, source_target_pairs={{4,0},{8,4},{12,8},{16,12},{20,16},{24,20},{28,24},{5,1},{9,5},{13... | collective-permute-start | bytes 61448 | tf_op jit(solution)/shard_map/ppermute | solution.py:755
  300.0 28.6 %collective-permute-start.27 = (bf16[256,2048]{1,0:T(8,128)(2,1)}, bf16[256,2048]{1,0:T(8,128)(2,1)}, u32[]{:S(2)}, u32[]{:S(2)}) collective-permute-start(bf16[256,2048]{1,0:T(8,128)(2,1)} %fusion.17), channel_id=1, source_target_pairs={{1,2},{2,1},{5,6},{6,5},{9,10},{10,9},{13,14},{14,13},{17,18},{18,... | collective-permute-start | bytes 3145736 | tf_op jit(solution)/shard_map/ppermute | solution.py:541
  301.7 34.6 %collective-permute-start.26 = (bf16[256,2048]{1,0:T(8,128)(2,1)}, bf16[256,2048]{1,0:T(8,128)(2,1)}, u32[]{:S(2)}, u32[]{:S(2)}) collective-permute-start(bf16[256,2048]{1,0:T(8,128)(2,1)} %fusion.11), channel_id=1, source_target_pairs={{2,3},{1,0},{6,7},{5,4},{10,11},{9,8},{14,15},{13,12},{18,19},{17,... | collective-permute-start | bytes 3145736 | tf_op jit(solution)/shard_map/ppermute | solution.py:541
  306.0 22.5 %collective-permute-start.25 = (bf16[128,2048]{1,0:T(8,128)(2,1)}, bf16[128,2048]{1,0:T(8,128)(2,1)}, u32[]{:S(2)}, u32[]{:S(2)}) collective-permute-start(bf16[128,2048]{1,0:T(8,128)(2,1)} %get-tuple-element.235), channel_id=1, source_target_pairs={{0,2},{3,1},{4,6},{7,5},{8,10},{11,9},{12,14},{15,13},{16,18},{19,... | collective-permute-start | bytes 1572872 | tf_op jit(solution)/shard_map/ppermute | solution.py:510
  313.3 15.3 %collective-permute-start.24 = (bf16[128,2048]{1,0:T(8,128)(2,1)}, bf16[128,2048]{1,0:T(8,128)(2,1)}, u32[]{:S(2)}, u32[]{:S(2)}) collective-permute-start(bf16[128,2048]{1,0:T(8,128)(2,1)} %get-tuple-element.236), channel_id=1, source_target_pairs={{3,2},{2,1},{7,6},{6,5},{11,10},{10,9},{15,14},{14,13},{19,18},{18... | collective-permute-start | bytes 1572872 | tf_op jit(solution)/shard_map/ppermute | solution.py:509
  314.8 21.5 %collective-permute-start.23 = (bf16[128,2048]{1,0:T(8,128)(2,1)}, bf16[128,2048]{1,0:T(8,128)(2,1)}, u32[]{:S(2)}, u32[]{:S(2)}) collective-permute-start(bf16[128,2048]{1,0:T(8,128)(2,1)} %get-tuple-element.236), channel_id=1, source_target_pairs={{0,1},{1,2},{4,5},{5,6},{8,9},{9,10},{12,13},{13,14},{16,17},{17,1... | collective-permute-start | bytes 1572872 | tf_op jit(solution)/shard_map/ppermute | solution.py:508
  337.7 33.6 %copy-start.48 = (bf16[512,2048]{1,0:T(8,128)(2,1)S(1)}, bf16[512,2048]{1,0:T(8,128)(2,1)}, u32[]{:S(2)}) copy-start(bf16[512,2048]{1,0:T(8,128)(2,1)} %copy-done.47) | copy-start | bytes 6291460
  340.0 30.0 %collective-permute-start.29 = (bf16[128,2048]{1,0:T(8,128)(2,1)S(1)}, bf16[128,2048]{1,0:T(8,128)(2,1)S(1)}, u32[]{:S(2)}, u32[]{:S(2)}) collective-permute-start(bf16[128,2048]{1,0:T(8,128)(2,1)S(1)} %get-tuple-element.229), channel_id=1, source_target_pairs={{1,0},{2,1},{3,2},{5,4},{6,5},{7,6},{9,8},{10,9},{11,10},{13,12},{... | collective-permute-start | bytes 1572872 | tf_op jit(solution)/shard_map/ppermute | solution.py:520
  341.4 36.1 %copy-start.52 = (f32[128,2048]{1,0:T(8,128)S(1)}, f32[128,2048]{1,0:T(8,128)}, u32[]{:S(2)}) copy-start(f32[128,2048]{1,0:T(8,128)} %get-tuple-element.223) | copy-start | bytes 3145732
  341.4 29.9 %collective-permute-start.28 = (bf16[128,2048]{1,0:T(8,128)(2,1)S(1)}, bf16[128,2048]{1,0:T(8,128)(2,1)S(1)}, u32[]{:S(2)}, u32[]{:S(2)}) collective-permute-start(bf16[128,2048]{1,0:T(8,128)(2,1)S(1)} %get-tuple-element.230), channel_id=1, source_target_pairs={{0,1},{1,2},{2,3},{4,5},{5,6},{6,7},{8,9},{9,10},{10,11},{12,13},{... | collective-permute-start | bytes 1572872 | tf_op jit(solution)/shard_map/ppermute | solution.py:520
  371.8 14.0 %collective-permute-start.37 = (f32[2,2048]{1,0:T(2,128)S(1)}, f32[2,2048]{1,0:T(2,128)S(1)}, u32[]{:S(2)}, u32[]{:S(2)}) collective-permute-start(f32[2,2048]{1,0:T(2,128)S(1)} %pad_maximum_fusion.1), channel_id=1, source_target_pairs={{0,2},{1,3},{2,0},{3,1},{4,6},{5,7},{6,4},{7,5},{8,10},{9,11},{10,... | collective-permute-start | bytes 49160 | tf_op jit(solution)/shard_map/ppermute | solution.py:479
  375.5 11.6 %collective-permute-start.38 = (f32[2,2048]{1,0:T(2,128)S(1)}, f32[2,2048]{1,0:T(2,128)S(1)}, u32[]{:S(2)}, u32[]{:S(2)}) collective-permute-start(f32[2,2048]{1,0:T(2,128)S(1)} %pad_maximum_fusion.1), channel_id=1, source_target_pairs={{0,3},{1,0},{2,1},{3,2},{4,7},{5,4},{6,5},{7,6},{8,11},{9,8},{10,9... | collective-permute-start | bytes 49160 | tf_op jit(solution)/shard_map/ppermute | solution.py:479
  376.7 10.4 %collective-permute-start.36 = (f32[2,2048]{1,0:T(2,128)S(1)}, f32[2,2048]{1,0:T(2,128)S(1)}, u32[]{:S(2)}, u32[]{:S(2)}) collective-permute-start(f32[2,2048]{1,0:T(2,128)S(1)} %pad_maximum_fusion.1), channel_id=1, source_target_pairs={{0,1},{1,2},{2,3},{3,0},{4,5},{5,6},{6,7},{7,4},{8,9},{9,10},{10,1... | collective-permute-start | bytes 49160 | tf_op jit(solution)/shard_map/ppermute | solution.py:479
  379.2 17.0 %collective-permute-start.31 = (bf16[128,2048]{1,0:T(8,128)(2,1)}, bf16[128,2048]{1,0:T(8,128)(2,1)S(1)}, u32[]{:S(2)}, u32[]{:S(2)}) collective-permute-start(bf16[128,2048]{1,0:T(8,128)(2,1)} %get-tuple-element.220), channel_id=1, source_target_pairs={{1,0},{2,1},{3,2},{5,4},{6,5},{7,6},{9,8},{10,9},{11,10},{13,12},{... | collective-permute-start | bytes 1572872 | tf_op jit(solution)/shard_map/ppermute | solution.py:524
  380.5 15.7 %collective-permute-start.30 = (bf16[128,2048]{1,0:T(8,128)(2,1)}, bf16[128,2048]{1,0:T(8,128)(2,1)}, u32[]{:S(2)}, u32[]{:S(2)}) collective-permute-start(bf16[128,2048]{1,0:T(8,128)(2,1)} %get-tuple-element.220), channel_id=1, source_target_pairs={{0,1},{1,2},{2,3},{4,5},{5,6},{6,7},{8,9},{9,10},{10,11},{12,13},{... | collective-permute-start | bytes 1572872 | tf_op jit(solution)/shard_map/ppermute | solution.py:524
  385.8 44.1 %collective-permute-start.35 = (bf16[256,2048]{1,0:T(8,128)(2,1)}, bf16[256,2048]{1,0:T(8,128)(2,1)}, u32[]{:S(2)}, u32[]{:S(2)}) collective-permute-start(bf16[256,2048]{1,0:T(8,128)(2,1)} %fusion.12), channel_id=1, source_target_pairs={{2,3},{1,0},{6,7},{5,4},{10,11},{9,8},{14,15},{13,12},{18,19},{17,... | collective-permute-start | bytes 3145736 | tf_op jit(solution)/shard_map/ppermute | solution.py:541
  395.3 34.7 %copy-start.38 = (bf16[256,2048]{1,0:T(8,128)(2,1)S(1)}, bf16[256,2048]{1,0:T(8,128)(2,1)}, u32[]{:S(2)}) copy-start(bf16[256,2048]{1,0:T(8,128)(2,1)} %copy-done.36) | copy-start | bytes 3145732
  395.3 34.7 %copy-start.50 = (bf16[256,2048]{1,0:T(8,128)(2,1)S(1)}, bf16[256,2048]{1,0:T(8,128)(2,1)}, u32[]{:S(2)}) copy-start(bf16[256,2048]{1,0:T(8,128)(2,1)} %copy-done.49) | copy-start | bytes 3145732
  397.3 41.9 %collective-permute-start.34 = (bf16[128,2048]{1,0:T(8,128)(2,1)S(1)}, bf16[128,2048]{1,0:T(8,128)(2,1)S(1)}, u32[]{:S(2)}, u32[]{:S(2)}) collective-permute-start(bf16[128,2048]{1,0:T(8,128)(2,1)S(1)} %get-tuple-element.246), channel_id=1, source_target_pairs={{1,3},{2,0},{5,7},{6,4},{9,11},{10,8},{13,15},{14,12},{17,19},{18,... | collective-permute-start | bytes 1572872 | tf_op jit(solution)/shard_map/ppermute | solution.py:535
  398.6 41.4 %collective-permute-start.32 = (bf16[128,2048]{1,0:T(8,128)(2,1)S(1)}, bf16[128,2048]{1,0:T(8,128)(2,1)S(1)}, u32[]{:S(2)}, u32[]{:S(2)}) collective-permute-start(bf16[128,2048]{1,0:T(8,128)(2,1)S(1)} %get-tuple-element.246), channel_id=1, source_target_pairs={{1,2},{2,1},{5,6},{6,5},{9,10},{10,9},{13,14},{14,13},{17,18},{18,... | collective-permute-start | bytes 1572872 | tf_op jit(solution)/shard_map/ppermute | solution.py:533
  399.3 39.1 %collective-permute-start.33 = (bf16[128,2048]{1,0:T(8,128)(2,1)S(1)}, bf16[128,2048]{1,0:T(8,128)(2,1)S(1)}, u32[]{:S(2)}, u32[]{:S(2)}) collective-permute-start(bf16[128,2048]{1,0:T(8,128)(2,1)S(1)} %get-tuple-element.245), channel_id=1, source_target_pairs={{1,0},{2,3},{5,4},{6,7},{9,8},{10,11},{13,12},{14,15},{17,16},{18,... | collective-permute-start | bytes 1572872 | tf_op jit(solution)/shard_map/ppermute | solution.py:534
  (57 other events, 398.8 us)
Sparse Core Ops, SparseCore 0:
  49.1 62.8 all-gather.8
  183.5 127.8 reduce-scatter.4
  336.4 89.6 reduce-scatter.2

commit v2 on v1

--- a/solution.py
+++ b/solution.py
@@ -25,7 +25,7 @@
         + [pl.BlockSpec(memory_space=pltpu.SMEM)] * scalars,
         out_specs=[pl.BlockSpec(memory_space=pltpu.VMEM)] * len(out_shape),
         scratch_shapes=scratch,
-        compiler_params=pltpu.CompilerParams(vmem_limit_bytes=48 << 20),
+        compiler_params=pltpu.CompilerParams(vmem_limit_bytes=26 << 20),
         cost_estimate=pl.CostEstimate(flops=1000, bytes_accessed=1000, transcendentals=0),
     )(*operands)
 
@@ -358,20 +358,6 @@
     )(own, *arrived, weight, inputs, gain, index)
 
 
-def rotated(own, arrived, index):
-    size, width = own.shape
-    peers = len(arrived) + 1
-
-    def body(*refs):
-        *part_refs, index_ref, out_ref = refs
-        for k, ref in enumerate(part_refs):
-            source = lax.rem(index_ref[0] + (peers - k), peers)
-            out_ref[pl.ds(pl.multiple_of(source * size, size), size), :] = ref[...]
-
-    whole = jax.ShapeDtypeStruct((peers * size, width), own.dtype)
-    return call(body, [whole], [], own, *arrived, index, scalars=1)[0]
-
-
 def assembled(own, first, second, index, kind):
     size, width = own.shape
     peers = lax.axis_size("head")
@@ -431,12 +417,77 @@
     )(*lefts, *rights, *extras)
 
 
+def finish_ffn(summed, count):
+    rows, width = summed.shape
+    span = width // count
+
+    def body(in_ref, *out_refs):
+        for k, ref in enumerate(out_refs):
+            part = in_ref[:, k * span : (k + 1) * span].astype(f32)
+            ref[...] = part.T if k == count - 1 else part
+
+    shapes = [jax.ShapeDtypeStruct((rows, span), f32)] * (count - 1)
+    return call(body, [*shapes, jax.ShapeDtypeStruct((span, rows), f32)], [], summed)
+
+
+def finish_rest(summed, channels, blocks, block_width, taps, owners):
+    rows = summed.shape[0]
+    patch, kept = block_width // owners, channels // owners
+
+    def body(in_ref, gate_ref, input_ref, out_ref, taps_ref, recur_ref, inward_ref, decay_ref):
+        gate_ref[...] = in_ref[:, 0:channels].astype(f32)
+        input_ref[...] = in_ref[:, channels : 2 * channels].astype(f32)
+        out_ref[...] = in_ref[:, 2 * channels : 3 * channels].astype(f32).T
+        small = in_ref[:, 3 * channels :].astype(f32)
+        _, lanes = packed_shape(blocks, block_width, taps, owners, owners * rows)
+        groups = -(-2 * block_width // lanes)
+        for b in range(blocks):
+            parts = []
+            for g in range(groups):
+                row = (g * blocks + b) * patch
+                parts.append(small[row : row + patch, 0 : min(lanes, 2 * block_width - g * lanes)])
+            both = jnp.concatenate(parts, axis=1)
+            recur_ref[b] = both[:, 0:block_width]
+            inward_ref[b] = both[:, block_width : 2 * block_width]
+        used = groups * blocks * patch
+        taps_ref[...] = small[used : used + taps, 0:kept]
+        decay_ref[...] = small[used + taps : used + taps + 1, 0:kept]
+
+    shapes = [
+        (rows, channels),
+        (rows, channels),
+        (channels, rows),
+        (taps, kept),
+        (blocks, patch, block_width),
+        (blocks, patch, block_width),
+        (1, kept),
+    ]
+    return call(body, [jax.ShapeDtypeStruct(shape, f32) for shape in shapes], [], summed)
+
+
+def add_last(base, last):
+    cut = last[0].shape[0]
+
+    def body(base_ref, first_ref, second_ref, out_ref):
+        out_ref[0:cut, :] = (base_ref[0:cut, :] + first_ref[...].astype(f32)).astype(bf16)
+        out_ref[cut:, :] = (base_ref[cut:, :] + second_ref[...].astype(f32)).astype(bf16)
+
+    return call(body, [jax.ShapeDtypeStruct(base.shape, bf16)], [], base, *last)[0]
+
+
+def packed_shape(blocks, width, taps, owners, rows):
+    groups = -(-2 * width // 128)
+    if groups * blocks * (width // owners) + taps + 1 <= rows // owners:
+        return 128, 128
+    return groups * 128, 2 * width
+
+
 def gate_grads(conv_low, d_both, taps_sums, decay_sums, blocks, owners, rows):
     channels = conv_low.shape[1]
     taps = taps_sums.shape[0] // 8
     width = channels // blocks
     patch, kept, span = width // owners, channels // owners, rows // owners
-    columns = -(-2 * width // 128) * 128
+    columns, lanes = packed_shape(blocks, width, taps, owners, rows)
 
     def body(conv_ref, both_ref, taps_ref, decay_ref, out_ref):
         out_ref[...] = jnp.zeros((rows, columns), bf16)
@@ -450,12 +501,16 @@
             at = slice(b * width, (b + 1) * width)
             recur = dense[at, b * width : (b + 1) * width].astype(bf16)
             inward = dense[at, channels + b * width : channels + (b + 1) * width].astype(bf16)
+            both = jnp.concatenate([recur, inward], axis=1)
             for s in range(owners):
-                row = s * span + b * patch
-                out_ref[row : row + patch, 0:width] = recur[s * patch : (s + 1) * patch, :]
-                out_ref[row : row + patch, width : 2 * width] = inward[s * patch : (s + 1) * patch, :]
+                mine = both[s * patch : (s + 1) * patch, :]
+                for g, start in enumerate(range(0, 2 * width, lanes)):
+                    row = s * span + (g * blocks + b) * patch
+                    part = mine[:, start : start + lanes]
+                    out_ref[row : row + patch, 0 : part.shape[1]] = part
+        used = -(-2 * width // lanes) * blocks * patch
         for s in range(owners):
-            row = s * span + blocks * patch
+            row = s * span + used
             out_ref[row : row + taps + 1, 0:kept] = sums[:, s * kept : (s + 1) * kept]
 
     return call(
@@ -594,7 +649,7 @@
     halo_in = lax.ppermute(block_in[tokens - 8 :], "seq", forward_pairs)
     columns = width // seq_count
     column_block = lax.dynamic_slice_in_dim(out_proj, seq_index * columns, columns, 1)
-    column_pieces = exchanged(lambda k: column_block)
+    column_block = lax.all_gather(column_block, "head").reshape(head_count * channels, columns)
     soft = jax.nn.softplus(-decay_param)[None, :]
     slide = sharpness * jax.nn.sigmoid(-decay_param)[None, :]
 
@@ -632,10 +687,6 @@
         flops=4 * tokens * channels * channels,
     )
     ends = lax.all_gather(end, "seq")
-    column_pieces, ends = together((column_pieces, ends))
-    projection = lax.all_gather(rotated(column_block, column_pieces, place_index), "seq")
-    if columns % 128:
-        projection = jnp.moveaxis(projection, 0, 1).reshape(1, head_count * channels, width)
     gate_pre = jnp.dot(normed, gate_proj, preferred_element_type=f32)
     states, mixed_low, entry = call(
         mix,
@@ -649,6 +700,10 @@
         here,
         scalars=1,
     )
+    column_block, mixed_low = together((column_block, mixed_low))
+    projection = lax.all_gather(column_block, "seq")
+    if columns % 128:
+        projection = jnp.moveaxis(projection, 0, 1).reshape(1, head_count * channels, width)
     first = gather_first(mixed_low)
     second = gather_second(first)
     d_hidden = jnp.einsum("td,fd->tf", cotangent, ffn_down, preferred_element_type=f32)
@@ -686,8 +741,8 @@
     first = gather_first(d_out_share)
     first, ffn_out = together((first, ffn_out))
     second = gather_second(first)
-    half = tokens // 2
-    ffn_halves = [ffn_out[:half], ffn_out[half:]]
+    cut = tokens * 5 // 8
+    ffn_halves = [ffn_out[:cut], ffn_out[cut:]]
     turn_one = [line_turn(1, ffn_halves[0])]
     d_out_low = assembled(d_out_share, first, second, place_index, bf16)
     d_out_low, ffn_halves[1] = together((d_out_low, ffn_halves[1]))
@@ -766,7 +821,6 @@
     first, grad_rest, turn_three, turn_two = together((first, grad_rest, turn_three, turn_two))
     second = scatter_second(d_normed, first)
     sent = added(ffn_halves[1], turn_two[1]).astype(bf16)
-    second, sent = together((second, sent))
     turn_three.append(line_turn(3, sent))
     grad_rest = lax.psum_scatter(grad_rest, "seq", scatter_dimension=0, tiled=True)
     d_normed = added(mine(d_normed), *second)
@@ -777,42 +831,30 @@
     first = gather_first(grad_input.astype(bf16))
     gains = jnp.stack([grad_pregain, grad_postgain])
     gain_pieces = exchanged(lambda k: gains)
+    base = residual + added(ffn_out, jnp.concatenate(turn_one), jnp.concatenate(turn_two))
+    block_out = add_last(base, turn_three)
+    grad_ffn = finish_ffn(grad_ffn, 3)
+    first, block_out, grad_ffn = together((first, block_out, grad_ffn))
     second = gather_second(first)
-    block_out = jnp.concatenate(
-        [
-            residual[half * h : half * (h + 1)] + added(ffn_halves[h], turn_one[h], turn_two[h], turn_three[h])
-            for h in range(2)
-        ],
-        axis=0,
-    ).astype(bf16)
-    second, block_out = together((second, block_out))
     gains = jnp.sum(lax.all_gather(sum(gain_pieces, gains), "seq"), axis=0)
     gain_share = width // seq_count
     gains = lax.dynamic_slice_in_dim(gains, seq_index * gain_share, gain_share, 1)
-    grad_ffn = grad_ffn.astype(f32)
-    grad_ffn = (
-        grad_ffn[:, :hidden_units],
-        grad_ffn[:, hidden_units : 2 * hidden_units],
-        grad_ffn[:, 2 * hidden_units :].T,
-    )
-    second, grad_rest, grad_ffn = together((second, grad_rest, grad_ffn))
+    grad_rest, grad_ffn = together((grad_rest, grad_ffn))
     grad_input = assembled(grad_input, first, second, place_index, f32)
-    grad_rest = grad_rest.astype(f32)
-    packed = grad_rest[:, 3 * channels :]
-    patch = block_width // seq_count
-    kept = channels // seq_count
-    small = packed[: blocks * patch, : 2 * block_width].reshape(blocks, patch, 2 * block_width)
+    grad_gate_proj, grad_input_proj, grad_out_proj, grad_taps, grad_recur, grad_inward, grad_decay = finish_rest(
+        grad_rest, channels, blocks, block_width, tap_count, seq_count
+    )
     return (
         block_out,
         grad_input,
         gains[0],
-        grad_rest[:, :channels],
-        grad_rest[:, channels : 2 * channels],
-        packed[blocks * patch : blocks * patch + tap_count, :kept],
-        small[:, :, :block_width],
-        small[:, :, block_width:],
-        packed[blocks * patch + tap_count, :kept],
-        grad_rest[:, 2 * channels : 3 * channels].T,
+        grad_gate_proj,
+        grad_input_proj,
+        grad_taps,
+        grad_recur,
+        grad_inward,
+        grad_decay[0],
+        grad_out_proj,
         gains[1],
         *grad_ffn,
     )

time: 483 us -> 430 us (0.89)
  local copies, waits for them, and re-layouts: 46 us -> 27.3 us
  starting transfers between devices: 106 us -> 87.5 us
  waiting for transfers between devices: 119 us -> 113 us
    ppermute x6, waiting for transfers between devices: 29.2 us -> 0.02 us  [line_turn(): lax.ppermute(sent, 'head', [(turn - 1, turn), (peers - turn, peers - turn...]
    ppermute x2, starting transfers between devices: 24.3 us -> 9.55 us  [scatter_second(): lax.ppermute(to_right, 'head', line_pairs(1))]
    all_gather x1 -> x2, waiting for transfers between devices: 0.01 us -> 12 us  [the longest x1 9.2 us: local(): projection = lax.all_gather(column_block, 'seq')]
    ppermute x6 -> x3, starting transfers between devices: 11.8 us -> 2.15 us  [exchanged(): lax.ppermute(blocks(k), 'head', shifted(peers, k))]
    unnamed x130 -> x124, local copies, waits for them, and re-layouts: 29.1 us -> 20.6 us
    slice x6 -> x2, local copies, waits for them, and re-layouts: 7.6 us -> 0.2 us  [local(): ffn_halves = [ffn_out[:cut], ffn_out[cut:]]]
    another operation x1 -> x0, other arithmetic: 5.96 us -> none
    ppermute x2, waiting for transfers between devices: 2.79 us -> 8.3 us  [scatter_second(): lax.ppermute(to_right, 'head', line_pairs(1))]
  transfers between devices with their start and end apart: 42 -> 40, of which waited for: 15 -> 17; matrix products, arithmetic and copies ran while one was open for 15% -> 15% of each run, Pallas kernels for 11% -> 13%
where the time goes in v2:
time: 430 us; the launch traced here: 422 us
  waiting for transfers between devices  113 us (26%)
  starting transfers between devices  87.5 us (20%)
  Pallas kernels  71.9 us (17%)
  matrix products  47.2 us (11%)
  other arithmetic  30.6 us (7%)
  blocking collectives  29.4 us (7%)
  local copies, waits for them, and re-layouts  27.3 us (6%)
  between operations  15.3 us (4%)
    ppermute x3, waiting for transfers between devices, gather_second(): lax.ppermute(back, 'head', [(1, 0), (2, 3)])  46.5 us
    pallas_call x10, Pallas kernels, call(): pl.pallas_call(body, out_shape=out_shape, in_specs=[pl.BlockSpec(memory_s...  31.9 us
    pallas_call x2, Pallas kernels, weight_grads(): pl.pallas_call(body, grid=(width // block,), in_specs=[pl.BlockSpec((toke...  25 us
    ppermute x3, waiting for transfers between devices, gather_first(): lax.ppermute(own, 'head', line_pairs(-1))  22.8 us
    unnamed x124, local copies, waits for them, and re-layouts  20.6 us
    ppermute x6, starting transfers between devices, line_turn(): lax.ppermute(sent, 'head', [(turn - 1, turn), (peers - turn, peers - turn...  17.1 us
    ppermute x3, starting transfers between devices, gather_first(): lax.ppermute(own, 'head', line_pairs(1))  15.8 us
    pallas_call x1, Pallas kernels, residual_norm(): pl.pallas_call(add_projection, grid=(blocks,), in_specs=[whole(tokens, ch...  15 us
  transfers between devices with their start and end apart: 40, of which 17 were waited for; matrix products, arithmetic and copies ran while one was open for 15% of the time, Pallas kernels for 13%

profile of v2, /device:TPU:0, one launch (start us, length us, event | category | flops | bytes accessed | tf_op | source)
XLA Modules:
  0.0 422.4 jit_solution(8806808257305683981)
XLA Ops:
  8.2 2.3 collective-permute-start
  12.3 2.2 fusion
  21.1 7.5 %shard_map.245 = (bf16[512,640]{1,0:T(8,128)(2,1)S(1)}, f32[512,640]{1,0:T(8,128)S(1)}, f32[512,640]{1,0:T(8,128)S(1)}, f32[5,512,128]{2,1,0:T(8,128)S(1)}, f32[...) custom-call(bf16[512,640]{1,0:T(8,128)(2,1)S(1)} %convolution_convert_fusi, ...), custom_call_target="tpu_custom_call" | custom-call | flops 1000 | bytes 1000 | tf_op jit(solution)/shard_map/pallas_call | solution.py:21
  31.9 10.2 %all-gather.5.ends_ref = f32[8,2,640]{2,1,0:T(2,128)S(1)} all-gather(f32[1,2,640]{2,1,0:T(2,128)S(1)} %bitcast.37), channel_id=3, replica_groups=mesh['seq'=8,'head'=4] {'seq'}, dimensions={0}, use_global_device_ids=true | all-gather | bytes 46080 | tf_op jit(solution)/shard_map/all_gather | solution.py:689
  44.8 2.8 all-gather.11.cloned.1.call-done
  49.0 5.4 %collective-permute-start.1 = (bf16[512,640]{1,0:T(8,128)(2,1)}, bf16[512,640]{1,0:T(8,128)(2,1)}, u32[]{:S(2)}, u32[]{:S(2)}) collective-permute-start(bf16[512,640]{1,0:T(8,128)(2,1)} %copy-done.19), channel_id=1, source_target_pairs={{0,1},{1,2},{2,3},{4,5},{5,6},{6,7},{8,9},{9,10},{10,11},{12,13},{... | collective-permute-start | bytes 1966088 | tf_op jit(solution)/shard_map/ppermute | solution.py:579
  54.4 11.5 %collective-permute-done.2.right_ref = bf16[512,640]{1,0:T(8,128)(2,1)} collective-permute-done((bf16[512,640]{1,0:T(8,128)(2,1)}, bf16[512,640]{1,0:T(8,128)(2,1)}, u32[]{:S(2)}, u32[]{:S(2)}) %collective-permute-start.2) | collective-permute-done | bytes 655392 | tf_op jit(solution)/shard_map/ppermute | solution.py:579
  72.0 7.9 %fusion.35 = f32[512,1536]{1,0:T(8,128)} fusion(bf16[512,2048]{1,0:T(8,128)(2,1)S(1)} %copy-done.50, bf16[1536,2048]{1,0:T(8,128)(2,1)} %param.26), kind=kOutput, calls=%fused_computation.87 | convolution fusion | flops 3221225472 | bytes 11534336 | tf_op jit(solution)/shard_map/td,fd->tf/dot_general | solution.py:709
  79.9 20.2 %collective-permute-done.4.back_ref = bf16[512,640]{1,0:T(8,128)(2,1)S(1)} collective-permute-done((bf16[512,640]{1,0:T(8,128)(2,1)S(1)}, bf16[512,640]{1,0:T(8,128)(2,1)S(1)}, u32[]{:S(2)}, u32[]{:S(2)}) %collective-permute-start.4) | collective-permute-done | bytes 655392 | tf_op jit(solution)/shard_map/ppermute | solution.py:589
  102.7 9.2 %all-gather.13.cloned.1.call-done = bf16[20480,256]{1,0:T(8,128)(2,1)} async-done(((bf16[2560,256]{1,0:T(8,128)(2,1)}), bf16[20480,256]{1,0:T(8,128)(2,1)}) %all-gather.13.cloned.1.call-update) | async-done | bytes 10485776 | tf_op jit(solution)/shard_map/all_gather | solution.py:704
  116.2 15.0 %shard_map.247 = (f32[512,2048]{1,0:T(8,128)}, bf16[512,2048]{1,0:T(8,128)(2,1)}, f32[512,1]{1,0:T(8,128)S(1)}) custom-call(bf16[512,640]{1,0:T(8,128)(2,1)S(1)} %copy-done.20, bf16[512,640]{1,0:T(8,128)(2,1)} %collective-permute-done.1.left_ref, bf16[512,640]{1,0:T(8,128)(2,1)} %collective-permute-done.2.right_ref, bf16[512,640]{1,0:T(8,128)(2,1)S(1)} %copy-done.30, ...), custom_call_target="tpu_custom_call" | custom-call | flops 5368709120 | bytes 20971520 | tf_op jit(solution)/shard_map/pallas_call | solution.py:335
  131.3 6.3 %fusion.36 = f32[512,1536]{1,0:T(8,128)S(1)} fusion(bf16[512,2048]{1,0:T(8,128)(2,1)} %get-tuple-element.110.refs_0_.refs_1_, bf16[2048,1536]{1,0:T(8,128)(2,1)} %param.24), kind=kOutput, calls=%fused_computation.88 | convolution fusion | flops 3221225472 | bytes 11534336 | tf_op jit(solution)/shard_map/dot_general | solution.py:719
  137.7 5.4 %multiply_convert_fusion = (bf16[512,1536]{1,0:T(8,128)(2,1)S(1)}, bf16[512,1536]{1,0:T(8,128)(2,1)S(1)}, bf16[512,1536]{1,0:T(8,128)(2,1)S(1)}) fusion(f32[512,1536]{1,0:T(8,128)S(1)} %fusion.36, f32[512,1536]{1,0:T(8,128)S(1)} %copy-done.56, bf16[512,2048]{1,0:T(8,128)(2,1)S(1)} %copy-done.55, bf16[2048,1536]{1,0:T(8,128)(2,1)S(1)} %bitcast.47), kind=kOutput, calls=%fused_computation.19 | convolution fusion | flops 3240886272 | bytes 19398656 | tf_op jit(solution)/shard_map/dot_general | solution.py:720
  143.1 5.0 %fusion.37 = f32[512,2048]{1,0:T(8,128)} fusion(bf16[512,1536]{1,0:T(8,128)(2,1)S(1)} %get-tuple-element.113.refs_4_, bf16[2048,1536]{1,0:T(8,128)(2,1)S(1)} %bitcast.47), kind=kOutput, calls=%fused_computation.89 | convolution fusion | flops 3221225472 | bytes 12058624 | tf_op jit(solution)/shard_map/tf,df->td/dot_general | solution.py:727
  148.1 5.3 %add_convert_fusion.1 = bf16[512,2048]{1,0:T(8,128)(2,1)S(1)} fusion(f32[512,2048]{1,0:T(8,128)} %fusion.37, bf16[512,1536]{1,0:T(8,128)(2,1)S(1)} %get-tuple-element.112.refs_3_, bf16[2048,1536]{1,0:T(8,128)(2,1)S(1)} %bitcast.49), kind=kOutput, calls=%fused_computation.9 | convolution fusion | flops 3223322624 | bytes 14155776 | tf_op jit(solution)/shard_map/tf,df->td/dot_general | solution.py:725
  157.2 4.0 collective-permute-start.6
  161.2 3.4 collective-permute-start.8
  164.6 14.9 %shard_map.248 = bf16[2048,4608]{1,0:T(8,128)(2,1)} custom-call(bf16[512,2048]{1,0:T(8,128)(2,1)} %get-tuple-element.110.refs_0_.refs_1_, bf16[512,2048]{1,0:T(8,128)(2,1)} %get-tuple-element.110.refs_0_.refs_1_, bf16[512,2048]{1,0:T(8,128)(2,1)} %refs_2_.1, bf16[512,1536]{1,0:T(8,128)(2,1)S(1)} %get-tuple-element.112.refs_3_, ...), custom_call_target="tpu_custom_call" | custom-call | flops 9663676416 | bytes 18874368 | tf_op jit(solution)/shard_map/pallas_call | solution.py:405
  179.5 4.1 collective-permute-done.8
  185.0 2.2 add_convert_fusion.5
  188.5 5.1 %collective-permute-start.9 = (bf16[128,2048]{1,0:T(8,128)(2,1)S(1)}, bf16[128,2048]{1,0:T(8,128)(2,1)S(1)}, u32[]{:S(2)}, u32[]{:S(2)}) collective-permute-start(bf16[128,2048]{1,0:T(8,128)(2,1)S(1)} %get-tuple-element.238), channel_id=1, source_target_pairs={{0,1},{1,2},{2,3},{4,5},{5,6},{6,7},{8,9},{9,10},{10,11},{12,13},{... | collective-permute-start | bytes 1572872 | tf_op jit(solution)/shard_map/ppermute | solution.py:575
  193.7 7.7 %convolution_convert_fusion = bf16[512,2048]{1,0:T(8,128)(2,1)S(1)} fusion(bf16[512,1536]{1,0:T(8,128)(2,1)S(1)} %copy-done.34, bf16[1536,2048]{1,0:T(8,128)(2,1)} %param.26), kind=kOutput, calls=%fused_computation.23 | convolution fusion | flops 3222274048 | bytes 9961472 | tf_op jit(solution)/shard_map/dot_general | solution.py:735
  204.7 2.7 fusion.32
  208.6 5.1 %collective-permute-start.11 = (bf16[128,2048]{1,0:T(8,128)(2,1)S(1)}, bf16[128,2048]{1,0:T(8,128)(2,1)S(1)}, u32[]{:S(2)}, u32[]{:S(2)}) collective-permute-start(bf16[128,2048]{1,0:T(8,128)(2,1)S(1)} %get-tuple-element.230.own_ref), channel_id=1, source_target_pairs={{0,1},{1,2},{2,3},{4,5},{5,6},{6,7},{8,9},{9,10},{10,11},{12,13},{... | collective-permute-start | bytes 1572872 | tf_op jit(solution)/shard_map/ppermute | solution.py:579
  213.7 8.5 %collective-permute-done.12.right_ref = bf16[128,2048]{1,0:T(8,128)(2,1)S(1)} collective-permute-done((bf16[128,2048]{1,0:T(8,128)(2,1)S(1)}, bf16[128,2048]{1,0:T(8,128)(2,1)S(1)}, u32[]{:S(2)}, u32[]{:S(2)}) %collective-permute-start.12) | collective-permute-done | bytes 524320 | tf_op jit(solution)/shard_map/ppermute | solution.py:579
  223.5 4.5 %collective-permute-start.16 = (bf16[320,2048]{1,0:T(8,128)(2,1)S(1)}, bf16[320,2048]{1,0:T(8,128)(2,1)S(1)}, u32[]{:S(2)}, u32[]{:S(2)}) collective-permute-start(bf16[320,2048]{1,0:T(8,128)(2,1)S(1)} %slice.17), channel_id=1, source_target_pairs={{0,1},{3,2},{4,5},{7,6},{8,9},{11,10},{12,13},{15,14},{16,17},{19,... | collective-permute-start | bytes 3932168 | tf_op jit(solution)/shard_map/ppermute | solution.py:596
  231.5 20.7 %collective-permute-done.14.back_ref = bf16[128,2048]{1,0:T(8,128)(2,1)S(1)} collective-permute-done((bf16[128,2048]{1,0:T(8,128)(2,1)S(1)}, bf16[128,2048]{1,0:T(8,128)(2,1)S(1)}, u32[]{:S(2)}, u32[]{:S(2)}) %collective-permute-start.14) | collective-permute-done | bytes 524320 | tf_op jit(solution)/shard_map/ppermute | solution.py:589
  255.8 7.5 %collective-permute-start.17 = (bf16[192,2048]{1,0:T(8,128)(2,1)S(1)}, bf16[192,2048]{1,0:T(8,128)(2,1)S(1)}, u32[]{:S(2)}, u32[]{:S(2)}) collective-permute-start(bf16[192,2048]{1,0:T(8,128)(2,1)S(1)} %slice.16), channel_id=1, source_target_pairs={{0,1},{3,2},{4,5},{7,6},{8,9},{11,10},{12,13},{15,14},{16,17},{19,... | collective-permute-start | bytes 2359304 | tf_op jit(solution)/shard_map/ppermute | solution.py:596
  263.4 5.6 %shard_map.250 = (bf16[512,640]{1,0:T(8,128)(2,1)S(1)}, f32[5,512,128]{2,1,0:T(8,128)S(1)}, f32[5,512,128]{2,1,0:T(8,128)S(1)}, f32[16,640]{1,0:T(8,128)S(1)}, f32[1,640]{1,0:T(1,128)S(1)}) custom-call(f32[512,640]{1,0:T(8,128)S(1)} %fusion.38.d_mixed_ref, f32[512,640]{1,0:T(8,128)S(1)} %copy-done.9, f32[512,640]{1,0:T(8,128)S(1)} %copy-done.7, ...), custom_call_target="tpu_custom_call" | custom-call | flops 1000 | bytes 1000 | tf_op jit(solution)/shard_map/pallas_call | solution.py:21
  269.0 8.9 %all-gather.6.backs_ref = f32[8,1,640]{2,1,0:T(1,128)S(1)} all-gather(f32[1,1,640]{2,1,0:T(1,128)S(1)} %bitcast.38), channel_id=5, replica_groups=mesh['seq'=8,'head'=4] {'seq'}, dimensions={0}, use_global_device_ids=true | all-gather | bytes 23040 | tf_op jit(solution)/shard_map/all_gather | solution.py:770
  280.7 5.8 %shard_map.251 = (bf16[512,1280]{1,0:T(8,128)(2,1)S(1)}, f32[512,640]{1,0:T(8,128)S(1)}, f32[8,640]{1,0:T(8,128)S(1)}, f32[8,640]{1,0:T(8,128)S(1)}, f32[32,640]{1,0:T(8,128)S(1)}) custom-call(f32[5,512,128]{2,1,0:T(8,128)S(1)} %get-tuple-element.130.local_ref, f32[5,512,128]{2,1,0:T(8,128)S(1)} %get-tuple-element.131.prod_ref, ...), custom_call_target="tpu_custom_call" | custom-call | flops 1000 | bytes 1000 | tf_op jit(solution)/shard_map/pallas_call | solution.py:21
  296.0 8.9 %collective-permute-start.22 = (bf16[128,2048]{1,0:T(8,128)(2,1)}, bf16[128,2048]{1,0:T(8,128)(2,1)}, u32[]{:S(2)}, u32[]{:S(2)}) collective-permute-start(bf16[128,2048]{1,0:T(8,128)(2,1)} %get-tuple-element.239), channel_id=1, source_target_pairs={{0,2},{3,1},{4,6},{7,5},{8,10},{11,9},{12,14},{15,13},{16,18},{19,... | collective-permute-start | bytes 1572872 | tf_op jit(solution)/shard_map/ppermute | solution.py:565
  309.6 10.1 %shard_map.253 = bf16[2048,2048]{1,0:T(8,128)(2,1)} custom-call(bf16[512,2048]{1,0:T(8,128)(2,1)S(1)} %copy-done.2, bf16[512,2048]{1,0:T(8,128)(2,1)S(1)} %copy-done.2, bf16[512,2048]{1,0:T(8,128)(2,1)} %copy-done.3, bf16[512,640]{1,0:T(8,128)(2,1)S(1)} %get-tuple-element.129.refs_3_, bf16[512,640]{1,0:T(8,128)(2,1)S(1)} %add_convert_fusion.2.refs_4_, ...), custom_call_target="tpu_custom_call" | custom-call | flops 4294967296 | bytes 8388608 | tf_op jit(solution)/shard_map/pallas_call | solution.py:405
  319.7 8.1 %collective-permute-done.20 = bf16[128,2048]{1,0:T(8,128)(2,1)} collective-permute-done((bf16[128,2048]{1,0:T(8,128)(2,1)}, bf16[128,2048]{1,0:T(8,128)(2,1)}, u32[]{:S(2)}, u32[]{:S(2)}) %collective-permute-start.20) | collective-permute-done | bytes 524320 | tf_op jit(solution)/shard_map/ppermute | solution.py:563
  329.0 3.1 add_convert_fusion.4
  332.2 4.4 %collective-permute-start.25 = (bf16[128,2048]{1,0:T(8,128)(2,1)}, bf16[128,2048]{1,0:T(8,128)(2,1)S(1)}, u32[]{:S(2)}, u32[]{:S(2)}) collective-permute-start(bf16[128,2048]{1,0:T(8,128)(2,1)} %get-tuple-element.235), channel_id=1, source_target_pairs={{0,1},{1,2},{2,3},{4,5},{5,6},{6,7},{8,9},{9,10},{10,11},{12,13},{... | collective-permute-start | bytes 1572872 | tf_op jit(solution)/shard_map/ppermute | solution.py:575
  341.5 6.8 %collective-permute-done.25 = bf16[128,2048]{1,0:T(8,128)(2,1)S(1)} collective-permute-done((bf16[128,2048]{1,0:T(8,128)(2,1)}, bf16[128,2048]{1,0:T(8,128)(2,1)S(1)}, u32[]{:S(2)}, u32[]{:S(2)}) %collective-permute-start.25) | collective-permute-done | bytes 524320 | tf_op jit(solution)/shard_map/ppermute | solution.py:575
  348.3 5.3 %collective-permute-done.26 = bf16[128,2048]{1,0:T(8,128)(2,1)} collective-permute-done((bf16[128,2048]{1,0:T(8,128)(2,1)}, bf16[128,2048]{1,0:T(8,128)(2,1)}, u32[]{:S(2)}, u32[]{:S(2)}) %collective-permute-start.26) | collective-permute-done | bytes 524320 | tf_op jit(solution)/shard_map/ppermute | solution.py:575
  355.8 3.3 fusion.30
  360.4 5.4 %collective-permute-start.27 = (bf16[128,2048]{1,0:T(8,128)(2,1)}, bf16[128,2048]{1,0:T(8,128)(2,1)}, u32[]{:S(2)}, u32[]{:S(2)}) collective-permute-start(bf16[128,2048]{1,0:T(8,128)(2,1)} %get-tuple-element.228), channel_id=1, source_target_pairs={{0,1},{1,2},{2,3},{4,5},{5,6},{6,7},{8,9},{9,10},{10,11},{12,13},{... | collective-permute-start | bytes 1572872 | tf_op jit(solution)/shard_map/ppermute | solution.py:579
  365.8 3.3 add_add_fusion.base_ref
  371.2 3.1 shard_map.254
  376.0 2.5 shard_map.255
  378.5 2.8 collective-permute-done.28.right_ref
  387.6 10.2 %all-gather.7 = f32[8,2,2048]{2,1,0:T(2,128)S(1)} all-gather(f32[1,2,2048]{2,1,0:T(2,128)S(1)} %add_bitcast_fusion), channel_id=6, replica_groups=mesh['seq'=8,'head'=4] {'seq'}, dimensions={0}, use_global_device_ids=true | all-gather | bytes 147456 | tf_op jit(solution)/shard_map/all_gather | solution.py:839
  398.5 2.4 reduce-scatter.5.cloned.1.call-done.in_ref
  404.9 5.5 %collective-permute-done.31.back_ref = bf16[128,2048]{1,0:T(8,128)(2,1)} collective-permute-done((bf16[128,2048]{1,0:T(8,128)(2,1)}, bf16[128,2048]{1,0:T(8,128)(2,1)}, u32[]{:S(2)}, u32[]{:S(2)}) %collective-permute-start.31) | collective-permute-done | bytes 524320 | tf_op jit(solution)/shard_map/ppermute | solution.py:589
  411.6 3.8 shard_map.256
  (228 shorter events, 91.2 us)
Async XLA Ops:
  7.2 40.4 %all-gather.11.cloned.1.call-start = ((), (), s32[]{:S(2)}) async-start(), calls=%async_computation.4 | async-start | bytes 1638400 | tf_op jit(solution)/shard_map/all_gather | solution.py:652
  8.2 11.4 %collective-permute-start = (bf16[8,2048]{1,0:T(8,128)(2,1)S(1)}, bf16[8,2048]{1,0:T(8,128)(2,1)S(1)}, u32[]{:S(2)}, u32[]{:S(2)}) collective-permute-start(bf16[8,2048]{1,0:T(8,128)(2,1)S(1)} %slice.15), channel_id=1, source_target_pairs={{0,4},{4,8},{8,12},{12,16},{16,20},{20,24},{24,28},{1,5},{5,9},{9,... | collective-permute-start | bytes 98312 | tf_op jit(solution)/shard_map/ppermute | solution.py:649
  12.3 99.6 %all-gather.13.cloned.1.call-start = ((), (), s32[]{:S(2)}) async-start(), calls=%async_computation.5 | async-start | bytes 11796480 | tf_op jit(solution)/shard_map/all_gather | solution.py:704
  19.5 22.6 %copy-start.8 = (f32[512,640]{1,0:T(8,128)}, f32[512,640]{1,0:T(8,128)S(1)}, u32[]{:S(2)}) copy-start(f32[512,640]{1,0:T(8,128)S(1)} %fusion.34.gate_ref) | copy-start | bytes 3932164
  47.6 326.7 %reduce-scatter.3.cloned.1.call-start = ((), (), s32[]{:S(2)}) async-start(), calls=%async_computation.2 | async-start | bytes 21233664 | tf_op jit(solution)/shard_map/reduce_scatter | solution.py:733
  47.7 18.2 %collective-permute-start.2 = (bf16[512,640]{1,0:T(8,128)(2,1)}, bf16[512,640]{1,0:T(8,128)(2,1)}, u32[]{:S(2)}, u32[]{:S(2)}) collective-permute-start(bf16[512,640]{1,0:T(8,128)(2,1)} %copy-done.19), channel_id=1, source_target_pairs={{1,0},{2,1},{3,2},{5,4},{6,5},{7,6},{9,8},{10,9},{11,10},{13,12},{... | collective-permute-start | bytes 1966088 | tf_op jit(solution)/shard_map/ppermute | solution.py:579
  49.0 18.1 %collective-permute-start.1 = (bf16[512,640]{1,0:T(8,128)(2,1)}, bf16[512,640]{1,0:T(8,128)(2,1)}, u32[]{:S(2)}, u32[]{:S(2)}) collective-permute-start(bf16[512,640]{1,0:T(8,128)(2,1)} %copy-done.19), channel_id=1, source_target_pairs={{0,1},{1,2},{2,3},{4,5},{5,6},{6,7},{8,9},{9,10},{10,11},{12,13},{... | collective-permute-start | bytes 1966088 | tf_op jit(solution)/shard_map/ppermute | solution.py:579
  68.5 32.5 %collective-permute-start.5 = (bf16[512,640]{1,0:T(8,128)(2,1)S(1)}, bf16[512,640]{1,0:T(8,128)(2,1)S(1)}, u32[]{:S(2)}, u32[]{:S(2)}) collective-permute-start(bf16[512,640]{1,0:T(8,128)(2,1)S(1)} %get-tuple-element.244), channel_id=1, source_target_pairs={{1,3},{2,0},{5,7},{6,4},{9,11},{10,8},{13,15},{14,12},{17,19},{18,... | collective-permute-start | bytes 1966088 | tf_op jit(solution)/shard_map/ppermute | solution.py:590
  69.8 32.0 %collective-permute-start.3 = (bf16[512,640]{1,0:T(8,128)(2,1)S(1)}, bf16[512,640]{1,0:T(8,128)(2,1)S(1)}, u32[]{:S(2)}, u32[]{:S(2)}) collective-permute-start(bf16[512,640]{1,0:T(8,128)(2,1)S(1)} %get-tuple-element.244), channel_id=1, source_target_pairs={{1,2},{2,1},{5,6},{6,5},{9,10},{10,9},{13,14},{14,13},{17,18},{18,... | collective-permute-start | bytes 1966088 | tf_op jit(solution)/shard_map/ppermute | solution.py:588
  70.5 41.4 %copy-start.25 = (f32[2048]{0:T(1024)S(1)}, f32[2048]{0:T(1024)}, u32[]{:S(2)}) copy-start(f32[2048]{0:T(1024)} %param.23) | copy-start | bytes 24580
  70.5 29.6 %collective-permute-start.4 = (bf16[512,640]{1,0:T(8,128)(2,1)S(1)}, bf16[512,640]{1,0:T(8,128)(2,1)S(1)}, u32[]{:S(2)}, u32[]{:S(2)}) collective-permute-start(bf16[512,640]{1,0:T(8,128)(2,1)S(1)} %get-tuple-element.243), channel_id=1, source_target_pairs={{1,0},{2,3},{5,4},{6,7},{9,8},{10,11},{13,12},{14,15},{17,16},{18,... | collective-permute-start | bytes 1966088 | tf_op jit(solution)/shard_map/ppermute | solution.py:589
  116.2 21.4 %slice-start = ((s8[6291456]{0:T(1024)(128)(4,1)}), s8[4194304]{0:T(1024)(128)(4,1)S(1)}, s32[]{:S(2)}) async-start(s8[6291456]{0:T(1024)(128)(4,1)} %bitcast.46), calls=%async_computation.6 | async-start | bytes 8388608
  143.1 21.5 %copy-start.33 = (bf16[512,1536]{1,0:T(8,128)(2,1)}, bf16[512,1536]{1,0:T(8,128)(2,1)S(1)}, u32[]{:S(2)}) copy-start(bf16[512,1536]{1,0:T(8,128)(2,1)S(1)} %get-tuple-element.114.refs_5_) | copy-start | bytes 4718596
  155.8 27.9 %collective-permute-start.7 = (bf16[128,2048]{1,0:T(8,128)(2,1)}, bf16[128,2048]{1,0:T(8,128)(2,1)}, u32[]{:S(2)}, u32[]{:S(2)}) collective-permute-start(bf16[128,2048]{1,0:T(8,128)(2,1)} %get-tuple-element.242), channel_id=1, source_target_pairs={{3,2},{2,1},{7,6},{6,5},{11,10},{10,9},{15,14},{14,13},{19,18},{18... | collective-permute-start | bytes 1572872 | tf_op jit(solution)/shard_map/ppermute | solution.py:564
  157.2 26.4 %collective-permute-start.6 = (bf16[128,2048]{1,0:T(8,128)(2,1)}, bf16[128,2048]{1,0:T(8,128)(2,1)}, u32[]{:S(2)}, u32[]{:S(2)}) collective-permute-start(bf16[128,2048]{1,0:T(8,128)(2,1)} %get-tuple-element.242), channel_id=1, source_target_pairs={{0,1},{1,2},{4,5},{5,6},{8,9},{9,10},{12,13},{13,14},{16,17},{17,1... | collective-permute-start | bytes 1572872 | tf_op jit(solution)/shard_map/ppermute | solution.py:563
  161.2 22.4 %collective-permute-start.8 = (bf16[128,2048]{1,0:T(8,128)(2,1)}, bf16[128,2048]{1,0:T(8,128)(2,1)}, u32[]{:S(2)}, u32[]{:S(2)}) collective-permute-start(bf16[128,2048]{1,0:T(8,128)(2,1)} %get-tuple-element.241), channel_id=1, source_target_pairs={{0,2},{3,1},{4,6},{7,5},{8,10},{11,9},{12,14},{15,13},{16,18},{19,... | collective-permute-start | bytes 1572872 | tf_op jit(solution)/shard_map/ppermute | solution.py:565
  183.6 217.3 %reduce-scatter.5.cloned.1.call-start = ((), (), s32[]{:S(2)}) async-start(), calls=%async_computation.3 | async-start | bytes 9437184 | tf_op jit(solution)/shard_map/reduce_scatter | solution.py:825
  187.2 15.5 %collective-permute-start.10 = (bf16[128,2048]{1,0:T(8,128)(2,1)S(1)}, bf16[128,2048]{1,0:T(8,128)(2,1)S(1)}, u32[]{:S(2)}, u32[]{:S(2)}) collective-permute-start(bf16[128,2048]{1,0:T(8,128)(2,1)S(1)} %get-tuple-element.237), channel_id=1, source_target_pairs={{1,0},{2,1},{3,2},{5,4},{6,5},{7,6},{9,8},{10,9},{11,10},{13,12},{... | collective-permute-start | bytes 1572872 | tf_op jit(solution)/shard_map/ppermute | solution.py:575
  188.5 15.6 %collective-permute-start.9 = (bf16[128,2048]{1,0:T(8,128)(2,1)S(1)}, bf16[128,2048]{1,0:T(8,128)(2,1)S(1)}, u32[]{:S(2)}, u32[]{:S(2)}) collective-permute-start(bf16[128,2048]{1,0:T(8,128)(2,1)S(1)} %get-tuple-element.238), channel_id=1, source_target_pairs={{0,1},{1,2},{2,3},{4,5},{5,6},{6,7},{8,9},{9,10},{10,11},{12,13},{... | collective-permute-start | bytes 1572872 | tf_op jit(solution)/shard_map/ppermute | solution.py:575
  201.3 85.2 %copy-start.35 = (bf16[512,2048]{1,0:T(8,128)(2,1)}, bf16[512,2048]{1,0:T(8,128)(2,1)S(1)}, u32[]{:S(2)}) copy-start(bf16[512,2048]{1,0:T(8,128)(2,1)S(1)} %convolution_convert_fusion) | copy-start | bytes 6291460
  207.3 14.9 %collective-permute-start.12 = (bf16[128,2048]{1,0:T(8,128)(2,1)S(1)}, bf16[128,2048]{1,0:T(8,128)(2,1)S(1)}, u32[]{:S(2)}, u32[]{:S(2)}) collective-permute-start(bf16[128,2048]{1,0:T(8,128)(2,1)S(1)} %get-tuple-element.230.own_ref), channel_id=1, source_target_pairs={{1,0},{2,1},{3,2},{5,4},{6,5},{7,6},{9,8},{10,9},{11,10},{13,12},{... | collective-permute-start | bytes 1572872 | tf_op jit(solution)/shard_map/ppermute | solution.py:579
  208.6 14.8 %collective-permute-start.11 = (bf16[128,2048]{1,0:T(8,128)(2,1)S(1)}, bf16[128,2048]{1,0:T(8,128)(2,1)S(1)}, u32[]{:S(2)}, u32[]{:S(2)}) collective-permute-start(bf16[128,2048]{1,0:T(8,128)(2,1)S(1)} %get-tuple-element.230.own_ref), channel_id=1, source_target_pairs={{0,1},{1,2},{2,3},{4,5},{5,6},{6,7},{8,9},{9,10},{10,11},{12,13},{... | collective-permute-start | bytes 1572872 | tf_op jit(solution)/shard_map/ppermute | solution.py:579
  223.5 30.8 %collective-permute-start.16 = (bf16[320,2048]{1,0:T(8,128)(2,1)S(1)}, bf16[320,2048]{1,0:T(8,128)(2,1)S(1)}, u32[]{:S(2)}, u32[]{:S(2)}) collective-permute-start(bf16[320,2048]{1,0:T(8,128)(2,1)S(1)} %slice.17), channel_id=1, source_target_pairs={{0,1},{3,2},{4,5},{7,6},{8,9},{11,10},{12,13},{15,14},{16,17},{19,... | collective-permute-start | bytes 3932168 | tf_op jit(solution)/shard_map/ppermute | solution.py:596
  228.1 24.1 %collective-permute-start.14 = (bf16[128,2048]{1,0:T(8,128)(2,1)S(1)}, bf16[128,2048]{1,0:T(8,128)(2,1)S(1)}, u32[]{:S(2)}, u32[]{:S(2)}) collective-permute-start(bf16[128,2048]{1,0:T(8,128)(2,1)S(1)} %get-tuple-element.247), channel_id=1, source_target_pairs={{1,0},{2,3},{5,4},{6,7},{9,8},{10,11},{13,12},{14,15},{17,16},{18,... | collective-permute-start | bytes 1572872 | tf_op jit(solution)/shard_map/ppermute | solution.py:589
  229.4 22.8 %collective-permute-start.15 = (bf16[128,2048]{1,0:T(8,128)(2,1)S(1)}, bf16[128,2048]{1,0:T(8,128)(2,1)S(1)}, u32[]{:S(2)}, u32[]{:S(2)}) collective-permute-start(bf16[128,2048]{1,0:T(8,128)(2,1)S(1)} %get-tuple-element.248), channel_id=1, source_target_pairs={{1,3},{2,0},{5,7},{6,4},{9,11},{10,8},{13,15},{14,12},{17,19},{18,... | collective-permute-start | bytes 1572872 | tf_op jit(solution)/shard_map/ppermute | solution.py:590
  230.7 21.5 %collective-permute-start.13 = (bf16[128,2048]{1,0:T(8,128)(2,1)S(1)}, bf16[128,2048]{1,0:T(8,128)(2,1)S(1)}, u32[]{:S(2)}, u32[]{:S(2)}) collective-permute-start(bf16[128,2048]{1,0:T(8,128)(2,1)S(1)} %get-tuple-element.248), channel_id=1, source_target_pairs={{1,2},{2,1},{5,6},{6,5},{9,10},{10,9},{13,14},{14,13},{17,18},{18,... | collective-permute-start | bytes 1572872 | tf_op jit(solution)/shard_map/ppermute | solution.py:588
  231.5 46.5 %copy-start.41 = (bf16[192,2048]{1,0:T(8,128)(2,1)}, bf16[192,2048]{1,0:T(8,128)(2,1)S(1)}, u32[]{:S(2)}) copy-start(bf16[192,2048]{1,0:T(8,128)(2,1)S(1)} %slice.16) | copy-start | bytes 2359300
  231.5 20.9 %copy-start.51 = (bf16[640,2048]{1,0:T(8,128)(2,1)S(1)}, bf16[640,2048]{1,0:T(8,128)(2,1)}, u32[]{:S(2)}) copy-start(bf16[640,2048]{1,0:T(8,128)(2,1)} %param.22) | copy-start | bytes 7864324
  254.9 31.6 %collective-permute-start.18 = (bf16[320,2048]{1,0:T(8,128)(2,1)S(1)}, bf16[320,2048]{1,0:T(8,128)(2,1)S(1)}, u32[]{:S(2)}, u32[]{:S(2)}) collective-permute-start(bf16[320,2048]{1,0:T(8,128)(2,1)S(1)} %fusion.11), channel_id=1, source_target_pairs={{1,2},{2,1},{5,6},{6,5},{9,10},{10,9},{13,14},{14,13},{17,18},{18,... | collective-permute-start | bytes 3932168 | tf_op jit(solution)/shard_map/ppermute | solution.py:596
  255.8 22.2 %collective-permute-start.17 = (bf16[192,2048]{1,0:T(8,128)(2,1)S(1)}, bf16[192,2048]{1,0:T(8,128)(2,1)S(1)}, u32[]{:S(2)}, u32[]{:S(2)}) collective-permute-start(bf16[192,2048]{1,0:T(8,128)(2,1)S(1)} %slice.16), channel_id=1, source_target_pairs={{0,1},{3,2},{4,5},{7,6},{8,9},{11,10},{12,13},{15,14},{16,17},{19,... | collective-permute-start | bytes 2359304 | tf_op jit(solution)/shard_map/ppermute | solution.py:596
  279.1 40.6 %collective-permute-start.24 = (bf16[192,2048]{1,0:T(8,128)(2,1)}, bf16[192,2048]{1,0:T(8,128)(2,1)}, u32[]{:S(2)}, u32[]{:S(2)}) collective-permute-start(bf16[192,2048]{1,0:T(8,128)(2,1)} %fusion.13), channel_id=1, source_target_pairs={{1,2},{2,1},{5,6},{6,5},{9,10},{10,9},{13,14},{14,13},{17,18},{18,... | collective-permute-start | bytes 2359304 | tf_op jit(solution)/shard_map/ppermute | solution.py:596
  288.1 4.8 %collective-permute-start.19 = (f32[8,640]{1,0:T(8,128)S(1)}, f32[8,640]{1,0:T(8,128)S(1)}, u32[]{:S(2)}, u32[]{:S(2)}) collective-permute-start(f32[8,640]{1,0:T(8,128)S(1)} %get-tuple-element.145), channel_id=1, source_target_pairs={{4,0},{8,4},{12,8},{16,12},{20,16},{24,20},{28,24},{5,1},{9,5},{13... | collective-permute-start | bytes 61448 | tf_op jit(solution)/shard_map/ppermute | solution.py:810
  291.6 36.2 %collective-permute-start.23 = (bf16[320,2048]{1,0:T(8,128)(2,1)}, bf16[320,2048]{1,0:T(8,128)(2,1)}, u32[]{:S(2)}, u32[]{:S(2)}) collective-permute-start(bf16[320,2048]{1,0:T(8,128)(2,1)} %fusion.12), channel_id=1, source_target_pairs={{2,3},{1,0},{6,7},{5,4},{10,11},{9,8},{14,15},{13,12},{18,19},{17,... | collective-permute-start | bytes 3932168 | tf_op jit(solution)/shard_map/ppermute | solution.py:596
  296.0 23.7 %collective-permute-start.22 = (bf16[128,2048]{1,0:T(8,128)(2,1)}, bf16[128,2048]{1,0:T(8,128)(2,1)}, u32[]{:S(2)}, u32[]{:S(2)}) collective-permute-start(bf16[128,2048]{1,0:T(8,128)(2,1)} %get-tuple-element.239), channel_id=1, source_target_pairs={{0,2},{3,1},{4,6},{7,5},{8,10},{11,9},{12,14},{15,13},{16,18},{19,... | collective-permute-start | bytes 1572872 | tf_op jit(solution)/shard_map/ppermute | solution.py:565
  304.9 14.8 %collective-permute-start.21 = (bf16[128,2048]{1,0:T(8,128)(2,1)}, bf16[128,2048]{1,0:T(8,128)(2,1)}, u32[]{:S(2)}, u32[]{:S(2)}) collective-permute-start(bf16[128,2048]{1,0:T(8,128)(2,1)} %get-tuple-element.240), channel_id=1, source_target_pairs={{3,2},{2,1},{7,6},{6,5},{11,10},{10,9},{15,14},{14,13},{19,18},{18... | collective-permute-start | bytes 1572872 | tf_op jit(solution)/shard_map/ppermute | solution.py:564
  306.3 21.4 %collective-permute-start.20 = (bf16[128,2048]{1,0:T(8,128)(2,1)}, bf16[128,2048]{1,0:T(8,128)(2,1)}, u32[]{:S(2)}, u32[]{:S(2)}) collective-permute-start(bf16[128,2048]{1,0:T(8,128)(2,1)} %get-tuple-element.240), channel_id=1, source_target_pairs={{0,1},{1,2},{4,5},{5,6},{8,9},{9,10},{12,13},{13,14},{16,17},{17,1... | collective-permute-start | bytes 1572872 | tf_op jit(solution)/shard_map/ppermute | solution.py:563
  332.2 16.1 %collective-permute-start.25 = (bf16[128,2048]{1,0:T(8,128)(2,1)}, bf16[128,2048]{1,0:T(8,128)(2,1)S(1)}, u32[]{:S(2)}, u32[]{:S(2)}) collective-permute-start(bf16[128,2048]{1,0:T(8,128)(2,1)} %get-tuple-element.235), channel_id=1, source_target_pairs={{0,1},{1,2},{2,3},{4,5},{5,6},{6,7},{8,9},{9,10},{10,11},{12,13},{... | collective-permute-start | bytes 1572872 | tf_op jit(solution)/shard_map/ppermute | solution.py:575
  336.6 17.0 %collective-permute-start.26 = (bf16[128,2048]{1,0:T(8,128)(2,1)}, bf16[128,2048]{1,0:T(8,128)(2,1)}, u32[]{:S(2)}, u32[]{:S(2)}) collective-permute-start(bf16[128,2048]{1,0:T(8,128)(2,1)} %get-tuple-element.236), channel_id=1, source_target_pairs={{1,0},{2,1},{3,2},{5,4},{6,5},{7,6},{9,8},{10,9},{11,10},{13,12},{... | collective-permute-start | bytes 1572872 | tf_op jit(solution)/shard_map/ppermute | solution.py:575
  337.9 27.8 %copy-start.48 = (bf16[192,2048]{1,0:T(8,128)(2,1)S(1)}, bf16[192,2048]{1,0:T(8,128)(2,1)}, u32[]{:S(2)}) copy-start(bf16[192,2048]{1,0:T(8,128)(2,1)} %copy-done.47) | copy-start | bytes 2359300
  340.1 30.9 %collective-permute-start.29 = (bf16[192,2048]{1,0:T(8,128)(2,1)S(1)}, bf16[192,2048]{1,0:T(8,128)(2,1)S(1)}, u32[]{:S(2)}, u32[]{:S(2)}) collective-permute-start(bf16[192,2048]{1,0:T(8,128)(2,1)S(1)} %fusion.14), channel_id=1, source_target_pairs={{2,3},{1,0},{6,7},{5,4},{10,11},{9,8},{14,15},{13,12},{18,19},{17,... | collective-permute-start | bytes 2359304 | tf_op jit(solution)/shard_map/ppermute | solution.py:596
  359.1 22.2 %collective-permute-start.28 = (bf16[128,2048]{1,0:T(8,128)(2,1)}, bf16[128,2048]{1,0:T(8,128)(2,1)S(1)}, u32[]{:S(2)}, u32[]{:S(2)}) collective-permute-start(bf16[128,2048]{1,0:T(8,128)(2,1)} %get-tuple-element.228), channel_id=1, source_target_pairs={{1,0},{2,1},{3,2},{5,4},{6,5},{7,6},{9,8},{10,9},{11,10},{13,12},{... | collective-permute-start | bytes 1572872 | tf_op jit(solution)/shard_map/ppermute | solution.py:579
  360.4 20.9 %collective-permute-start.27 = (bf16[128,2048]{1,0:T(8,128)(2,1)}, bf16[128,2048]{1,0:T(8,128)(2,1)}, u32[]{:S(2)}, u32[]{:S(2)}) collective-permute-start(bf16[128,2048]{1,0:T(8,128)(2,1)} %get-tuple-element.228), channel_id=1, source_target_pairs={{0,1},{1,2},{2,3},{4,5},{5,6},{6,7},{8,9},{9,10},{10,11},{12,13},{... | collective-permute-start | bytes 1572872 | tf_op jit(solution)/shard_map/ppermute | solution.py:579
  369.1 17.1 %collective-permute-start.34 = (f32[2,2048]{1,0:T(2,128)S(1)}, f32[2,2048]{1,0:T(2,128)S(1)}, u32[]{:S(2)}, u32[]{:S(2)}) collective-permute-start(f32[2,2048]{1,0:T(2,128)S(1)} %pad_maximum_fusion), channel_id=1, source_target_pairs={{0,2},{1,3},{2,0},{3,1},{4,6},{5,7},{6,4},{7,5},{8,10},{9,11},{10,... | collective-permute-start | bytes 49160 | tf_op jit(solution)/shard_map/ppermute | solution.py:534
  369.1 18.3 %collective-permute-start.35 = (f32[2,2048]{1,0:T(2,128)S(1)}, f32[2,2048]{1,0:T(2,128)S(1)}, u32[]{:S(2)}, u32[]{:S(2)}) collective-permute-start(f32[2,2048]{1,0:T(2,128)S(1)} %pad_maximum_fusion), channel_id=1, source_target_pairs={{0,3},{1,0},{2,1},{3,2},{4,7},{5,4},{6,5},{7,6},{8,11},{9,8},{10,9... | collective-permute-start | bytes 49160 | tf_op jit(solution)/shard_map/ppermute | solution.py:534
  370.9 16.6 %collective-permute-start.33 = (f32[2,2048]{1,0:T(2,128)S(1)}, f32[2,2048]{1,0:T(2,128)S(1)}, u32[]{:S(2)}, u32[]{:S(2)}) collective-permute-start(f32[2,2048]{1,0:T(2,128)S(1)} %pad_maximum_fusion), channel_id=1, source_target_pairs={{0,1},{1,2},{2,3},{3,0},{4,5},{5,6},{6,7},{7,4},{8,9},{9,10},{10,1... | collective-permute-start | bytes 49160 | tf_op jit(solution)/shard_map/ppermute | solution.py:534
  383.4 27.0 %collective-permute-start.32 = (bf16[128,2048]{1,0:T(8,128)(2,1)}, bf16[128,2048]{1,0:T(8,128)(2,1)}, u32[]{:S(2)}, u32[]{:S(2)}) collective-permute-start(bf16[128,2048]{1,0:T(8,128)(2,1)} %get-tuple-element.246), channel_id=1, source_target_pairs={{1,3},{2,0},{5,7},{6,4},{9,11},{10,8},{13,15},{14,12},{17,19},{18,... | collective-permute-start | bytes 1572872 | tf_op jit(solution)/shard_map/ppermute | solution.py:590
  384.7 25.7 %collective-permute-start.30 = (bf16[128,2048]{1,0:T(8,128)(2,1)}, bf16[128,2048]{1,0:T(8,128)(2,1)}, u32[]{:S(2)}, u32[]{:S(2)}) collective-permute-start(bf16[128,2048]{1,0:T(8,128)(2,1)} %get-tuple-element.246), channel_id=1, source_target_pairs={{1,2},{2,1},{5,6},{6,5},{9,10},{10,9},{13,14},{14,13},{17,18},{18,... | collective-permute-start | bytes 1572872 | tf_op jit(solution)/shard_map/ppermute | solution.py:588
  386.2 24.2 %collective-permute-start.31 = (bf16[128,2048]{1,0:T(8,128)(2,1)}, bf16[128,2048]{1,0:T(8,128)(2,1)}, u32[]{:S(2)}, u32[]{:S(2)}) collective-permute-start(bf16[128,2048]{1,0:T(8,128)(2,1)} %get-tuple-element.245), channel_id=1, source_target_pairs={{1,0},{2,3},{5,4},{6,7},{9,8},{10,11},{13,12},{14,15},{17,16},{18,... | collective-permute-start | bytes 1572872 | tf_op jit(solution)/shard_map/ppermute | solution.py:589
  (53 other events, 347.3 us)
Sparse Core Ops, SparseCore 0:
  12.4 35.1 all-gather.10
  49.5 62.3 all-gather.12
  183.8 127.1 reduce-scatter.2
  327.9 72.9 reduce-scatter.4

commit v3 on v2

--- a/solution.py
+++ b/solution.py
@@ -294,7 +294,7 @@
 
 def add_projection(
     own_ref, left_ref, right_ref, over_ref, back_ref, far_ref, weight_ref, inputs_ref, gain_ref, index_ref,
-    residual_ref, normed_ref, inverse_ref,
+    residual_ref, normed_ref,
     mixed, rows,
 ):
     tokens, channels = own_ref.shape
@@ -302,7 +302,11 @@
     step = pl.program_id(0)
 
     def store(source, ref):
-        mixed[:, source * channels : (source + 1) * channels] = ref[...]
+        def copy(row):
+            at = pl.ds(row, rows_at_once)
+            mixed[at, source * channels : (source + 1) * channels] = ref[at, :]
+
+        over_rows(tokens, copy)
 
     @pl.when(step == 0)
     def _():
@@ -318,7 +322,6 @@
             at = pl.ds(row, rows_at_once)
             values = rows[at, :]
             inverse = inverse_rms(values)
-            inverse_ref[at, :] = inverse
             normed_ref[at, :] = (values * inverse * gain_ref[...]).astype(bf16)
 
         over_rows(tokens, normalise)
@@ -342,14 +345,13 @@
             whole(1, width),
             pl.BlockSpec(memory_space=pltpu.SMEM),
         ],
-        out_specs=[pl.BlockSpec((tokens, columns), lambda j: (0, j)), whole(tokens, width), whole(tokens, 1)],
+        out_specs=[pl.BlockSpec((tokens, columns), lambda j: (0, j)), whole(tokens, width)],
         out_shape=[
             jax.ShapeDtypeStruct((tokens, width), f32),
             jax.ShapeDtypeStruct((tokens, width), bf16),
-            jax.ShapeDtypeStruct((tokens, 1), f32),
         ],
         scratch_shapes=[pltpu.VMEM((tokens, depth), bf16), pltpu.VMEM((tokens, width), f32)],
-        compiler_params=pltpu.CompilerParams(vmem_limit_bytes=48 << 20),
+        compiler_params=pltpu.CompilerParams(vmem_limit_bytes=60 << 20),
         cost_estimate=pl.CostEstimate(
             flops=2 * tokens * depth * width,
             bytes_accessed=2 * (depth * width + 5 * tokens * width),
@@ -362,22 +364,32 @@
     size, width = own.shape
     peers = lax.axis_size("head")
 
-    def body(own_ref, left_ref, right_ref, over_ref, back_ref, far_ref, index_ref, out_ref):
+    def body(index_ref, own_ref, left_ref, right_ref, over_ref, back_ref, far_ref, out_ref):
+        step = pl.program_id(0)
+
         def store(source, ref):
-            out_ref[source * size : (source + 1) * size, :] = ref[...].astype(kind)
+            @pl.when(step == source)
+            def _():
+                def copy(row):
+                    at = pl.ds(row, rows_at_once)
+                    out_ref[at, :] = ref[at, :].astype(kind)
+
+                over_rows(size, copy)
 
         place(index_ref[0], own_ref, (left_ref, right_ref, over_ref, back_ref, far_ref), store)
 
-    return call(
+    return pl.pallas_call(
         body,
-        [jax.ShapeDtypeStruct((peers * size, width), kind)],
-        [],
-        own,
-        *first,
-        *second,
-        index,
-        scalars=1,
-    )[0]
+        grid_spec=pltpu.PrefetchScalarGridSpec(
+            num_scalar_prefetch=1,
+            grid=(peers,),
+            in_specs=[pl.BlockSpec((size, width), lambda i, m: (0, 0))] * 6,
+            out_specs=pl.BlockSpec((size, width), lambda i, m: (i, 0)),
+        ),
+        out_shape=jax.ShapeDtypeStruct((peers * size, width), kind),
+        compiler_params=pltpu.CompilerParams(vmem_limit_bytes=26 << 20),
+        cost_estimate=pl.CostEstimate(flops=1000, bytes_accessed=1000, transcendentals=0),
+    )(index, own, *first, *second)
 
 
 def weight_grads(products, extra=None):
@@ -422,9 +434,15 @@
     span = width // count
 
     def body(in_ref, *out_refs):
-        for k, ref in enumerate(out_refs):
-            part = in_ref[:, k * span : (k + 1) * span].astype(f32)
-            ref[...] = part.T if k == count - 1 else part
+        def convert(row):
+            at = pl.ds(row, rows_at_once)
+            for k, ref in enumerate(out_refs[:-1]):
+                ref[at, :] = in_ref[at, k * span : (k + 1) * span].astype(f32)
+
+        over_rows(rows, convert)
+        for place in range(0, span, 128):
+            part = in_ref[:, (count - 1) * span + place : (count - 1) * span + place + 128]
+            out_refs[-1][place : place + 128, :] = part.astype(f32).T
 
     shapes = [jax.ShapeDtypeStruct((rows, span), f32)] * (count - 1)
     return call(body, [*shapes, jax.ShapeDtypeStruct((span, rows), f32)], [], summed)
@@ -435,8 +453,12 @@
     patch, kept = block_width // owners, channels // owners
 
     def body(in_ref, gate_ref, input_ref, out_ref, taps_ref, recur_ref, inward_ref, decay_ref):
-        gate_ref[...] = in_ref[:, 0:channels].astype(f32)
-        input_ref[...] = in_ref[:, channels : 2 * channels].astype(f32)
+        def convert(row):
+            at = pl.ds(row, rows_at_once)
+            gate_ref[at, :] = in_ref[at, 0:channels].astype(f32)
+            input_ref[at, :] = in_ref[at, channels : 2 * channels].astype(f32)
+
+        over_rows(rows, convert)
         out_ref[...] = in_ref[:, 2 * channels : 3 * channels].astype(f32).T
         small = in_ref[:, 3 * channels :].astype(f32)
         _, lanes = packed_shape(blocks, block_width, taps, owners, owners * rows)
@@ -469,8 +491,13 @@
     cut = last[0].shape[0]
 
     def body(base_ref, first_ref, second_ref, out_ref):
-        out_ref[0:cut, :] = (base_ref[0:cut, :] + first_ref[...].astype(f32)).astype(bf16)
-        out_ref[cut:, :] = (base_ref[cut:, :] + second_ref[...].astype(f32)).astype(bf16)
+        for start, ref in ((0, first_ref), (cut, second_ref)):
+
+            def add(row):
+                at = pl.ds(start + row, rows_at_once)
+                out_ref[at, :] = (base_ref[at, :] + ref[pl.ds(row, rows_at_once), :].astype(f32)).astype(bf16)
+
+            over_rows(ref.shape[0], add)
 
     return call(body, [jax.ShapeDtypeStruct(base.shape, bf16)], [], base, *last)[0]
 
@@ -566,12 +593,59 @@
     )
 
 
-def scatter_second(low, first):
-    me = lax.axis_index("head")
+def by_rows(body, index, shares, rest, outputs, grant=60 << 20):
+    peers = lax.axis_size("head")
+    arrays = [array for array, _ in shares]
+    rows = min(array.shape[0] // (1 if where is None else peers) for array, where in shares)
+    size = min(rows, 64)
+    steps = rows // size
+
+    def row_spec(array, where):
+        if where is None:
+            return pl.BlockSpec((size, array.shape[1]), lambda i, m: (i, 0))
+        return pl.BlockSpec(
+            (size, array.shape[1]), lambda i, m, where=where: (lax.rem(m[0] + where + peers, peers) * steps + i, 0)
+        )
+
+    return pl.pallas_call(
+        body,
+        grid_spec=pltpu.PrefetchScalarGridSpec(
+            num_scalar_prefetch=1,
+            grid=(steps,),
+            in_specs=[row_spec(*share) for share in shares]
+            + [pl.BlockSpec(array.shape, lambda i, m: (0, 0)) for array in rest],
+            out_specs=[
+                pl.BlockSpec((1, width), lambda i, m: (0, 0))
+                if height == 1
+                else pl.BlockSpec((size, width), lambda i, m: (i, 0))
+                for (height, width), _ in outputs
+            ],
+        ),
+        out_shape=[jax.ShapeDtypeStruct(shape, kind) for shape, kind in outputs],
+        compiler_params=pltpu.CompilerParams(vmem_limit_bytes=grant),
+        cost_estimate=pl.CostEstimate(flops=1000, bytes_accessed=1000, transcendentals=0),
+    )(index, *arrays, *rest)
+
+
+def both_ways(me_ref, right_ref, left_ref, from_left_ref, from_right_ref, far_ref, to_right_ref, to_left_ref):
+    far = far_ref[...].astype(f32)
+    me = me_ref[0]
+    to_right = right_ref[...].astype(f32) + from_left_ref[...].astype(f32)
+    to_right_ref[...] = (to_right + jnp.where(me == 2, far, 0.0)).astype(bf16)
+    to_left = left_ref[...].astype(f32) + from_right_ref[...].astype(f32)
+    to_left_ref[...] = (to_left + jnp.where(me == 1, far, 0.0)).astype(bf16)
+
+
+def scatter_second(low, first, index):
     from_left, from_right, far = first
-    none = jnp.zeros_like(far)
-    to_right = added(shard(low, me + 1), from_left, jnp.where(me == 2, far, none)).astype(bf16)
-    to_left = added(shard(low, me - 1), from_right, jnp.where(me == 1, far, none)).astype(bf16)
+    shape = far.shape
+    to_right, to_left = by_rows(
+        both_ways,
+        index,
+        [(low, 1), (low, -1), (from_left, None), (from_right, None), (far, None)],
+        [],
+        [(shape, bf16), (shape, bf16)],
+    )
     return lax.ppermute(to_right, "head", line_pairs(1)), lax.ppermute(to_left, "head", line_pairs(-1))
 
 
@@ -603,11 +677,40 @@
     return lax.rsqrt(jnp.mean(values * values, axis=-1, keepdims=True) + epsilon)
 
 
-def norm_back(values, inverse, scales, grad):
+def sum_up(ref, row):
+    @pl.when(pl.program_id(0) == 0)
+    def _():
+        ref[...] = jnp.zeros(ref.shape, f32)
+
+    ref[...] += row
+
+
+def norm_grads(values, scales, grad):
+    inverse = inverse_rms(values)
     unit = values * inverse
     scaled = grad * scales
     inner = jnp.mean(scaled * unit, axis=-1, keepdims=True)
-    return inverse * (scaled - unit * inner), jnp.sum(grad * unit, axis=0)
+    return inverse * (scaled - unit * inner), jnp.sum(grad * unit, axis=0, keepdims=True)
+
+
+def second_norm(
+    me_ref, own_ref, residual_ref, cotangent_ref, right_ref, left_ref, gain_ref, low_ref, d_resid_ref, sum_ref
+):
+    grad = own_ref[...].astype(f32) + right_ref[...].astype(f32) + left_ref[...].astype(f32)
+    part, gains = norm_grads(residual_ref[...], gain_ref[...], grad)
+    total = cotangent_ref[...].astype(f32) + part
+    d_resid_ref[...] = total
+    low_ref[...] = total.astype(bf16)
+    sum_up(sum_ref, gains)
+
+
+def first_norm(me_ref, own_ref, inputs_ref, right_ref, left_ref, d_resid_ref, gain_ref, low_ref, grad_ref, sum_ref):
+    grad = own_ref[...].astype(f32) + right_ref[...].astype(f32) + left_ref[...].astype(f32)
+    part, gains = norm_grads(inputs_ref[...].astype(f32), gain_ref[...], grad)
+    total = d_resid_ref[...] + part
+    grad_ref[...] = total
+    low_ref[...] = total.astype(bf16)
+    sum_up(sum_ref, gains)
 
 
 def local(
@@ -708,7 +811,7 @@
     second = gather_second(first)
     d_hidden = jnp.einsum("td,fd->tf", cotangent, ffn_down, preferred_element_type=f32)
     second, d_hidden = together((second, d_hidden))
-    residual, normed_two, inverse_two = residual_norm(
+    residual, normed_two = residual_norm(
         mixed_low,
         (*first, *second),
         projection,
@@ -731,13 +834,18 @@
     grad_ffn = weight_grads([(normed_two, d_gpre), (normed_two, d_upre), (cotangent, hidden)])
     first, grad_ffn = together((first, grad_ffn))
     grad_ffn = lax.psum_scatter(grad_ffn, "seq", scatter_dimension=0, tiled=True)
-    second = scatter_second(d_normed_two, first)
+    second = scatter_second(d_normed_two, first, place_index)
     ffn_out = jnp.dot(hidden, ffn_down, preferred_element_type=f32).astype(bf16)
     second, ffn_out = together((second, ffn_out))
-    d_normed_two = added(mine(d_normed_two), *second)
-    d_norm_part, grad_postgain = norm_back(mine(residual), mine(inverse_two), post_gain, d_normed_two)
-    d_resid = mine(cotangent).astype(f32) + d_norm_part
-    d_out_share = d_resid.astype(bf16)
+    own_rows = (share, width)
+    d_out_share, d_resid, grad_postgain = by_rows(
+        second_norm,
+        place_index,
+        [(d_normed_two, 0), (residual, 0), (cotangent, 0), (second[0], None), (second[1], None)],
+        [post_gain[None, :]],
+        [(own_rows, bf16), (own_rows, f32), ((1, width), f32)],
+        grant=26 << 20,
+    )
     first = gather_first(d_out_share)
     first, ffn_out = together((first, ffn_out))
     second = gather_second(first)
@@ -818,32 +926,36 @@
     first = scatter_first(d_normed)
     packed = gate_grads(conv_low, d_both, taps_sums, decay_sums, blocks, seq_count, width)
     grad_rest = weight_grads([(normed, d_gate_low), (normed, d_branch_low), (d_out_low, mixed_low)], packed)
-    first, grad_rest, turn_three, turn_two = together((first, grad_rest, turn_three, turn_two))
-    second = scatter_second(d_normed, first)
+    grad_ffn = finish_ffn(grad_ffn, 3)
+    first, grad_rest, turn_three, turn_two, grad_ffn = together(
+        (first, grad_rest, turn_three, turn_two, grad_ffn)
+    )
+    second = scatter_second(d_normed, first, place_index)
     sent = added(ffn_halves[1], turn_two[1]).astype(bf16)
     turn_three.append(line_turn(3, sent))
     grad_rest = lax.psum_scatter(grad_rest, "seq", scatter_dimension=0, tiled=True)
-    d_normed = added(mine(d_normed), *second)
-    inputs = mine(block_in).astype(f32)
-    inverse_one = inverse_rms(inputs)
-    d_inputs, grad_pregain = norm_back(inputs, inverse_one, pre_gain, d_normed)
-    grad_input = d_resid + d_inputs
-    first = gather_first(grad_input.astype(bf16))
-    gains = jnp.stack([grad_pregain, grad_postgain])
+    grad_low, grad_input, grad_pregain = by_rows(
+        first_norm,
+        place_index,
+        [(d_normed, 0), (block_in, 0), (second[0], None), (second[1], None), (d_resid, None)],
+        [pre_gain[None, :]],
+        [(own_rows, bf16), (own_rows, f32), ((1, width), f32)],
+    )
+    first = gather_first(grad_low)
+    gains = jnp.concatenate([grad_pregain, grad_postgain], axis=0)
     gain_pieces = exchanged(lambda k: gains)
     base = residual + added(ffn_out, jnp.concatenate(turn_one), jnp.concatenate(turn_two))
     block_out = add_last(base, turn_three)
-    grad_ffn = finish_ffn(grad_ffn, 3)
-    first, block_out, grad_ffn = together((first, block_out, grad_ffn))
+    first, block_out = together((first, block_out))
     second = gather_second(first)
     gains = jnp.sum(lax.all_gather(sum(gain_pieces, gains), "seq"), axis=0)
     gain_share = width // seq_count
     gains = lax.dynamic_slice_in_dim(gains, seq_index * gain_share, gain_share, 1)
     grad_rest, grad_ffn = together((grad_rest, grad_ffn))
+    grad_rest = finish_rest(grad_rest, channels, blocks, block_width, tap_count, seq_count)
+    second, grad_rest = together((second, grad_rest))
+    grad_gate_proj, grad_input_proj, grad_out_proj, grad_taps, grad_recur, grad_inward, grad_decay = grad_rest
     grad_input = assembled(grad_input, first, second, place_index, f32)
-    grad_gate_proj, grad_input_proj, grad_out_proj, grad_taps, grad_recur, grad_inward, grad_decay = finish_rest(
-        grad_rest, channels, blocks, block_width, tap_count, seq_count
-    )
     return (
         block_out,
         grad_input,

time: 430 us -> 426 us (level)
  other arithmetic: 30.6 us -> 17 us
  Pallas kernels: 71.9 us -> 83.3 us
  local copies, waits for them, and re-layouts: 27.3 us -> 22.9 us
    pallas_call x0 -> x6, Pallas kernels: none -> 14.4 us  [the longest x4 10.2 us: by_rows(): pl.pallas_call(body, grid_spec=pltpu.PrefetchScalarGridSpec(num_scalar_pr...]
    convert_element_type x4 -> x0, other arithmetic: 11.3 us -> none  [the longest x1 3.31 us: local(): first = gather_first(grad_input.astype(bf16))]
    pallas_call x10 -> x8, Pallas kernels: 31.9 us -> 28 us  [call(): pl.pallas_call(body, out_shape=out_shape, in_specs=[pl.BlockSpec(memory_s...]
    unnamed x124 -> x114, local copies, waits for them, and re-layouts: 20.6 us -> 17.3 us
  transfers between devices with their start and end apart: 40 -> 40, of which waited for: 17 -> 17; matrix products, arithmetic and copies ran while one was open for 15% -> 11% of each run, Pallas kernels for 13% -> 15%
where the time goes in v3:
time: 426 us; the launch traced here: 418 us
  waiting for transfers between devices  114 us (27%)
  starting transfers between devices  84.6 us (20%)
  Pallas kernels  83.3 us (20%)
  matrix products  51.2 us (12%)
  blocking collectives  29.5 us (7%)
  local copies, waits for them, and re-layouts  22.9 us (5%)
  other arithmetic  17 us (4%)
  between operations  15.2 us (4%)
    ppermute x3, waiting for transfers between devices, gather_second(): lax.ppermute(back, 'head', [(1, 0), (2, 3)])  44.7 us
    pallas_call x8, Pallas kernels, call(): pl.pallas_call(body, out_shape=out_shape, in_specs=[pl.BlockSpec(memory_s...  28 us
    ppermute x3, waiting for transfers between devices, gather_first(): lax.ppermute(own, 'head', line_pairs(-1))  26 us
    pallas_call x2, Pallas kernels, weight_grads(): pl.pallas_call(body, grid=(width // block,), in_specs=[pl.BlockSpec((toke...  25 us
    unnamed x114, local copies, waits for them, and re-layouts  17.3 us
    ppermute x6, starting transfers between devices, line_turn(): lax.ppermute(sent, 'head', [(turn - 1, turn), (peers - turn, peers - turn...  16.8 us
    pallas_call x1, Pallas kernels, residual_norm(): pl.pallas_call(add_projection, grid=(blocks,), in_specs=[whole(tokens, ch...  15.9 us
    ppermute x3, starting transfers between devices, gather_first(): lax.ppermute(own, 'head', line_pairs(1))  14.5 us
  transfers between devices with their start and end apart: 40, of which 17 were waited for; matrix products, arithmetic and copies ran while one was open for 11% of the time, Pallas kernels for 15%

profile of v3, /device:TPU:0, one launch (start us, length us, event | category | flops | bytes accessed | tf_op | source)
XLA Modules:
  0.0 417.7 jit_solution(4513433915532022276)
XLA Ops:
  8.2 2.3 collective-permute-start
  21.0 7.5 %shard_map.245 = (bf16[512,640]{1,0:T(8,128)(2,1)S(1)}, f32[512,640]{1,0:T(8,128)S(1)}, f32[512,640]{1,0:T(8,128)S(1)}, f32[5,512,128]{2,1,0:T(8,128)S(1)}, f32[...) custom-call(bf16[512,640]{1,0:T(8,128)(2,1)S(1)} %convolution_convert_fusi, ...), custom_call_target="tpu_custom_call" | custom-call | flops 1000 | bytes 1000 | tf_op jit(solution)/shard_map/pallas_call | solution.py:21
  31.9 10.2 %all-gather.5.ends_ref = f32[8,2,640]{2,1,0:T(2,128)S(1)} all-gather(f32[1,2,640]{2,1,0:T(2,128)S(1)} %bitcast.37), channel_id=3, replica_groups=mesh['seq'=8,'head'=4] {'seq'}, dimensions={0}, use_global_device_ids=true | all-gather | bytes 46080 | tf_op jit(solution)/shard_map/all_gather | solution.py:792
  44.8 2.8 all-gather.11.cloned.1.call-done
  49.0 5.4 %collective-permute-start.1 = (bf16[512,640]{1,0:T(8,128)(2,1)}, bf16[512,640]{1,0:T(8,128)(2,1)}, u32[]{:S(2)}, u32[]{:S(2)}) collective-permute-start(bf16[512,640]{1,0:T(8,128)(2,1)} %copy-done.27), channel_id=1, source_target_pairs={{0,1},{1,2},{2,3},{4,5},{5,6},{6,7},{8,9},{9,10},{10,11},{12,13},{... | collective-permute-start | bytes 1966088 | tf_op jit(solution)/shard_map/ppermute | solution.py:653
  54.4 11.5 %collective-permute-done.2.right_ref = bf16[512,640]{1,0:T(8,128)(2,1)} collective-permute-done((bf16[512,640]{1,0:T(8,128)(2,1)}, bf16[512,640]{1,0:T(8,128)(2,1)}, u32[]{:S(2)}, u32[]{:S(2)}) %collective-permute-start.2) | collective-permute-done | bytes 655392 | tf_op jit(solution)/shard_map/ppermute | solution.py:653
  72.8 8.3 %fusion.23 = f32[512,1536]{1,0:T(8,128)} fusion(bf16[512,2048]{1,0:T(8,128)(2,1)S(1)} %copy-done.18, bf16[1536,2048]{1,0:T(8,128)(2,1)} %param.26), kind=kOutput, calls=%fused_computation.60 | convolution fusion | flops 3221225472 | bytes 11534336 | tf_op jit(solution)/shard_map/td,fd->tf/dot_general | solution.py:812
  81.1 19.0 %collective-permute-done.4.back_ref = bf16[512,640]{1,0:T(8,128)(2,1)S(1)} collective-permute-done((bf16[512,640]{1,0:T(8,128)(2,1)S(1)}, bf16[512,640]{1,0:T(8,128)(2,1)S(1)}, u32[]{:S(2)}, u32[]{:S(2)}) %collective-permute-start.4) | collective-permute-done | bytes 655392 | tf_op jit(solution)/shard_map/ppermute | solution.py:663
  101.8 10.1 %all-gather.13.cloned.1.call-done = bf16[20480,256]{1,0:T(8,128)(2,1)} async-done(((bf16[2560,256]{1,0:T(8,128)(2,1)}), bf16[20480,256]{1,0:T(8,128)(2,1)}) %all-gather.13.cloned.1.call-update) | async-done | bytes 10485776 | tf_op jit(solution)/shard_map/all_gather | solution.py:807
  111.9 15.9 %shard_map.247 = (f32[512,2048]{1,0:T(8,128)}, bf16[512,2048]{1,0:T(8,128)(2,1)}) custom-call(bf16[512,640]{1,0:T(8,128)(2,1)} %copy-done.27, bf16[512,640]{1,0:T(8,128)(2,1)} %collective-permute-done.1.left_ref, bf16[512,640]{1,0:T(8,128)(2,1)} %collective-permute-done.2.right_ref, bf16[512,640]{1,0:T(8,128)(2,1)} %collective-permute-done.3.over_ref, ...), custom_call_target="tpu_custom_call" | custom-call | flops 5368709120 | bytes 20971520 | tf_op jit(solution)/shard_map/pallas_call | solution.py:338
  127.8 6.9 %fusion.24 = f32[512,1536]{1,0:T(8,128)S(1)} fusion(bf16[512,2048]{1,0:T(8,128)(2,1)} %get-tuple-element.128.refs_0_.refs_1_, bf16[2048,1536]{1,0:T(8,128)(2,1)} %param.24), kind=kOutput, calls=%fused_computation.61 | convolution fusion | flops 3221225472 | bytes 11534336 | tf_op jit(solution)/shard_map/dot_general | solution.py:822
  134.7 7.4 %multiply_convert_fusion = (bf16[512,1536]{1,0:T(8,128)(2,1)S(1)}, bf16[512,1536]{1,0:T(8,128)(2,1)S(1)}, bf16[512,1536]{1,0:T(8,128)(2,1)S(1)}) fusion(f32[512,1536]{1,0:T(8,128)S(1)} %fusion.24, f32[512,1536]{1,0:T(8,128)S(1)} %copy-done.51, bf16[512,2048]{1,0:T(8,128)(2,1)S(1)} %copy-done.50, bf16[2048,1536]{1,0:T(8,128)(2,1)} %param.25), kind=kOutput, calls=%fused_computation.19 | convolution fusion | flops 3240886272 | bytes 19398656 | tf_op jit(solution)/shard_map/dot_general | solution.py:823
  142.2 5.1 %fusion.25 = f32[512,2048]{1,0:T(8,128)} fusion(bf16[512,1536]{1,0:T(8,128)(2,1)S(1)} %get-tuple-element.132.refs_4_, bf16[2048,1536]{1,0:T(8,128)(2,1)S(1)} %bitcast.44), kind=kOutput, calls=%fused_computation.62 | convolution fusion | flops 3221225472 | bytes 12058624 | tf_op jit(solution)/shard_map/tf,df->td/dot_general | solution.py:830
  147.3 5.3 %add_convert_fusion.1.right_ref.left_ref.own_ref = bf16[512,2048]{1,0:T(8,128)(2,1)S(1)} fusion(f32[512,2048]{1,0:T(8,128)} %fusion.25, bf16[512,1536]{1,0:T(8,128)(2,1)S(1)} %get-tuple-element.131.refs_3_, bf16[2048,1536]{1,0:T(8,128)(2,1)S(1)} %bitcast.46), kind=kOutput, calls=%fused_computation.9 | convolution fusion | flops 3223322624 | bytes 14155776 | tf_op jit(solution)/shard_map/tf,df->td/dot_general | solution.py:828
  156.4 4.0 collective-permute-start.6
  160.4 3.4 collective-permute-start.8
  163.8 15.0 %shard_map.248 = bf16[2048,4608]{1,0:T(8,128)(2,1)} custom-call(bf16[512,2048]{1,0:T(8,128)(2,1)} %get-tuple-element.128.refs_0_.refs_1_, bf16[512,2048]{1,0:T(8,128)(2,1)} %get-tuple-element.128.refs_0_.refs_1_, bf16[512,2048]{1,0:T(8,128)(2,1)} %cotangent_ref.1, bf16[512,1536]{1,0:T(8,128)(2,1)S(1)} %get-tuple-element.131.refs_3_, ...), custom_call_target="tpu_custom_call" | custom-call | flops 9663676416 | bytes 18874368 | tf_op jit(solution)/shard_map/pallas_call | solution.py:417
  178.8 4.0 collective-permute-done.8.far_ref
  182.9 2.6 shard_map.249
  185.5 4.2 %collective-permute-start.9 = (bf16[128,2048]{1,0:T(8,128)(2,1)}, bf16[128,2048]{1,0:T(8,128)(2,1)S(1)}, u32[]{:S(2)}, u32[]{:S(2)}) collective-permute-start(bf16[128,2048]{1,0:T(8,128)(2,1)} %get-tuple-element.137), channel_id=1, source_target_pairs={{0,1},{1,2},{2,3},{4,5},{5,6},{6,7},{8,9},{9,10},{10,11},{12,13},{... | collective-permute-start | bytes 1572872 | tf_op jit(solution)/shard_map/ppermute | solution.py:649
  191.6 8.6 %convolution_convert_fusion = bf16[512,2048]{1,0:T(8,128)(2,1)S(1)} fusion(bf16[512,1536]{1,0:T(8,128)(2,1)} %copy-done.33, bf16[1536,2048]{1,0:T(8,128)(2,1)} %param.26), kind=kOutput, calls=%fused_computation.23 | convolution fusion | flops 3222274048 | bytes 9961472 | tf_op jit(solution)/shard_map/dot_general | solution.py:838
  200.6 4.6 %collective-permute-done.10.left_ref = bf16[128,2048]{1,0:T(8,128)(2,1)S(1)} collective-permute-done((bf16[128,2048]{1,0:T(8,128)(2,1)}, bf16[128,2048]{1,0:T(8,128)(2,1)S(1)}, u32[]{:S(2)}, u32[]{:S(2)}) %collective-permute-start.10) | collective-permute-done | bytes 524320 | tf_op jit(solution)/shard_map/ppermute | solution.py:649
  207.5 4.6 %collective-permute-start.11 = (bf16[128,2048]{1,0:T(8,128)(2,1)S(1)}, bf16[128,2048]{1,0:T(8,128)(2,1)S(1)}, u32[]{:S(2)}, u32[]{:S(2)}) collective-permute-start(bf16[128,2048]{1,0:T(8,128)(2,1)S(1)} %get-tuple-element.141.own_ref), channel_id=1, source_target_pairs={{0,1},{1,2},{2,3},{4,5},{5,6},{6,7},{8,9},{9,10},{10,11},{12,13},{... | collective-permute-start | bytes 1572872 | tf_op jit(solution)/shard_map/ppermute | solution.py:653
  212.1 7.5 %collective-permute-done.12.right_ref = bf16[128,2048]{1,0:T(8,128)(2,1)S(1)} collective-permute-done((bf16[128,2048]{1,0:T(8,128)(2,1)S(1)}, bf16[128,2048]{1,0:T(8,128)(2,1)S(1)}, u32[]{:S(2)}, u32[]{:S(2)}) %collective-permute-start.12) | collective-permute-done | bytes 524320 | tf_op jit(solution)/shard_map/ppermute | solution.py:653
  220.9 4.5 %collective-permute-start.16 = (bf16[320,2048]{1,0:T(8,128)(2,1)S(1)}, bf16[320,2048]{1,0:T(8,128)(2,1)S(1)}, u32[]{:S(2)}, u32[]{:S(2)}) collective-permute-start(bf16[320,2048]{1,0:T(8,128)(2,1)S(1)} %slice.17), channel_id=1, source_target_pairs={{0,1},{3,2},{4,5},{7,6},{8,9},{11,10},{12,13},{15,14},{16,17},{19,... | collective-permute-start | bytes 3932168 | tf_op jit(solution)/shard_map/ppermute | solution.py:670
  228.9 19.8 %collective-permute-done.14.back_ref = bf16[128,2048]{1,0:T(8,128)(2,1)S(1)} collective-permute-done((bf16[128,2048]{1,0:T(8,128)(2,1)S(1)}, bf16[128,2048]{1,0:T(8,128)(2,1)S(1)}, u32[]{:S(2)}, u32[]{:S(2)}) %collective-permute-start.14) | collective-permute-done | bytes 524320 | tf_op jit(solution)/shard_map/ppermute | solution.py:663
  252.3 7.1 %collective-permute-start.17 = (bf16[192,2048]{1,0:T(8,128)(2,1)S(1)}, bf16[192,2048]{1,0:T(8,128)(2,1)S(1)}, u32[]{:S(2)}, u32[]{:S(2)}) collective-permute-start(bf16[192,2048]{1,0:T(8,128)(2,1)S(1)} %slice.16), channel_id=1, source_target_pairs={{0,1},{3,2},{4,5},{7,6},{8,9},{11,10},{12,13},{15,14},{16,17},{19,... | collective-permute-start | bytes 2359304 | tf_op jit(solution)/shard_map/ppermute | solution.py:670
  259.5 5.6 %shard_map.252 = (bf16[512,640]{1,0:T(8,128)(2,1)S(1)}, f32[5,512,128]{2,1,0:T(8,128)S(1)}, f32[5,512,128]{2,1,0:T(8,128)S(1)}, f32[16,640]{1,0:T(8,128)S(1)}, f32[1,640]{1,0:T(1,128)S(1)}) custom-call(f32[512,640]{1,0:T(8,128)S(1)} %fusion.26.d_mixed_ref, f32[512,640]{1,0:T(8,128)S(1)} %copy-done.12, f32[512,640]{1,0:T(8,128)S(1)} %copy-done.10, ...), custom_call_target="tpu_custom_call" | custom-call | flops 1000 | bytes 1000 | tf_op jit(solution)/shard_map/pallas_call | solution.py:21
  265.1 9.0 %all-gather.6.backs_ref = f32[8,1,640]{2,1,0:T(1,128)S(1)} all-gather(f32[1,1,640]{2,1,0:T(1,128)S(1)} %bitcast.38), channel_id=5, replica_groups=mesh['seq'=8,'head'=4] {'seq'}, dimensions={0}, use_global_device_ids=true | all-gather | bytes 23040 | tf_op jit(solution)/shard_map/all_gather | solution.py:878
  276.8 5.9 %shard_map.253 = (bf16[512,1280]{1,0:T(8,128)(2,1)S(1)}, f32[512,640]{1,0:T(8,128)S(1)}, f32[8,640]{1,0:T(8,128)S(1)}, f32[8,640]{1,0:T(8,128)S(1)}, f32[32,640]{1,0:T(8,128)S(1)}) custom-call(f32[5,512,128]{2,1,0:T(8,128)S(1)} %get-tuple-element.151.local_ref, f32[5,512,128]{2,1,0:T(8,128)S(1)} %get-tuple-element.152.prod_ref, ...), custom_call_target="tpu_custom_call" | custom-call | flops 1000 | bytes 1000 | tf_op jit(solution)/shard_map/pallas_call | solution.py:21
  292.2 7.1 %collective-permute-start.22 = (bf16[128,2048]{1,0:T(8,128)(2,1)}, bf16[128,2048]{1,0:T(8,128)(2,1)}, u32[]{:S(2)}, u32[]{:S(2)}) collective-permute-start(bf16[128,2048]{1,0:T(8,128)(2,1)} %get-tuple-element.251), channel_id=1, source_target_pairs={{0,2},{3,1},{4,6},{7,5},{8,10},{11,9},{12,14},{15,13},{16,18},{19,... | collective-permute-start | bytes 1572872 | tf_op jit(solution)/shard_map/ppermute | solution.py:592
  304.0 10.0 %shard_map.255 = bf16[2048,2048]{1,0:T(8,128)(2,1)} custom-call(bf16[512,2048]{1,0:T(8,128)(2,1)S(1)} %copy-done.4, bf16[512,2048]{1,0:T(8,128)(2,1)S(1)} %copy-done.4, bf16[512,2048]{1,0:T(8,128)(2,1)} %copy-done.6, bf16[512,640]{1,0:T(8,128)(2,1)S(1)} %get-tuple-element.150.refs_3_, bf16[512,640]{1,0:T(8,128)(2,1)S(1)} %add_convert_fusion.2.refs_4_, ...), custom_call_target="tpu_custom_call" | custom-call | flops 4294967296 | bytes 8388608 | tf_op jit(solution)/shard_map/pallas_call | solution.py:417
  315.7 2.4 shard_map.256
  318.1 4.1 collective-permute-done.20.from_left_ref
  322.3 2.6 shard_map.257
  324.9 4.8 %collective-permute-start.25 = (bf16[128,2048]{1,0:T(8,128)(2,1)}, bf16[128,2048]{1,0:T(8,128)(2,1)S(1)}, u32[]{:S(2)}, u32[]{:S(2)}) collective-permute-start(bf16[128,2048]{1,0:T(8,128)(2,1)} %get-tuple-element.182), channel_id=1, source_target_pairs={{0,1},{1,2},{2,3},{4,5},{5,6},{6,7},{8,9},{9,10},{10,11},{12,13},{... | collective-permute-start | bytes 1572872 | tf_op jit(solution)/shard_map/ppermute | solution.py:649
  331.1 2.8 fusion.14
  335.2 6.3 %collective-permute-done.25.right_ref = bf16[128,2048]{1,0:T(8,128)(2,1)S(1)} collective-permute-done((bf16[128,2048]{1,0:T(8,128)(2,1)}, bf16[128,2048]{1,0:T(8,128)(2,1)S(1)}, u32[]{:S(2)}, u32[]{:S(2)}) %collective-permute-start.25) | collective-permute-done | bytes 524320 | tf_op jit(solution)/shard_map/ppermute | solution.py:649
  341.5 5.3 %collective-permute-done.26.left_ref = bf16[128,2048]{1,0:T(8,128)(2,1)} collective-permute-done((bf16[128,2048]{1,0:T(8,128)(2,1)}, bf16[128,2048]{1,0:T(8,128)(2,1)}, u32[]{:S(2)}, u32[]{:S(2)}) %collective-permute-start.26) | collective-permute-done | bytes 524320 | tf_op jit(solution)/shard_map/ppermute | solution.py:649
  346.8 3.9 shard_map.258
  352.1 4.6 %collective-permute-start.27 = (bf16[128,2048]{1,0:T(8,128)(2,1)}, bf16[128,2048]{1,0:T(8,128)(2,1)S(1)}, u32[]{:S(2)}, u32[]{:S(2)}) collective-permute-start(bf16[128,2048]{1,0:T(8,128)(2,1)} %get-tuple-element.185), channel_id=1, source_target_pairs={{0,1},{1,2},{2,3},{4,5},{5,6},{6,7},{8,9},{9,10},{10,11},{12,13},{... | collective-permute-start | bytes 1572872 | tf_op jit(solution)/shard_map/ppermute | solution.py:653
  356.7 5.2 %add_add_fusion.base_ref = f32[512,2048]{1,0:T(8,128)S(1)} fusion(f32[512,2048]{1,0:T(8,128)} %get-tuple-element.130.residual_ref, bf16[512,2048]{1,0:T(8,128)(2,1)} %copy-done.35, bf16[192,2048]{1,0:T(8,128)(2,1)} %copy-done.40, bf16[320,2048]{1,0:T(8,128)(2,1)} %copy-done.38, bf16[192,2048]{1,0:T(8,128)(2,1)} %collective-permute-done.24, ...), kind=kLoop, calls=%fused_computation.7 | loop fusion | flops 12582912 | bytes 14680064 | tf_op jit(solution)/shard_map/add | solution.py:947
  364.2 3.3 shard_map.259
  367.5 7.0 %collective-permute-done.28.right_ref = bf16[128,2048]{1,0:T(8,128)(2,1)S(1)} collective-permute-done((bf16[128,2048]{1,0:T(8,128)(2,1)}, bf16[128,2048]{1,0:T(8,128)(2,1)S(1)}, u32[]{:S(2)}, u32[]{:S(2)}) %collective-permute-start.28) | collective-permute-done | bytes 524320 | tf_op jit(solution)/shard_map/ppermute | solution.py:653
  380.4 10.3 %all-gather.7 = f32[8,2,2048]{2,1,0:T(2,128)S(1)} all-gather(f32[1,2,2048]{2,1,0:T(2,128)S(1)} %add_bitcast_fusion), channel_id=6, replica_groups=mesh['seq'=8,'head'=4] {'seq'}, dimensions={0}, use_global_device_ids=true | all-gather | bytes 147456 | tf_op jit(solution)/shard_map/all_gather | solution.py:951
  391.4 3.3 reduce-scatter.5.cloned.1.call-done.in_ref
  397.3 5.9 %collective-permute-done.31.back_ref = bf16[128,2048]{1,0:T(8,128)(2,1)} collective-permute-done((bf16[128,2048]{1,0:T(8,128)(2,1)}, bf16[128,2048]{1,0:T(8,128)(2,1)}, u32[]{:S(2)}, u32[]{:S(2)}) %collective-permute-start.31) | collective-permute-done | bytes 524320 | tf_op jit(solution)/shard_map/ppermute | solution.py:663
  406.9 3.8 shard_map.261
  (211 shorter events, 81.6 us)
Async XLA Ops:
  7.2 40.4 %all-gather.11.cloned.1.call-start = ((), (), s32[]{:S(2)}) async-start(), calls=%async_computation.4 | async-start | bytes 1638400 | tf_op jit(solution)/shard_map/all_gather | solution.py:755
  8.2 11.4 %collective-permute-start = (bf16[8,2048]{1,0:T(8,128)(2,1)S(1)}, bf16[8,2048]{1,0:T(8,128)(2,1)S(1)}, u32[]{:S(2)}, u32[]{:S(2)}) collective-permute-start(bf16[8,2048]{1,0:T(8,128)(2,1)S(1)} %slice.15), channel_id=1, source_target_pairs={{0,4},{4,8},{8,12},{12,16},{16,20},{20,24},{24,28},{1,5},{5,9},{9,... | collective-permute-start | bytes 98312 | tf_op jit(solution)/shard_map/ppermute | solution.py:752
  12.3 99.6 %all-gather.13.cloned.1.call-start = ((), (), s32[]{:S(2)}) async-start(), calls=%async_computation.5 | async-start | bytes 11796480 | tf_op jit(solution)/shard_map/all_gather | solution.py:807
  19.5 22.6 %copy-start.11 = (f32[512,640]{1,0:T(8,128)}, f32[512,640]{1,0:T(8,128)S(1)}, u32[]{:S(2)}) copy-start(f32[512,640]{1,0:T(8,128)S(1)} %fusion.22.gate_ref) | copy-start | bytes 3932164
  47.6 266.4 %reduce-scatter.3.cloned.1.call-start = ((), (), s32[]{:S(2)}) async-start(), calls=%async_computation.2 | async-start | bytes 21233664 | tf_op jit(solution)/shard_map/reduce_scatter | solution.py:836
  47.7 18.2 %collective-permute-start.2 = (bf16[512,640]{1,0:T(8,128)(2,1)}, bf16[512,640]{1,0:T(8,128)(2,1)}, u32[]{:S(2)}, u32[]{:S(2)}) collective-permute-start(bf16[512,640]{1,0:T(8,128)(2,1)} %copy-done.27), channel_id=1, source_target_pairs={{1,0},{2,1},{3,2},{5,4},{6,5},{7,6},{9,8},{10,9},{11,10},{13,12},{... | collective-permute-start | bytes 1966088 | tf_op jit(solution)/shard_map/ppermute | solution.py:653
  49.0 18.1 %collective-permute-start.1 = (bf16[512,640]{1,0:T(8,128)(2,1)}, bf16[512,640]{1,0:T(8,128)(2,1)}, u32[]{:S(2)}, u32[]{:S(2)}) collective-permute-start(bf16[512,640]{1,0:T(8,128)(2,1)} %copy-done.27), channel_id=1, source_target_pairs={{0,1},{1,2},{2,3},{4,5},{5,6},{6,7},{8,9},{9,10},{10,11},{12,13},{... | collective-permute-start | bytes 1966088 | tf_op jit(solution)/shard_map/ppermute | solution.py:653
  54.4 18.4 %copy-start.18 = (bf16[512,2048]{1,0:T(8,128)(2,1)S(1)}, bf16[512,2048]{1,0:T(8,128)(2,1)}, u32[]{:S(2)}) copy-start(bf16[512,2048]{1,0:T(8,128)(2,1)} %cotangent_ref.1) | copy-start | bytes 6291460
  68.5 31.6 %collective-permute-start.5 = (bf16[512,640]{1,0:T(8,128)(2,1)S(1)}, bf16[512,640]{1,0:T(8,128)(2,1)S(1)}, u32[]{:S(2)}, u32[]{:S(2)}) collective-permute-start(bf16[512,640]{1,0:T(8,128)(2,1)S(1)} %get-tuple-element.256), channel_id=1, source_target_pairs={{1,3},{2,0},{5,7},{6,4},{9,11},{10,8},{13,15},{14,12},{17,19},{18,... | collective-permute-start | bytes 1966088 | tf_op jit(solution)/shard_map/ppermute | solution.py:664
  69.8 32.0 %collective-permute-start.3 = (bf16[512,640]{1,0:T(8,128)(2,1)S(1)}, bf16[512,640]{1,0:T(8,128)(2,1)}, u32[]{:S(2)}, u32[]{:S(2)}) collective-permute-start(bf16[512,640]{1,0:T(8,128)(2,1)S(1)} %get-tuple-element.256), channel_id=1, source_target_pairs={{1,2},{2,1},{5,6},{6,5},{9,10},{10,9},{13,14},{14,13},{17,18},{18,... | collective-permute-start | bytes 1966088 | tf_op jit(solution)/shard_map/ppermute | solution.py:662
  71.3 28.8 %collective-permute-start.4 = (bf16[512,640]{1,0:T(8,128)(2,1)S(1)}, bf16[512,640]{1,0:T(8,128)(2,1)S(1)}, u32[]{:S(2)}, u32[]{:S(2)}) collective-permute-start(bf16[512,640]{1,0:T(8,128)(2,1)S(1)} %get-tuple-element.255), channel_id=1, source_target_pairs={{1,0},{2,3},{5,4},{6,7},{9,8},{10,11},{13,12},{14,15},{17,16},{18,... | collective-permute-start | bytes 1966088 | tf_op jit(solution)/shard_map/ppermute | solution.py:663
  127.8 19.5 %slice-start.2 = ((s8[6291456]{0:T(1024)(128)(4,1)}), s8[4194304]{0:T(1024)(128)(4,1)S(1)}, s32[]{:S(2)}) async-start(s8[6291456]{0:T(1024)(128)(4,1)} %bitcast.45), calls=%async_computation.8 | async-start | bytes 8388608
  142.1 21.7 %copy-start.33 = (bf16[512,1536]{1,0:T(8,128)(2,1)}, bf16[512,1536]{1,0:T(8,128)(2,1)S(1)}, u32[]{:S(2)}) copy-start(bf16[512,1536]{1,0:T(8,128)(2,1)S(1)} %get-tuple-element.133.refs_5_) | copy-start | bytes 4718596
  155.0 27.9 %collective-permute-start.7 = (bf16[128,2048]{1,0:T(8,128)(2,1)}, bf16[128,2048]{1,0:T(8,128)(2,1)}, u32[]{:S(2)}, u32[]{:S(2)}) collective-permute-start(bf16[128,2048]{1,0:T(8,128)(2,1)} %get-tuple-element.254), channel_id=1, source_target_pairs={{3,2},{2,1},{7,6},{6,5},{11,10},{10,9},{15,14},{14,13},{19,18},{18... | collective-permute-start | bytes 1572872 | tf_op jit(solution)/shard_map/ppermute | solution.py:591
  156.4 26.4 %collective-permute-start.6 = (bf16[128,2048]{1,0:T(8,128)(2,1)}, bf16[128,2048]{1,0:T(8,128)(2,1)}, u32[]{:S(2)}, u32[]{:S(2)}) collective-permute-start(bf16[128,2048]{1,0:T(8,128)(2,1)} %get-tuple-element.254), channel_id=1, source_target_pairs={{0,1},{1,2},{4,5},{5,6},{8,9},{9,10},{12,13},{13,14},{16,17},{17,1... | collective-permute-start | bytes 1572872 | tf_op jit(solution)/shard_map/ppermute | solution.py:590
  160.4 22.4 %collective-permute-start.8 = (bf16[128,2048]{1,0:T(8,128)(2,1)}, bf16[128,2048]{1,0:T(8,128)(2,1)}, u32[]{:S(2)}, u32[]{:S(2)}) collective-permute-start(bf16[128,2048]{1,0:T(8,128)(2,1)} %get-tuple-element.253), channel_id=1, source_target_pairs={{0,2},{3,1},{4,6},{7,5},{8,10},{11,9},{12,14},{15,13},{16,18},{19,... | collective-permute-start | bytes 1572872 | tf_op jit(solution)/shard_map/ppermute | solution.py:592
  182.9 211.8 %reduce-scatter.5.cloned.1.call-start = ((), (), s32[]{:S(2)}) async-start(), calls=%async_computation.3 | async-start | bytes 9437184 | tf_op jit(solution)/shard_map/reduce_scatter | solution.py:936
  185.5 15.1 %collective-permute-start.9 = (bf16[128,2048]{1,0:T(8,128)(2,1)}, bf16[128,2048]{1,0:T(8,128)(2,1)S(1)}, u32[]{:S(2)}, u32[]{:S(2)}) collective-permute-start(bf16[128,2048]{1,0:T(8,128)(2,1)} %get-tuple-element.137), channel_id=1, source_target_pairs={{0,1},{1,2},{2,3},{4,5},{5,6},{6,7},{8,9},{9,10},{10,11},{12,13},{... | collective-permute-start | bytes 1572872 | tf_op jit(solution)/shard_map/ppermute | solution.py:649
  189.8 15.4 %collective-permute-start.10 = (bf16[128,2048]{1,0:T(8,128)(2,1)}, bf16[128,2048]{1,0:T(8,128)(2,1)S(1)}, u32[]{:S(2)}, u32[]{:S(2)}) collective-permute-start(bf16[128,2048]{1,0:T(8,128)(2,1)} %get-tuple-element.138), channel_id=1, source_target_pairs={{1,0},{2,1},{3,2},{5,4},{6,5},{7,6},{9,8},{10,9},{11,10},{13,12},{... | collective-permute-start | bytes 1572872 | tf_op jit(solution)/shard_map/ppermute | solution.py:649
  200.2 82.6 %copy-start.35 = (bf16[512,2048]{1,0:T(8,128)(2,1)}, bf16[512,2048]{1,0:T(8,128)(2,1)S(1)}, u32[]{:S(2)}) copy-start(bf16[512,2048]{1,0:T(8,128)(2,1)S(1)} %convolution_convert_fusion) | copy-start | bytes 6291460
  206.2 22.6 %copy-start.24 = (f32[128,2048]{1,0:T(8,128)}, f32[128,2048]{1,0:T(8,128)S(1)}, u32[]{:S(2)}) copy-start(f32[128,2048]{1,0:T(8,128)S(1)} %get-tuple-element.184.d_resid_ref) | copy-start | bytes 3145732
  206.2 13.4 %collective-permute-start.12 = (bf16[128,2048]{1,0:T(8,128)(2,1)S(1)}, bf16[128,2048]{1,0:T(8,128)(2,1)S(1)}, u32[]{:S(2)}, u32[]{:S(2)}) collective-permute-start(bf16[128,2048]{1,0:T(8,128)(2,1)S(1)} %get-tuple-element.141.own_ref), channel_id=1, source_target_pairs={{1,0},{2,1},{3,2},{5,4},{6,5},{7,6},{9,8},{10,9},{11,10},{13,12},{... | collective-permute-start | bytes 1572872 | tf_op jit(solution)/shard_map/ppermute | solution.py:653
  207.5 13.3 %collective-permute-start.11 = (bf16[128,2048]{1,0:T(8,128)(2,1)S(1)}, bf16[128,2048]{1,0:T(8,128)(2,1)S(1)}, u32[]{:S(2)}, u32[]{:S(2)}) collective-permute-start(bf16[128,2048]{1,0:T(8,128)(2,1)S(1)} %get-tuple-element.141.own_ref), channel_id=1, source_target_pairs={{0,1},{1,2},{2,3},{4,5},{5,6},{6,7},{8,9},{9,10},{10,11},{12,13},{... | collective-permute-start | bytes 1572872 | tf_op jit(solution)/shard_map/ppermute | solution.py:653
  220.9 30.0 %collective-permute-start.16 = (bf16[320,2048]{1,0:T(8,128)(2,1)S(1)}, bf16[320,2048]{1,0:T(8,128)(2,1)S(1)}, u32[]{:S(2)}, u32[]{:S(2)}) collective-permute-start(bf16[320,2048]{1,0:T(8,128)(2,1)S(1)} %slice.17), channel_id=1, source_target_pairs={{0,1},{3,2},{4,5},{7,6},{8,9},{11,10},{12,13},{15,14},{16,17},{19,... | collective-permute-start | bytes 3932168 | tf_op jit(solution)/shard_map/ppermute | solution.py:670
  225.5 23.2 %collective-permute-start.14 = (bf16[128,2048]{1,0:T(8,128)(2,1)S(1)}, bf16[128,2048]{1,0:T(8,128)(2,1)S(1)}, u32[]{:S(2)}, u32[]{:S(2)}) collective-permute-start(bf16[128,2048]{1,0:T(8,128)(2,1)S(1)} %get-tuple-element.259), channel_id=1, source_target_pairs={{1,0},{2,3},{5,4},{6,7},{9,8},{10,11},{13,12},{14,15},{17,16},{18,... | collective-permute-start | bytes 1572872 | tf_op jit(solution)/shard_map/ppermute | solution.py:663
  226.8 21.9 %collective-permute-start.15 = (bf16[128,2048]{1,0:T(8,128)(2,1)S(1)}, bf16[128,2048]{1,0:T(8,128)(2,1)S(1)}, u32[]{:S(2)}, u32[]{:S(2)}) collective-permute-start(bf16[128,2048]{1,0:T(8,128)(2,1)S(1)} %get-tuple-element.260), channel_id=1, source_target_pairs={{1,3},{2,0},{5,7},{6,4},{9,11},{10,8},{13,15},{14,12},{17,19},{18,... | collective-permute-start | bytes 1572872 | tf_op jit(solution)/shard_map/ppermute | solution.py:664
  228.1 20.6 %collective-permute-start.13 = (bf16[128,2048]{1,0:T(8,128)(2,1)S(1)}, bf16[128,2048]{1,0:T(8,128)(2,1)S(1)}, u32[]{:S(2)}, u32[]{:S(2)}) collective-permute-start(bf16[128,2048]{1,0:T(8,128)(2,1)S(1)} %get-tuple-element.260), channel_id=1, source_target_pairs={{1,2},{2,1},{5,6},{6,5},{9,10},{10,9},{13,14},{14,13},{17,18},{18,... | collective-permute-start | bytes 1572872 | tf_op jit(solution)/shard_map/ppermute | solution.py:662
  228.8 45.2 %copy-start.37 = (bf16[192,2048]{1,0:T(8,128)(2,1)}, bf16[192,2048]{1,0:T(8,128)(2,1)S(1)}, u32[]{:S(2)}) copy-start(bf16[192,2048]{1,0:T(8,128)(2,1)S(1)} %slice.16) | copy-start | bytes 2359300
  228.8 20.1 %copy-start.43 = (bf16[640,2048]{1,0:T(8,128)(2,1)S(1)}, bf16[640,2048]{1,0:T(8,128)(2,1)}, u32[]{:S(2)}) copy-start(bf16[640,2048]{1,0:T(8,128)(2,1)} %param.22) | copy-start | bytes 7864324
  251.4 31.3 %collective-permute-start.18 = (bf16[320,2048]{1,0:T(8,128)(2,1)S(1)}, bf16[320,2048]{1,0:T(8,128)(2,1)S(1)}, u32[]{:S(2)}, u32[]{:S(2)}) collective-permute-start(bf16[320,2048]{1,0:T(8,128)(2,1)S(1)} %fusion.11), channel_id=1, source_target_pairs={{1,2},{2,1},{5,6},{6,5},{9,10},{10,9},{13,14},{14,13},{17,18},{18,... | collective-permute-start | bytes 3932168 | tf_op jit(solution)/shard_map/ppermute | solution.py:670
  252.3 21.8 %collective-permute-start.17 = (bf16[192,2048]{1,0:T(8,128)(2,1)S(1)}, bf16[192,2048]{1,0:T(8,128)(2,1)S(1)}, u32[]{:S(2)}, u32[]{:S(2)}) collective-permute-start(bf16[192,2048]{1,0:T(8,128)(2,1)S(1)} %slice.16), channel_id=1, source_target_pairs={{0,1},{3,2},{4,5},{7,6},{8,9},{11,10},{12,13},{15,14},{16,17},{19,... | collective-permute-start | bytes 2359304 | tf_op jit(solution)/shard_map/ppermute | solution.py:670
  275.3 42.9 %collective-permute-start.24 = (bf16[192,2048]{1,0:T(8,128)(2,1)}, bf16[192,2048]{1,0:T(8,128)(2,1)}, u32[]{:S(2)}, u32[]{:S(2)}) collective-permute-start(bf16[192,2048]{1,0:T(8,128)(2,1)} %fusion.13), channel_id=1, source_target_pairs={{1,2},{2,1},{5,6},{6,5},{9,10},{10,9},{13,14},{14,13},{17,18},{18,... | collective-permute-start | bytes 2359304 | tf_op jit(solution)/shard_map/ppermute | solution.py:670
  284.3 4.8 %collective-permute-start.19 = (f32[8,640]{1,0:T(8,128)S(1)}, f32[8,640]{1,0:T(8,128)S(1)}, u32[]{:S(2)}, u32[]{:S(2)}) collective-permute-start(f32[8,640]{1,0:T(8,128)S(1)} %get-tuple-element.166), channel_id=1, source_target_pairs={{4,0},{8,4},{12,8},{16,12},{20,16},{24,20},{28,24},{5,1},{9,5},{13... | collective-permute-start | bytes 61448 | tf_op jit(solution)/shard_map/ppermute | solution.py:918
  287.6 34.7 %collective-permute-start.23 = (bf16[320,2048]{1,0:T(8,128)(2,1)}, bf16[320,2048]{1,0:T(8,128)(2,1)}, u32[]{:S(2)}, u32[]{:S(2)}) collective-permute-start(bf16[320,2048]{1,0:T(8,128)(2,1)} %fusion.12), channel_id=1, source_target_pairs={{2,3},{1,0},{6,7},{5,4},{10,11},{9,8},{14,15},{13,12},{18,19},{17,... | collective-permute-start | bytes 3932168 | tf_op jit(solution)/shard_map/ppermute | solution.py:670
  292.2 25.9 %collective-permute-start.22 = (bf16[128,2048]{1,0:T(8,128)(2,1)}, bf16[128,2048]{1,0:T(8,128)(2,1)}, u32[]{:S(2)}, u32[]{:S(2)}) collective-permute-start(bf16[128,2048]{1,0:T(8,128)(2,1)} %get-tuple-element.251), channel_id=1, source_target_pairs={{0,2},{3,1},{4,6},{7,5},{8,10},{11,9},{12,14},{15,13},{16,18},{19,... | collective-permute-start | bytes 1572872 | tf_op jit(solution)/shard_map/ppermute | solution.py:592
  299.3 18.8 %collective-permute-start.21 = (bf16[128,2048]{1,0:T(8,128)(2,1)}, bf16[128,2048]{1,0:T(8,128)(2,1)}, u32[]{:S(2)}, u32[]{:S(2)}) collective-permute-start(bf16[128,2048]{1,0:T(8,128)(2,1)} %get-tuple-element.252), channel_id=1, source_target_pairs={{3,2},{2,1},{7,6},{6,5},{11,10},{10,9},{15,14},{14,13},{19,18},{18... | collective-permute-start | bytes 1572872 | tf_op jit(solution)/shard_map/ppermute | solution.py:591
  300.7 21.5 %collective-permute-start.20 = (bf16[128,2048]{1,0:T(8,128)(2,1)}, bf16[128,2048]{1,0:T(8,128)(2,1)}, u32[]{:S(2)}, u32[]{:S(2)}) collective-permute-start(bf16[128,2048]{1,0:T(8,128)(2,1)} %get-tuple-element.252), channel_id=1, source_target_pairs={{0,1},{1,2},{4,5},{5,6},{8,9},{9,10},{12,13},{13,14},{16,17},{17,1... | collective-permute-start | bytes 1572872 | tf_op jit(solution)/shard_map/ppermute | solution.py:590
  324.9 16.6 %collective-permute-start.25 = (bf16[128,2048]{1,0:T(8,128)(2,1)}, bf16[128,2048]{1,0:T(8,128)(2,1)S(1)}, u32[]{:S(2)}, u32[]{:S(2)}) collective-permute-start(bf16[128,2048]{1,0:T(8,128)(2,1)} %get-tuple-element.182), channel_id=1, source_target_pairs={{0,1},{1,2},{2,3},{4,5},{5,6},{6,7},{8,9},{9,10},{10,11},{12,13},{... | collective-permute-start | bytes 1572872 | tf_op jit(solution)/shard_map/ppermute | solution.py:649
  329.8 17.0 %collective-permute-start.26 = (bf16[128,2048]{1,0:T(8,128)(2,1)}, bf16[128,2048]{1,0:T(8,128)(2,1)}, u32[]{:S(2)}, u32[]{:S(2)}) collective-permute-start(bf16[128,2048]{1,0:T(8,128)(2,1)} %get-tuple-element.183), channel_id=1, source_target_pairs={{1,0},{2,1},{3,2},{5,4},{6,5},{7,6},{9,8},{10,9},{11,10},{13,12},{... | collective-permute-start | bytes 1572872 | tf_op jit(solution)/shard_map/ppermute | solution.py:649
  333.9 30.3 %collective-permute-start.29 = (bf16[192,2048]{1,0:T(8,128)(2,1)}, bf16[192,2048]{1,0:T(8,128)(2,1)}, u32[]{:S(2)}, u32[]{:S(2)}) collective-permute-start(bf16[192,2048]{1,0:T(8,128)(2,1)} %fusion.14), channel_id=1, source_target_pairs={{2,3},{1,0},{6,7},{5,4},{10,11},{9,8},{14,15},{13,12},{18,19},{17,... | collective-permute-start | bytes 2359304 | tf_op jit(solution)/shard_map/ppermute | solution.py:670
  350.7 23.8 %collective-permute-start.28 = (bf16[128,2048]{1,0:T(8,128)(2,1)}, bf16[128,2048]{1,0:T(8,128)(2,1)S(1)}, u32[]{:S(2)}, u32[]{:S(2)}) collective-permute-start(bf16[128,2048]{1,0:T(8,128)(2,1)} %get-tuple-element.185), channel_id=1, source_target_pairs={{1,0},{2,1},{3,2},{5,4},{6,5},{7,6},{9,8},{10,9},{11,10},{13,12},{... | collective-permute-start | bytes 1572872 | tf_op jit(solution)/shard_map/ppermute | solution.py:653
  352.1 22.3 %collective-permute-start.27 = (bf16[128,2048]{1,0:T(8,128)(2,1)}, bf16[128,2048]{1,0:T(8,128)(2,1)S(1)}, u32[]{:S(2)}, u32[]{:S(2)}) collective-permute-start(bf16[128,2048]{1,0:T(8,128)(2,1)} %get-tuple-element.185), channel_id=1, source_target_pairs={{0,1},{1,2},{2,3},{4,5},{5,6},{6,7},{8,9},{9,10},{10,11},{12,13},{... | collective-permute-start | bytes 1572872 | tf_op jit(solution)/shard_map/ppermute | solution.py:653
  362.0 17.1 %collective-permute-start.34 = (f32[2,2048]{1,0:T(2,128)S(1)}, f32[2,2048]{1,0:T(2,128)S(1)}, u32[]{:S(2)}, u32[]{:S(2)}) collective-permute-start(f32[2,2048]{1,0:T(2,128)S(1)} %pad_maximum_fusion), channel_id=1, source_target_pairs={{0,2},{1,3},{2,0},{3,1},{4,6},{5,7},{6,4},{7,5},{8,10},{9,11},{10,... | collective-permute-start | bytes 49160 | tf_op jit(solution)/shard_map/ppermute | solution.py:561
  362.1 18.3 %collective-permute-start.35 = (f32[2,2048]{1,0:T(2,128)S(1)}, f32[2,2048]{1,0:T(2,128)S(1)}, u32[]{:S(2)}, u32[]{:S(2)}) collective-permute-start(f32[2,2048]{1,0:T(2,128)S(1)} %pad_maximum_fusion), channel_id=1, source_target_pairs={{0,3},{1,0},{2,1},{3,2},{4,7},{5,4},{6,5},{7,6},{8,11},{9,8},{10,9... | collective-permute-start | bytes 49160 | tf_op jit(solution)/shard_map/ppermute | solution.py:561
  364.2 16.1 %collective-permute-start.33 = (f32[2,2048]{1,0:T(2,128)S(1)}, f32[2,2048]{1,0:T(2,128)S(1)}, u32[]{:S(2)}, u32[]{:S(2)}) collective-permute-start(f32[2,2048]{1,0:T(2,128)S(1)} %pad_maximum_fusion), channel_id=1, source_target_pairs={{0,1},{1,2},{2,3},{3,0},{4,5},{5,6},{6,7},{7,4},{8,9},{9,10},{10,1... | collective-permute-start | bytes 49160 | tf_op jit(solution)/shard_map/ppermute | solution.py:561
  376.3 26.9 %collective-permute-start.32 = (bf16[128,2048]{1,0:T(8,128)(2,1)}, bf16[128,2048]{1,0:T(8,128)(2,1)}, u32[]{:S(2)}, u32[]{:S(2)}) collective-permute-start(bf16[128,2048]{1,0:T(8,128)(2,1)} %get-tuple-element.258), channel_id=1, source_target_pairs={{1,3},{2,0},{5,7},{6,4},{9,11},{10,8},{13,15},{14,12},{17,19},{18,... | collective-permute-start | bytes 1572872 | tf_op jit(solution)/shard_map/ppermute | solution.py:664
  377.6 25.7 %collective-permute-start.30 = (bf16[128,2048]{1,0:T(8,128)(2,1)}, bf16[128,2048]{1,0:T(8,128)(2,1)}, u32[]{:S(2)}, u32[]{:S(2)}) collective-permute-start(bf16[128,2048]{1,0:T(8,128)(2,1)} %get-tuple-element.258), channel_id=1, source_target_pairs={{1,2},{2,1},{5,6},{6,5},{9,10},{10,9},{13,14},{14,13},{17,18},{18,... | collective-permute-start | bytes 1572872 | tf_op jit(solution)/shard_map/ppermute | solution.py:662
  379.1 24.2 %collective-permute-start.31 = (bf16[128,2048]{1,0:T(8,128)(2,1)}, bf16[128,2048]{1,0:T(8,128)(2,1)}, u32[]{:S(2)}, u32[]{:S(2)}) collective-permute-start(bf16[128,2048]{1,0:T(8,128)(2,1)} %get-tuple-element.257), channel_id=1, source_target_pairs={{1,0},{2,3},{5,4},{6,7},{9,8},{10,11},{13,12},{14,15},{17,16},{18,... | collective-permute-start | bytes 1572872 | tf_op jit(solution)/shard_map/ppermute | solution.py:663
  (48 other events, 312.7 us)
Sparse Core Ops, SparseCore 0:
  12.4 35.1 all-gather.10
  49.5 62.3 all-gather.12
  183.0 127.1 reduce-scatter.2
  322.4 72.2 reduce-scatter.4

commit v4 on v3

--- a/solution.py
+++ b/solution.py
@@ -422,7 +422,7 @@
         + [pl.BlockSpec((block, e.shape[1]), lambda i: (i, 0)) for e in extras],
         out_specs=pl.BlockSpec((block, total), lambda i: (i, 0)),
         out_shape=jax.ShapeDtypeStruct((width, total), bf16),
-        compiler_params=pltpu.CompilerParams(vmem_limit_bytes=48 << 20),
+        compiler_params=pltpu.CompilerParams(vmem_limit_bytes=60 << 20),
         cost_estimate=pl.CostEstimate(
             flops=2 * tokens * width * total, bytes_accessed=2 * width * total, transcendentals=0
         ),
@@ -803,7 +803,7 @@
         here,
         scalars=1,
     )
-    column_block, mixed_low = together((column_block, mixed_low))
+    column_block, _ = together((column_block, mixed_low))
     projection = lax.all_gather(column_block, "seq")
     if columns % 128:
         projection = jnp.moveaxis(projection, 0, 1).reshape(1, head_count * channels, width)

time: 426 us -> 424 us (level)
    unnamed x114 -> x118, local copies, waits for them, and re-layouts: 17.3 us -> 18.1 us
  transfers between devices with their start and end apart: 40 -> 40, of which waited for: 17 -> 17; matrix products, arithmetic and copies ran while one was open for 11% -> 11% of each run, Pallas kernels for 15% -> 16%
where the time goes in v4:
time: 424 us; the launch traced here: 416 us
  waiting for transfers between devices  110 us (26%)
  Pallas kernels  86.6 us (20%)
  starting transfers between devices  84.4 us (20%)
  matrix products  49.4 us (12%)
  blocking collectives  29.5 us (7%)
  local copies, waits for them, and re-layouts  23.7 us (6%)
  other arithmetic  17 us (4%)
  between operations  15.3 us (4%)
    ppermute x3, waiting for transfers between devices, gather_second(): lax.ppermute(back, 'head', [(1, 0), (2, 3)])  44.8 us
    pallas_call x2, Pallas kernels, weight_grads(): pl.pallas_call(body, grid=(width // block,), in_specs=[pl.BlockSpec((toke...  28.2 us
    pallas_call x8, Pallas kernels, call(): pl.pallas_call(body, out_shape=out_shape, in_specs=[pl.BlockSpec(memory_s...  28 us
    ppermute x3, waiting for transfers between devices, gather_first(): lax.ppermute(own, 'head', line_pairs(-1))  26 us
    unnamed x118, local copies, waits for them, and re-layouts  18.1 us
    ppermute x6, starting transfers between devices, line_turn(): lax.ppermute(sent, 'head', [(turn - 1, turn), (peers - turn, peers - turn...  16.7 us
    pallas_call x1, Pallas kernels, residual_norm(): pl.pallas_call(add_projection, grid=(blocks,), in_specs=[whole(tokens, ch...  15.9 us
    ppermute x3, starting transfers between devices, gather_first(): lax.ppermute(own, 'head', line_pairs(1))  14.6 us
  transfers between devices with their start and end apart: 40, of which 17 were waited for; matrix products, arithmetic and copies ran while one was open for 11% of the time, Pallas kernels for 16%

profile of v4, /device:TPU:0, one launch (start us, length us, event | category | flops | bytes accessed | tf_op | source)
XLA Modules:
  0.0 416.0 jit_solution(11050754753141583249)
XLA Ops:
  8.2 2.3 collective-permute-start
  12.3 2.2 fusion
  21.0 7.5 %shard_map.245 = (bf16[512,640]{1,0:T(8,128)(2,1)S(1)}, f32[512,640]{1,0:T(8,128)S(1)}, f32[512,640]{1,0:T(8,128)S(1)}, f32[5,512,128]{2,1,0:T(8,128)S(1)}, f32[...) custom-call(bf16[512,640]{1,0:T(8,128)(2,1)S(1)} %convolution_convert_fusi, ...), custom_call_target="tpu_custom_call" | custom-call | flops 1000 | bytes 1000 | tf_op jit(solution)/shard_map/pallas_call | solution.py:21
  31.9 10.2 %all-gather.5.ends_ref = f32[8,2,640]{2,1,0:T(2,128)S(1)} all-gather(f32[1,2,640]{2,1,0:T(2,128)S(1)} %bitcast.37), channel_id=2, replica_groups=mesh['seq'=8,'head'=4] {'seq'}, dimensions={0}, use_global_device_ids=true | all-gather | bytes 46080 | tf_op jit(solution)/shard_map/all_gather | solution.py:792
  44.9 2.7 all-gather.11.cloned.1.call-done
  49.0 5.4 %collective-permute-start.1 = (bf16[512,640]{1,0:T(8,128)(2,1)}, bf16[512,640]{1,0:T(8,128)(2,1)}, u32[]{:S(2)}, u32[]{:S(2)}) collective-permute-start(bf16[512,640]{1,0:T(8,128)(2,1)} %copy-done.26), channel_id=1, source_target_pairs={{0,1},{1,2},{2,3},{4,5},{5,6},{6,7},{8,9},{9,10},{10,11},{12,13},{... | collective-permute-start | bytes 1966088 | tf_op jit(solution)/shard_map/ppermute | solution.py:653
  54.4 11.5 %collective-permute-done.2.right_ref = bf16[512,640]{1,0:T(8,128)(2,1)} collective-permute-done((bf16[512,640]{1,0:T(8,128)(2,1)}, bf16[512,640]{1,0:T(8,128)(2,1)}, u32[]{:S(2)}, u32[]{:S(2)}) %collective-permute-start.2) | collective-permute-done | bytes 655392 | tf_op jit(solution)/shard_map/ppermute | solution.py:653
  72.8 8.3 %fusion.23 = f32[512,1536]{1,0:T(8,128)} fusion(bf16[512,2048]{1,0:T(8,128)(2,1)S(1)} %copy-done.17, bf16[1536,2048]{1,0:T(8,128)(2,1)} %param.26), kind=kOutput, calls=%fused_computation.60 | convolution fusion | flops 3221225472 | bytes 11534336 | tf_op jit(solution)/shard_map/td,fd->tf/dot_general | solution.py:812
  81.1 19.0 %collective-permute-done.4.back_ref = bf16[512,640]{1,0:T(8,128)(2,1)S(1)} collective-permute-done((bf16[512,640]{1,0:T(8,128)(2,1)S(1)}, bf16[512,640]{1,0:T(8,128)(2,1)S(1)}, u32[]{:S(2)}, u32[]{:S(2)}) %collective-permute-start.4) | collective-permute-done | bytes 655392 | tf_op jit(solution)/shard_map/ppermute | solution.py:663
  101.8 10.1 %all-gather.13.cloned.1.call-done = bf16[20480,256]{1,0:T(8,128)(2,1)} async-done(((bf16[2560,256]{1,0:T(8,128)(2,1)}), bf16[20480,256]{1,0:T(8,128)(2,1)}) %all-gather.13.cloned.1.call-update) | async-done | bytes 10485776 | tf_op jit(solution)/shard_map/all_gather | solution.py:807
  111.9 15.9 %shard_map.247 = (f32[512,2048]{1,0:T(8,128)}, bf16[512,2048]{1,0:T(8,128)(2,1)}) custom-call(bf16[512,640]{1,0:T(8,128)(2,1)} %copy-done.26, bf16[512,640]{1,0:T(8,128)(2,1)} %collective-permute-done.1.left_ref, bf16[512,640]{1,0:T(8,128)(2,1)} %collective-permute-done.2.right_ref, bf16[512,640]{1,0:T(8,128)(2,1)} %collective-permute-done.3.over_ref, ...), custom_call_target="tpu_custom_call" | custom-call | flops 5368709120 | bytes 20971520 | tf_op jit(solution)/shard_map/pallas_call | solution.py:338
  127.8 6.8 %fusion.24 = f32[512,1536]{1,0:T(8,128)S(1)} fusion(bf16[512,2048]{1,0:T(8,128)(2,1)} %get-tuple-element.126.refs_0_.refs_1_, bf16[2048,1536]{1,0:T(8,128)(2,1)} %param.24), kind=kOutput, calls=%fused_computation.61 | convolution fusion | flops 3221225472 | bytes 11534336 | tf_op jit(solution)/shard_map/dot_general | solution.py:822
  134.7 9.1 %multiply_convert_fusion = (bf16[512,1536]{1,0:T(8,128)(2,1)}, bf16[512,1536]{1,0:T(8,128)(2,1)S(1)}, bf16[512,1536]{1,0:T(8,128)(2,1)S(1)}) fusion(f32[512,1536]{1,0:T(8,128)S(1)} %fusion.24, f32[512,1536]{1,0:T(8,128)S(1)} %copy-done.53, bf16[512,2048]{1,0:T(8,128)(2,1)S(1)} %copy-done.50, bf16[2048,1536]{1,0:T(8,128)(2,1)} %param.25), kind=kOutput, calls=%fused_computation.19 | convolution fusion | flops 3240886272 | bytes 19398656 | tf_op jit(solution)/shard_map/dot_general | solution.py:823
  143.8 3.4 fusion.25
  147.3 3.7 add_convert_fusion.1.right_ref.left_ref.own_ref
  154.8 4.0 collective-permute-start.6
  158.8 3.6 collective-permute-start.8
  162.4 16.6 %shard_map.248 = bf16[2048,4608]{1,0:T(8,128)(2,1)} custom-call(bf16[512,2048]{1,0:T(8,128)(2,1)} %get-tuple-element.126.refs_0_.refs_1_, bf16[512,2048]{1,0:T(8,128)(2,1)} %get-tuple-element.126.refs_0_.refs_1_, bf16[512,2048]{1,0:T(8,128)(2,1)} %cotangent_ref.1, bf16[512,1536]{1,0:T(8,128)(2,1)} %copy-done.51, bf16[512,1536]{1,0:T(8,128)(2,1)} %copy-done.52, ...), custom_call_target="tpu_custom_call" | custom-call | flops 9663676416 | bytes 18874368 | tf_op jit(solution)/shard_map/pallas_call | solution.py:417
  179.0 2.2 collective-permute-done.8.far_ref
  181.3 2.6 shard_map.249
  183.9 4.2 %collective-permute-start.9 = (bf16[128,2048]{1,0:T(8,128)(2,1)}, bf16[128,2048]{1,0:T(8,128)(2,1)S(1)}, u32[]{:S(2)}, u32[]{:S(2)}) collective-permute-start(bf16[128,2048]{1,0:T(8,128)(2,1)} %get-tuple-element.135), channel_id=1, source_target_pairs={{0,1},{1,2},{2,3},{4,5},{5,6},{6,7},{8,9},{9,10},{10,11},{12,13},{... | collective-permute-start | bytes 1572872 | tf_op jit(solution)/shard_map/ppermute | solution.py:649
  189.8 8.5 %convolution_convert_fusion = bf16[512,2048]{1,0:T(8,128)(2,1)S(1)} fusion(bf16[512,1536]{1,0:T(8,128)(2,1)} %get-tuple-element.131.refs_5_, bf16[1536,2048]{1,0:T(8,128)(2,1)} %param.26), kind=kOutput, calls=%fused_computation.23 | convolution fusion | flops 3222274048 | bytes 9961472 | tf_op jit(solution)/shard_map/dot_general | solution.py:838
  199.0 4.6 %collective-permute-done.10.left_ref = bf16[128,2048]{1,0:T(8,128)(2,1)S(1)} collective-permute-done((bf16[128,2048]{1,0:T(8,128)(2,1)}, bf16[128,2048]{1,0:T(8,128)(2,1)S(1)}, u32[]{:S(2)}, u32[]{:S(2)}) %collective-permute-start.10) | collective-permute-done | bytes 524320 | tf_op jit(solution)/shard_map/ppermute | solution.py:649
  205.9 4.6 %collective-permute-start.11 = (bf16[128,2048]{1,0:T(8,128)(2,1)S(1)}, bf16[128,2048]{1,0:T(8,128)(2,1)S(1)}, u32[]{:S(2)}, u32[]{:S(2)}) collective-permute-start(bf16[128,2048]{1,0:T(8,128)(2,1)S(1)} %get-tuple-element.139.own_ref), channel_id=1, source_target_pairs={{0,1},{1,2},{2,3},{4,5},{5,6},{6,7},{8,9},{9,10},{10,11},{12,13},{... | collective-permute-start | bytes 1572872 | tf_op jit(solution)/shard_map/ppermute | solution.py:653
  210.5 7.5 %collective-permute-done.12.right_ref = bf16[128,2048]{1,0:T(8,128)(2,1)S(1)} collective-permute-done((bf16[128,2048]{1,0:T(8,128)(2,1)S(1)}, bf16[128,2048]{1,0:T(8,128)(2,1)S(1)}, u32[]{:S(2)}, u32[]{:S(2)}) %collective-permute-start.12) | collective-permute-done | bytes 524320 | tf_op jit(solution)/shard_map/ppermute | solution.py:653
  219.3 4.5 %collective-permute-start.16 = (bf16[320,2048]{1,0:T(8,128)(2,1)S(1)}, bf16[320,2048]{1,0:T(8,128)(2,1)S(1)}, u32[]{:S(2)}, u32[]{:S(2)}) collective-permute-start(bf16[320,2048]{1,0:T(8,128)(2,1)S(1)} %slice.17), channel_id=1, source_target_pairs={{0,1},{3,2},{4,5},{7,6},{8,9},{11,10},{12,13},{15,14},{16,17},{19,... | collective-permute-start | bytes 3932168 | tf_op jit(solution)/shard_map/ppermute | solution.py:670
  227.3 19.7 %collective-permute-done.14.back_ref = bf16[128,2048]{1,0:T(8,128)(2,1)S(1)} collective-permute-done((bf16[128,2048]{1,0:T(8,128)(2,1)S(1)}, bf16[128,2048]{1,0:T(8,128)(2,1)S(1)}, u32[]{:S(2)}, u32[]{:S(2)}) %collective-permute-start.14) | collective-permute-done | bytes 524320 | tf_op jit(solution)/shard_map/ppermute | solution.py:663
  250.7 7.1 %collective-permute-start.17 = (bf16[192,2048]{1,0:T(8,128)(2,1)S(1)}, bf16[192,2048]{1,0:T(8,128)(2,1)S(1)}, u32[]{:S(2)}, u32[]{:S(2)}) collective-permute-start(bf16[192,2048]{1,0:T(8,128)(2,1)S(1)} %slice.16), channel_id=1, source_target_pairs={{0,1},{3,2},{4,5},{7,6},{8,9},{11,10},{12,13},{15,14},{16,17},{19,... | collective-permute-start | bytes 2359304 | tf_op jit(solution)/shard_map/ppermute | solution.py:670
  257.9 5.6 %shard_map.252 = (bf16[512,640]{1,0:T(8,128)(2,1)S(1)}, f32[5,512,128]{2,1,0:T(8,128)S(1)}, f32[5,512,128]{2,1,0:T(8,128)S(1)}, f32[16,640]{1,0:T(8,128)S(1)}, f32[1,640]{1,0:T(1,128)S(1)}) custom-call(f32[512,640]{1,0:T(8,128)S(1)} %fusion.26.d_mixed_ref, f32[512,640]{1,0:T(8,128)S(1)} %copy-done.10, f32[512,640]{1,0:T(8,128)S(1)} %copy-done.8, ...), custom_call_target="tpu_custom_call" | custom-call | flops 1000 | bytes 1000 | tf_op jit(solution)/shard_map/pallas_call | solution.py:21
  263.6 9.1 %all-gather.6.backs_ref = f32[8,1,640]{2,1,0:T(1,128)S(1)} all-gather(f32[1,1,640]{2,1,0:T(1,128)S(1)} %bitcast.38), channel_id=5, replica_groups=mesh['seq'=8,'head'=4] {'seq'}, dimensions={0}, use_global_device_ids=true | all-gather | bytes 23040 | tf_op jit(solution)/shard_map/all_gather | solution.py:878
  275.6 5.9 %shard_map.253 = (bf16[512,1280]{1,0:T(8,128)(2,1)S(1)}, f32[512,640]{1,0:T(8,128)S(1)}, f32[8,640]{1,0:T(8,128)S(1)}, f32[8,640]{1,0:T(8,128)S(1)}, f32[32,640]{1,0:T(8,128)S(1)}) custom-call(f32[5,512,128]{2,1,0:T(8,128)S(1)} %get-tuple-element.149.local_ref, f32[5,512,128]{2,1,0:T(8,128)S(1)} %get-tuple-element.150.prod_ref, ...), custom_call_target="tpu_custom_call" | custom-call | flops 1000 | bytes 1000 | tf_op jit(solution)/shard_map/pallas_call | solution.py:21
  290.7 6.8 %collective-permute-start.22 = (bf16[128,2048]{1,0:T(8,128)(2,1)}, bf16[128,2048]{1,0:T(8,128)(2,1)}, u32[]{:S(2)}, u32[]{:S(2)}) collective-permute-start(bf16[128,2048]{1,0:T(8,128)(2,1)} %get-tuple-element.249), channel_id=1, source_target_pairs={{0,2},{3,1},{4,6},{7,5},{8,10},{11,9},{12,14},{15,13},{16,18},{19,... | collective-permute-start | bytes 1572872 | tf_op jit(solution)/shard_map/ppermute | solution.py:592
  303.1 11.6 %shard_map.255 = bf16[2048,2048]{1,0:T(8,128)(2,1)} custom-call(bf16[512,2048]{1,0:T(8,128)(2,1)} %copy-done.35, bf16[512,2048]{1,0:T(8,128)(2,1)} %copy-done.35, bf16[512,2048]{1,0:T(8,128)(2,1)} %copy-done.4, bf16[512,640]{1,0:T(8,128)(2,1)} %copy-done.27, bf16[512,640]{1,0:T(8,128)(2,1)} %copy-done.40, bf16[512,640]{1,0:T(8,128)(2,1)} %copy-done.26, ...), custom_call_target="tpu_custom_call" | custom-call | flops 4294967296 | bytes 8388608 | tf_op jit(solution)/shard_map/pallas_call | solution.py:417
  316.4 2.4 shard_map.256
  320.6 2.6 shard_map.257
  323.2 4.8 %collective-permute-start.25 = (bf16[128,2048]{1,0:T(8,128)(2,1)}, bf16[128,2048]{1,0:T(8,128)(2,1)S(1)}, u32[]{:S(2)}, u32[]{:S(2)}) collective-permute-start(bf16[128,2048]{1,0:T(8,128)(2,1)} %get-tuple-element.180), channel_id=1, source_target_pairs={{0,1},{1,2},{2,3},{4,5},{5,6},{6,7},{8,9},{9,10},{10,11},{12,13},{... | collective-permute-start | bytes 1572872 | tf_op jit(solution)/shard_map/ppermute | solution.py:649
  329.3 2.9 fusion.14
  333.5 6.2 %collective-permute-done.25.right_ref = bf16[128,2048]{1,0:T(8,128)(2,1)S(1)} collective-permute-done((bf16[128,2048]{1,0:T(8,128)(2,1)}, bf16[128,2048]{1,0:T(8,128)(2,1)S(1)}, u32[]{:S(2)}, u32[]{:S(2)}) %collective-permute-start.25) | collective-permute-done | bytes 524320 | tf_op jit(solution)/shard_map/ppermute | solution.py:649
  339.7 5.3 %collective-permute-done.26.left_ref = bf16[128,2048]{1,0:T(8,128)(2,1)} collective-permute-done((bf16[128,2048]{1,0:T(8,128)(2,1)}, bf16[128,2048]{1,0:T(8,128)(2,1)}, u32[]{:S(2)}, u32[]{:S(2)}) %collective-permute-start.26) | collective-permute-done | bytes 524320 | tf_op jit(solution)/shard_map/ppermute | solution.py:649
  345.0 3.9 shard_map.258
  350.4 4.6 %collective-permute-start.27 = (bf16[128,2048]{1,0:T(8,128)(2,1)}, bf16[128,2048]{1,0:T(8,128)(2,1)S(1)}, u32[]{:S(2)}, u32[]{:S(2)}) collective-permute-start(bf16[128,2048]{1,0:T(8,128)(2,1)} %get-tuple-element.183), channel_id=1, source_target_pairs={{0,1},{1,2},{2,3},{4,5},{5,6},{6,7},{8,9},{9,10},{10,11},{12,13},{... | collective-permute-start | bytes 1572872 | tf_op jit(solution)/shard_map/ppermute | solution.py:653
  355.0 5.2 %add_add_fusion.base_ref = f32[512,2048]{1,0:T(8,128)S(1)} fusion(f32[512,2048]{1,0:T(8,128)} %get-tuple-element.128.residual_ref, bf16[512,2048]{1,0:T(8,128)(2,1)} %copy-done.33, bf16[192,2048]{1,0:T(8,128)(2,1)} %copy-done.39, bf16[320,2048]{1,0:T(8,128)(2,1)} %copy-done.37, bf16[192,2048]{1,0:T(8,128)(2,1)} %collective-permute-done.24, ...), kind=kLoop, calls=%fused_computation.7 | loop fusion | flops 12582912 | bytes 14680064 | tf_op jit(solution)/shard_map/add | solution.py:947
  362.5 3.3 shard_map.259
  365.8 7.0 %collective-permute-done.28.right_ref = bf16[128,2048]{1,0:T(8,128)(2,1)S(1)} collective-permute-done((bf16[128,2048]{1,0:T(8,128)(2,1)}, bf16[128,2048]{1,0:T(8,128)(2,1)S(1)}, u32[]{:S(2)}, u32[]{:S(2)}) %collective-permute-start.28) | collective-permute-done | bytes 524320 | tf_op jit(solution)/shard_map/ppermute | solution.py:653
  378.7 10.2 %all-gather.7 = f32[8,2,2048]{2,1,0:T(2,128)S(1)} all-gather(f32[1,2,2048]{2,1,0:T(2,128)S(1)} %add_bitcast_fusion), channel_id=6, replica_groups=mesh['seq'=8,'head'=4] {'seq'}, dimensions={0}, use_global_device_ids=true | all-gather | bytes 147456 | tf_op jit(solution)/shard_map/all_gather | solution.py:951
  389.6 3.3 reduce-scatter.5.cloned.1.call-done.in_ref
  395.5 6.1 %collective-permute-done.31.back_ref = bf16[128,2048]{1,0:T(8,128)(2,1)} collective-permute-done((bf16[128,2048]{1,0:T(8,128)(2,1)}, bf16[128,2048]{1,0:T(8,128)(2,1)}, u32[]{:S(2)}, u32[]{:S(2)}) %collective-permute-start.31) | collective-permute-done | bytes 524320 | tf_op jit(solution)/shard_map/ppermute | solution.py:663
  405.2 3.8 shard_map.261
  (215 shorter events, 82.1 us)
Async XLA Ops:
  7.2 40.4 %all-gather.11.cloned.1.call-start = ((), (), s32[]{:S(2)}) async-start(), calls=%async_computation.4 | async-start | bytes 1638400 | tf_op jit(solution)/shard_map/all_gather | solution.py:755
  8.2 11.4 %collective-permute-start = (bf16[8,2048]{1,0:T(8,128)(2,1)S(1)}, bf16[8,2048]{1,0:T(8,128)(2,1)S(1)}, u32[]{:S(2)}, u32[]{:S(2)}) collective-permute-start(bf16[8,2048]{1,0:T(8,128)(2,1)S(1)} %slice.15), channel_id=1, source_target_pairs={{0,4},{4,8},{8,12},{12,16},{16,20},{20,24},{24,28},{1,5},{5,9},{9,... | collective-permute-start | bytes 98312 | tf_op jit(solution)/shard_map/ppermute | solution.py:752
  12.3 99.6 %all-gather.13.cloned.1.call-start = ((), (), s32[]{:S(2)}) async-start(), calls=%async_computation.5 | async-start | bytes 11796480 | tf_op jit(solution)/shard_map/all_gather | solution.py:807
  19.5 22.6 %copy-start.9 = (f32[512,640]{1,0:T(8,128)}, f32[512,640]{1,0:T(8,128)S(1)}, u32[]{:S(2)}) copy-start(f32[512,640]{1,0:T(8,128)S(1)} %fusion.22.gate_ref) | copy-start | bytes 3932164
  47.6 267.1 %reduce-scatter.3.cloned.1.call-start = ((), (), s32[]{:S(2)}) async-start(), calls=%async_computation.2 | async-start | bytes 21233664 | tf_op jit(solution)/shard_map/reduce_scatter | solution.py:836
  47.7 18.2 %collective-permute-start.2 = (bf16[512,640]{1,0:T(8,128)(2,1)}, bf16[512,640]{1,0:T(8,128)(2,1)}, u32[]{:S(2)}, u32[]{:S(2)}) collective-permute-start(bf16[512,640]{1,0:T(8,128)(2,1)} %copy-done.26), channel_id=1, source_target_pairs={{1,0},{2,1},{3,2},{5,4},{6,5},{7,6},{9,8},{10,9},{11,10},{13,12},{... | collective-permute-start | bytes 1966088 | tf_op jit(solution)/shard_map/ppermute | solution.py:653
  49.0 18.1 %collective-permute-start.1 = (bf16[512,640]{1,0:T(8,128)(2,1)}, bf16[512,640]{1,0:T(8,128)(2,1)}, u32[]{:S(2)}, u32[]{:S(2)}) collective-permute-start(bf16[512,640]{1,0:T(8,128)(2,1)} %copy-done.26), channel_id=1, source_target_pairs={{0,1},{1,2},{2,3},{4,5},{5,6},{6,7},{8,9},{9,10},{10,11},{12,13},{... | collective-permute-start | bytes 1966088 | tf_op jit(solution)/shard_map/ppermute | solution.py:653
  54.4 18.4 %copy-start.17 = (bf16[512,2048]{1,0:T(8,128)(2,1)S(1)}, bf16[512,2048]{1,0:T(8,128)(2,1)}, u32[]{:S(2)}) copy-start(bf16[512,2048]{1,0:T(8,128)(2,1)} %cotangent_ref.1) | copy-start | bytes 6291460
  68.5 31.7 %collective-permute-start.5 = (bf16[512,640]{1,0:T(8,128)(2,1)S(1)}, bf16[512,640]{1,0:T(8,128)(2,1)S(1)}, u32[]{:S(2)}, u32[]{:S(2)}) collective-permute-start(bf16[512,640]{1,0:T(8,128)(2,1)S(1)} %get-tuple-element.254), channel_id=1, source_target_pairs={{1,3},{2,0},{5,7},{6,4},{9,11},{10,8},{13,15},{14,12},{17,19},{18,... | collective-permute-start | bytes 1966088 | tf_op jit(solution)/shard_map/ppermute | solution.py:664
  69.8 32.0 %collective-permute-start.3 = (bf16[512,640]{1,0:T(8,128)(2,1)S(1)}, bf16[512,640]{1,0:T(8,128)(2,1)}, u32[]{:S(2)}, u32[]{:S(2)}) collective-permute-start(bf16[512,640]{1,0:T(8,128)(2,1)S(1)} %get-tuple-element.254), channel_id=1, source_target_pairs={{1,2},{2,1},{5,6},{6,5},{9,10},{10,9},{13,14},{14,13},{17,18},{18,... | collective-permute-start | bytes 1966088 | tf_op jit(solution)/shard_map/ppermute | solution.py:662
  71.3 28.8 %collective-permute-start.4 = (bf16[512,640]{1,0:T(8,128)(2,1)S(1)}, bf16[512,640]{1,0:T(8,128)(2,1)S(1)}, u32[]{:S(2)}, u32[]{:S(2)}) collective-permute-start(bf16[512,640]{1,0:T(8,128)(2,1)S(1)} %get-tuple-element.253), channel_id=1, source_target_pairs={{1,0},{2,3},{5,4},{6,7},{9,8},{10,11},{13,12},{14,15},{17,16},{18,... | collective-permute-start | bytes 1966088 | tf_op jit(solution)/shard_map/ppermute | solution.py:663
  127.8 19.4 %slice-start.2 = ((s8[6291456]{0:T(1024)(128)(4,1)}), s8[4194304]{0:T(1024)(128)(4,1)S(1)}, s32[]{:S(2)}) async-start(s8[6291456]{0:T(1024)(128)(4,1)} %bitcast.45), calls=%async_computation.8 | async-start | bytes 8388608
  153.3 27.9 %collective-permute-start.7 = (bf16[128,2048]{1,0:T(8,128)(2,1)}, bf16[128,2048]{1,0:T(8,128)(2,1)}, u32[]{:S(2)}, u32[]{:S(2)}) collective-permute-start(bf16[128,2048]{1,0:T(8,128)(2,1)} %get-tuple-element.252), channel_id=1, source_target_pairs={{3,2},{2,1},{7,6},{6,5},{11,10},{10,9},{15,14},{14,13},{19,18},{18... | collective-permute-start | bytes 1572872 | tf_op jit(solution)/shard_map/ppermute | solution.py:591
  154.8 26.4 %collective-permute-start.6 = (bf16[128,2048]{1,0:T(8,128)(2,1)}, bf16[128,2048]{1,0:T(8,128)(2,1)}, u32[]{:S(2)}, u32[]{:S(2)}) collective-permute-start(bf16[128,2048]{1,0:T(8,128)(2,1)} %get-tuple-element.252), channel_id=1, source_target_pairs={{0,1},{1,2},{4,5},{5,6},{8,9},{9,10},{12,13},{13,14},{16,17},{17,1... | collective-permute-start | bytes 1572872 | tf_op jit(solution)/shard_map/ppermute | solution.py:590
  158.8 22.4 %collective-permute-start.8 = (bf16[128,2048]{1,0:T(8,128)(2,1)}, bf16[128,2048]{1,0:T(8,128)(2,1)}, u32[]{:S(2)}, u32[]{:S(2)}) collective-permute-start(bf16[128,2048]{1,0:T(8,128)(2,1)} %get-tuple-element.251), channel_id=1, source_target_pairs={{0,2},{3,1},{4,6},{7,5},{8,10},{11,9},{12,14},{15,13},{16,18},{19,... | collective-permute-start | bytes 1572872 | tf_op jit(solution)/shard_map/ppermute | solution.py:592
  181.2 211.6 %reduce-scatter.5.cloned.1.call-start = ((), (), s32[]{:S(2)}) async-start(), calls=%async_computation.3 | async-start | bytes 9437184 | tf_op jit(solution)/shard_map/reduce_scatter | solution.py:936
  183.9 15.0 %collective-permute-start.9 = (bf16[128,2048]{1,0:T(8,128)(2,1)}, bf16[128,2048]{1,0:T(8,128)(2,1)S(1)}, u32[]{:S(2)}, u32[]{:S(2)}) collective-permute-start(bf16[128,2048]{1,0:T(8,128)(2,1)} %get-tuple-element.135), channel_id=1, source_target_pairs={{0,1},{1,2},{2,3},{4,5},{5,6},{6,7},{8,9},{9,10},{10,11},{12,13},{... | collective-permute-start | bytes 1572872 | tf_op jit(solution)/shard_map/ppermute | solution.py:649
  188.2 15.3 %collective-permute-start.10 = (bf16[128,2048]{1,0:T(8,128)(2,1)}, bf16[128,2048]{1,0:T(8,128)(2,1)S(1)}, u32[]{:S(2)}, u32[]{:S(2)}) collective-permute-start(bf16[128,2048]{1,0:T(8,128)(2,1)} %get-tuple-element.136), channel_id=1, source_target_pairs={{1,0},{2,1},{3,2},{5,4},{6,5},{7,6},{9,8},{10,9},{11,10},{13,12},{... | collective-permute-start | bytes 1572872 | tf_op jit(solution)/shard_map/ppermute | solution.py:649
  198.3 83.3 %copy-start.33 = (bf16[512,2048]{1,0:T(8,128)(2,1)}, bf16[512,2048]{1,0:T(8,128)(2,1)S(1)}, u32[]{:S(2)}) copy-start(bf16[512,2048]{1,0:T(8,128)(2,1)S(1)} %convolution_convert_fusion) | copy-start | bytes 6291460
  204.6 22.6 %copy-start.23 = (f32[128,2048]{1,0:T(8,128)}, f32[128,2048]{1,0:T(8,128)S(1)}, u32[]{:S(2)}) copy-start(f32[128,2048]{1,0:T(8,128)S(1)} %get-tuple-element.182.d_resid_ref) | copy-start | bytes 3145732
  204.6 13.4 %collective-permute-start.12 = (bf16[128,2048]{1,0:T(8,128)(2,1)S(1)}, bf16[128,2048]{1,0:T(8,128)(2,1)S(1)}, u32[]{:S(2)}, u32[]{:S(2)}) collective-permute-start(bf16[128,2048]{1,0:T(8,128)(2,1)S(1)} %get-tuple-element.139.own_ref), channel_id=1, source_target_pairs={{1,0},{2,1},{3,2},{5,4},{6,5},{7,6},{9,8},{10,9},{11,10},{13,12},{... | collective-permute-start | bytes 1572872 | tf_op jit(solution)/shard_map/ppermute | solution.py:653
  205.9 13.3 %collective-permute-start.11 = (bf16[128,2048]{1,0:T(8,128)(2,1)S(1)}, bf16[128,2048]{1,0:T(8,128)(2,1)S(1)}, u32[]{:S(2)}, u32[]{:S(2)}) collective-permute-start(bf16[128,2048]{1,0:T(8,128)(2,1)S(1)} %get-tuple-element.139.own_ref), channel_id=1, source_target_pairs={{0,1},{1,2},{2,3},{4,5},{5,6},{6,7},{8,9},{9,10},{10,11},{12,13},{... | collective-permute-start | bytes 1572872 | tf_op jit(solution)/shard_map/ppermute | solution.py:653
  219.3 30.0 %collective-permute-start.16 = (bf16[320,2048]{1,0:T(8,128)(2,1)S(1)}, bf16[320,2048]{1,0:T(8,128)(2,1)S(1)}, u32[]{:S(2)}, u32[]{:S(2)}) collective-permute-start(bf16[320,2048]{1,0:T(8,128)(2,1)S(1)} %slice.17), channel_id=1, source_target_pairs={{0,1},{3,2},{4,5},{7,6},{8,9},{11,10},{12,13},{15,14},{16,17},{19,... | collective-permute-start | bytes 3932168 | tf_op jit(solution)/shard_map/ppermute | solution.py:670
  223.9 23.1 %collective-permute-start.14 = (bf16[128,2048]{1,0:T(8,128)(2,1)S(1)}, bf16[128,2048]{1,0:T(8,128)(2,1)S(1)}, u32[]{:S(2)}, u32[]{:S(2)}) collective-permute-start(bf16[128,2048]{1,0:T(8,128)(2,1)S(1)} %get-tuple-element.257), channel_id=1, source_target_pairs={{1,0},{2,3},{5,4},{6,7},{9,8},{10,11},{13,12},{14,15},{17,16},{18,... | collective-permute-start | bytes 1572872 | tf_op jit(solution)/shard_map/ppermute | solution.py:663
  225.2 21.8 %collective-permute-start.15 = (bf16[128,2048]{1,0:T(8,128)(2,1)S(1)}, bf16[128,2048]{1,0:T(8,128)(2,1)S(1)}, u32[]{:S(2)}, u32[]{:S(2)}) collective-permute-start(bf16[128,2048]{1,0:T(8,128)(2,1)S(1)} %get-tuple-element.258), channel_id=1, source_target_pairs={{1,3},{2,0},{5,7},{6,4},{9,11},{10,8},{13,15},{14,12},{17,19},{18,... | collective-permute-start | bytes 1572872 | tf_op jit(solution)/shard_map/ppermute | solution.py:664
  226.5 20.5 %collective-permute-start.13 = (bf16[128,2048]{1,0:T(8,128)(2,1)S(1)}, bf16[128,2048]{1,0:T(8,128)(2,1)S(1)}, u32[]{:S(2)}, u32[]{:S(2)}) collective-permute-start(bf16[128,2048]{1,0:T(8,128)(2,1)S(1)} %get-tuple-element.258), channel_id=1, source_target_pairs={{1,2},{2,1},{5,6},{6,5},{9,10},{10,9},{13,14},{14,13},{17,18},{18,... | collective-permute-start | bytes 1572872 | tf_op jit(solution)/shard_map/ppermute | solution.py:662
  227.2 45.4 %copy-start.36 = (bf16[192,2048]{1,0:T(8,128)(2,1)}, bf16[192,2048]{1,0:T(8,128)(2,1)S(1)}, u32[]{:S(2)}) copy-start(bf16[192,2048]{1,0:T(8,128)(2,1)S(1)} %slice.16) | copy-start | bytes 2359300
  227.2 20.1 %copy-start.43 = (bf16[640,2048]{1,0:T(8,128)(2,1)S(1)}, bf16[640,2048]{1,0:T(8,128)(2,1)}, u32[]{:S(2)}) copy-start(bf16[640,2048]{1,0:T(8,128)(2,1)} %param.22) | copy-start | bytes 7864324
  249.9 31.6 %collective-permute-start.18 = (bf16[320,2048]{1,0:T(8,128)(2,1)S(1)}, bf16[320,2048]{1,0:T(8,128)(2,1)S(1)}, u32[]{:S(2)}, u32[]{:S(2)}) collective-permute-start(bf16[320,2048]{1,0:T(8,128)(2,1)S(1)} %fusion.11), channel_id=1, source_target_pairs={{1,2},{2,1},{5,6},{6,5},{9,10},{10,9},{13,14},{14,13},{17,18},{18,... | collective-permute-start | bytes 3932168 | tf_op jit(solution)/shard_map/ppermute | solution.py:670
  250.7 21.9 %collective-permute-start.17 = (bf16[192,2048]{1,0:T(8,128)(2,1)S(1)}, bf16[192,2048]{1,0:T(8,128)(2,1)S(1)}, u32[]{:S(2)}, u32[]{:S(2)}) collective-permute-start(bf16[192,2048]{1,0:T(8,128)(2,1)S(1)} %slice.16), channel_id=1, source_target_pairs={{0,1},{3,2},{4,5},{7,6},{8,9},{11,10},{12,13},{15,14},{16,17},{19,... | collective-permute-start | bytes 2359304 | tf_op jit(solution)/shard_map/ppermute | solution.py:670
  263.5 21.0 %copy-start.27 = (bf16[512,640]{1,0:T(8,128)(2,1)}, bf16[512,640]{1,0:T(8,128)(2,1)S(1)}, u32[]{:S(2)}) copy-start(bf16[512,640]{1,0:T(8,128)(2,1)S(1)} %get-tuple-element.148.refs_3_) | copy-start | bytes 1966084
  273.8 45.0 %collective-permute-start.24 = (bf16[192,2048]{1,0:T(8,128)(2,1)}, bf16[192,2048]{1,0:T(8,128)(2,1)}, u32[]{:S(2)}, u32[]{:S(2)}) collective-permute-start(bf16[192,2048]{1,0:T(8,128)(2,1)} %fusion.13), channel_id=1, source_target_pairs={{1,2},{2,1},{5,6},{6,5},{9,10},{10,9},{13,14},{14,13},{17,18},{18,... | collective-permute-start | bytes 2359304 | tf_op jit(solution)/shard_map/ppermute | solution.py:670
  283.1 4.6 %collective-permute-start.19 = (f32[8,640]{1,0:T(8,128)S(1)}, f32[8,640]{1,0:T(8,128)S(1)}, u32[]{:S(2)}, u32[]{:S(2)}) collective-permute-start(f32[8,640]{1,0:T(8,128)S(1)} %get-tuple-element.164), channel_id=1, source_target_pairs={{4,0},{8,4},{12,8},{16,12},{20,16},{24,20},{28,24},{5,1},{9,5},{13... | collective-permute-start | bytes 61448 | tf_op jit(solution)/shard_map/ppermute | solution.py:918
  286.4 34.2 %collective-permute-start.23 = (bf16[320,2048]{1,0:T(8,128)(2,1)}, bf16[320,2048]{1,0:T(8,128)(2,1)}, u32[]{:S(2)}, u32[]{:S(2)}) collective-permute-start(bf16[320,2048]{1,0:T(8,128)(2,1)} %fusion.12), channel_id=1, source_target_pairs={{2,3},{1,0},{6,7},{5,4},{10,11},{9,8},{14,15},{13,12},{18,19},{17,... | collective-permute-start | bytes 3932168 | tf_op jit(solution)/shard_map/ppermute | solution.py:670
  290.7 28.1 %collective-permute-start.22 = (bf16[128,2048]{1,0:T(8,128)(2,1)}, bf16[128,2048]{1,0:T(8,128)(2,1)}, u32[]{:S(2)}, u32[]{:S(2)}) collective-permute-start(bf16[128,2048]{1,0:T(8,128)(2,1)} %get-tuple-element.249), channel_id=1, source_target_pairs={{0,2},{3,1},{4,6},{7,5},{8,10},{11,9},{12,14},{15,13},{16,18},{19,... | collective-permute-start | bytes 1572872 | tf_op jit(solution)/shard_map/ppermute | solution.py:592
  297.6 21.3 %collective-permute-start.21 = (bf16[128,2048]{1,0:T(8,128)(2,1)}, bf16[128,2048]{1,0:T(8,128)(2,1)}, u32[]{:S(2)}, u32[]{:S(2)}) collective-permute-start(bf16[128,2048]{1,0:T(8,128)(2,1)} %get-tuple-element.250), channel_id=1, source_target_pairs={{3,2},{2,1},{7,6},{6,5},{11,10},{10,9},{15,14},{14,13},{19,18},{18... | collective-permute-start | bytes 1572872 | tf_op jit(solution)/shard_map/ppermute | solution.py:591
  299.0 21.5 %collective-permute-start.20 = (bf16[128,2048]{1,0:T(8,128)(2,1)}, bf16[128,2048]{1,0:T(8,128)(2,1)}, u32[]{:S(2)}, u32[]{:S(2)}) collective-permute-start(bf16[128,2048]{1,0:T(8,128)(2,1)} %get-tuple-element.250), channel_id=1, source_target_pairs={{0,1},{1,2},{4,5},{5,6},{8,9},{9,10},{12,13},{13,14},{16,17},{17,1... | collective-permute-start | bytes 1572872 | tf_op jit(solution)/shard_map/ppermute | solution.py:590
  323.2 16.5 %collective-permute-start.25 = (bf16[128,2048]{1,0:T(8,128)(2,1)}, bf16[128,2048]{1,0:T(8,128)(2,1)S(1)}, u32[]{:S(2)}, u32[]{:S(2)}) collective-permute-start(bf16[128,2048]{1,0:T(8,128)(2,1)} %get-tuple-element.180), channel_id=1, source_target_pairs={{0,1},{1,2},{2,3},{4,5},{5,6},{6,7},{8,9},{9,10},{10,11},{12,13},{... | collective-permute-start | bytes 1572872 | tf_op jit(solution)/shard_map/ppermute | solution.py:649
  328.0 17.0 %collective-permute-start.26 = (bf16[128,2048]{1,0:T(8,128)(2,1)}, bf16[128,2048]{1,0:T(8,128)(2,1)}, u32[]{:S(2)}, u32[]{:S(2)}) collective-permute-start(bf16[128,2048]{1,0:T(8,128)(2,1)} %get-tuple-element.181), channel_id=1, source_target_pairs={{1,0},{2,1},{3,2},{5,4},{6,5},{7,6},{9,8},{10,9},{11,10},{13,12},{... | collective-permute-start | bytes 1572872 | tf_op jit(solution)/shard_map/ppermute | solution.py:649
  332.2 30.3 %collective-permute-start.29 = (bf16[192,2048]{1,0:T(8,128)(2,1)}, bf16[192,2048]{1,0:T(8,128)(2,1)}, u32[]{:S(2)}, u32[]{:S(2)}) collective-permute-start(bf16[192,2048]{1,0:T(8,128)(2,1)} %fusion.14), channel_id=1, source_target_pairs={{2,3},{1,0},{6,7},{5,4},{10,11},{9,8},{14,15},{13,12},{18,19},{17,... | collective-permute-start | bytes 2359304 | tf_op jit(solution)/shard_map/ppermute | solution.py:670
  349.0 23.8 %collective-permute-start.28 = (bf16[128,2048]{1,0:T(8,128)(2,1)}, bf16[128,2048]{1,0:T(8,128)(2,1)S(1)}, u32[]{:S(2)}, u32[]{:S(2)}) collective-permute-start(bf16[128,2048]{1,0:T(8,128)(2,1)} %get-tuple-element.183), channel_id=1, source_target_pairs={{1,0},{2,1},{3,2},{5,4},{6,5},{7,6},{9,8},{10,9},{11,10},{13,12},{... | collective-permute-start | bytes 1572872 | tf_op jit(solution)/shard_map/ppermute | solution.py:653
  350.4 22.4 %collective-permute-start.27 = (bf16[128,2048]{1,0:T(8,128)(2,1)}, bf16[128,2048]{1,0:T(8,128)(2,1)S(1)}, u32[]{:S(2)}, u32[]{:S(2)}) collective-permute-start(bf16[128,2048]{1,0:T(8,128)(2,1)} %get-tuple-element.183), channel_id=1, source_target_pairs={{0,1},{1,2},{2,3},{4,5},{5,6},{6,7},{8,9},{9,10},{10,11},{12,13},{... | collective-permute-start | bytes 1572872 | tf_op jit(solution)/shard_map/ppermute | solution.py:653
  360.2 17.1 %collective-permute-start.34 = (f32[2,2048]{1,0:T(2,128)S(1)}, f32[2,2048]{1,0:T(2,128)S(1)}, u32[]{:S(2)}, u32[]{:S(2)}) collective-permute-start(f32[2,2048]{1,0:T(2,128)S(1)} %pad_maximum_fusion), channel_id=1, source_target_pairs={{0,2},{1,3},{2,0},{3,1},{4,6},{5,7},{6,4},{7,5},{8,10},{9,11},{10,... | collective-permute-start | bytes 49160 | tf_op jit(solution)/shard_map/ppermute | solution.py:561
  360.3 18.3 %collective-permute-start.35 = (f32[2,2048]{1,0:T(2,128)S(1)}, f32[2,2048]{1,0:T(2,128)S(1)}, u32[]{:S(2)}, u32[]{:S(2)}) collective-permute-start(f32[2,2048]{1,0:T(2,128)S(1)} %pad_maximum_fusion), channel_id=1, source_target_pairs={{0,3},{1,0},{2,1},{3,2},{4,7},{5,4},{6,5},{7,6},{8,11},{9,8},{10,9... | collective-permute-start | bytes 49160 | tf_op jit(solution)/shard_map/ppermute | solution.py:561
  362.5 16.2 %collective-permute-start.33 = (f32[2,2048]{1,0:T(2,128)S(1)}, f32[2,2048]{1,0:T(2,128)S(1)}, u32[]{:S(2)}, u32[]{:S(2)}) collective-permute-start(f32[2,2048]{1,0:T(2,128)S(1)} %pad_maximum_fusion), channel_id=1, source_target_pairs={{0,1},{1,2},{2,3},{3,0},{4,5},{5,6},{6,7},{7,4},{8,9},{9,10},{10,1... | collective-permute-start | bytes 49160 | tf_op jit(solution)/shard_map/ppermute | solution.py:561
  374.6 26.9 %collective-permute-start.32 = (bf16[128,2048]{1,0:T(8,128)(2,1)}, bf16[128,2048]{1,0:T(8,128)(2,1)}, u32[]{:S(2)}, u32[]{:S(2)}) collective-permute-start(bf16[128,2048]{1,0:T(8,128)(2,1)} %get-tuple-element.256), channel_id=1, source_target_pairs={{1,3},{2,0},{5,7},{6,4},{9,11},{10,8},{13,15},{14,12},{17,19},{18,... | collective-permute-start | bytes 1572872 | tf_op jit(solution)/shard_map/ppermute | solution.py:664
  375.9 25.7 %collective-permute-start.30 = (bf16[128,2048]{1,0:T(8,128)(2,1)}, bf16[128,2048]{1,0:T(8,128)(2,1)}, u32[]{:S(2)}, u32[]{:S(2)}) collective-permute-start(bf16[128,2048]{1,0:T(8,128)(2,1)} %get-tuple-element.256), channel_id=1, source_target_pairs={{1,2},{2,1},{5,6},{6,5},{9,10},{10,9},{13,14},{14,13},{17,18},{18,... | collective-permute-start | bytes 1572872 | tf_op jit(solution)/shard_map/ppermute | solution.py:662
  377.4 24.2 %collective-permute-start.31 = (bf16[128,2048]{1,0:T(8,128)(2,1)}, bf16[128,2048]{1,0:T(8,128)(2,1)}, u32[]{:S(2)}, u32[]{:S(2)}) collective-permute-start(bf16[128,2048]{1,0:T(8,128)(2,1)} %get-tuple-element.255), channel_id=1, source_target_pairs={{1,0},{2,3},{5,4},{6,7},{9,8},{10,11},{13,12},{14,15},{17,16},{18,... | collective-permute-start | bytes 1572872 | tf_op jit(solution)/shard_map/ppermute | solution.py:663
  (50 other events, 299.9 us)
Sparse Core Ops, SparseCore 0:
  12.4 35.1 all-gather.10
  49.5 62.3 all-gather.12
  181.4 127.1 reduce-scatter.2
  320.7 72.1 reduce-scatter.4

commit v5 on v4

--- a/solution.py
+++ b/solution.py
@@ -25,7 +25,7 @@
         + [pl.BlockSpec(memory_space=pltpu.SMEM)] * scalars,
         out_specs=[pl.BlockSpec(memory_space=pltpu.VMEM)] * len(out_shape),
         scratch_shapes=scratch,
-        compiler_params=pltpu.CompilerParams(vmem_limit_bytes=26 << 20),
+        compiler_params=pltpu.CompilerParams(vmem_limit_bytes=32 << 20),
         cost_estimate=pl.CostEstimate(flops=1000, bytes_accessed=1000, transcendentals=0),
     )(*operands)
 

time: 424 us -> 424 us (level)
  no operation moved by 1% of the time
where the time goes in v5:
time: 424 us; the launch traced here: 416 us
  waiting for transfers between devices  110 us (26%)
  Pallas kernels  86.6 us (20%)
  starting transfers between devices  84.3 us (20%)
  matrix products  49.4 us (12%)
  blocking collectives  29.6 us (7%)
  local copies, waits for them, and re-layouts  23.8 us (6%)
  other arithmetic  17.1 us (4%)
  between operations  15.3 us (4%)
    ppermute x3, waiting for transfers between devices, gather_second(): lax.ppermute(back, 'head', [(1, 0), (2, 3)])  44.7 us
    pallas_call x2, Pallas kernels, weight_grads(): pl.pallas_call(body, grid=(width // block,), in_specs=[pl.BlockSpec((toke...  28.3 us
    pallas_call x8, Pallas kernels, call(): pl.pallas_call(body, out_shape=out_shape, in_specs=[pl.BlockSpec(memory_s...  28 us
    ppermute x3, waiting for transfers between devices, gather_first(): lax.ppermute(own, 'head', line_pairs(-1))  25.9 us
    unnamed x118, local copies, waits for them, and re-layouts  18.1 us
    ppermute x6, starting transfers between devices, line_turn(): lax.ppermute(sent, 'head', [(turn - 1, turn), (peers - turn, peers - turn...  16.7 us
    pallas_call x1, Pallas kernels, residual_norm(): pl.pallas_call(add_projection, grid=(blocks,), in_specs=[whole(tokens, ch...  15.9 us
    ppermute x3, starting transfers between devices, gather_first(): lax.ppermute(own, 'head', line_pairs(1))  14.6 us
  transfers between devices with their start and end apart: 40, of which 17 were waited for; matrix products, arithmetic and copies ran while one was open for 11% of the time, Pallas kernels for 16%

profile of v5, /device:TPU:0, one launch (start us, length us, event | category | flops | bytes accessed | tf_op | source)
XLA Modules:
  0.0 416.0 jit_solution(6713125755417321861)
XLA Ops:
  8.2 2.3 collective-permute-start
  12.3 2.2 fusion
  21.0 7.5 %shard_map.245 = (bf16[512,640]{1,0:T(8,128)(2,1)S(1)}, f32[512,640]{1,0:T(8,128)S(1)}, f32[512,640]{1,0:T(8,128)S(1)}, f32[5,512,128]{2,1,0:T(8,128)S(1)}, f32[...) custom-call(bf16[512,640]{1,0:T(8,128)(2,1)S(1)} %convolution_convert_fusi, ...), custom_call_target="tpu_custom_call" | custom-call | flops 1000 | bytes 1000 | tf_op jit(solution)/shard_map/pallas_call | solution.py:21
  31.9 10.2 %all-gather.5.ends_ref = f32[8,2,640]{2,1,0:T(2,128)S(1)} all-gather(f32[1,2,640]{2,1,0:T(2,128)S(1)} %bitcast.37), channel_id=2, replica_groups=mesh['seq'=8,'head'=4] {'seq'}, dimensions={0}, use_global_device_ids=true | all-gather | bytes 46080 | tf_op jit(solution)/shard_map/all_gather | solution.py:792
  44.8 2.8 all-gather.11.cloned.1.call-done
  49.0 5.4 %collective-permute-start.1 = (bf16[512,640]{1,0:T(8,128)(2,1)}, bf16[512,640]{1,0:T(8,128)(2,1)}, u32[]{:S(2)}, u32[]{:S(2)}) collective-permute-start(bf16[512,640]{1,0:T(8,128)(2,1)} %copy-done.26), channel_id=1, source_target_pairs={{0,1},{1,2},{2,3},{4,5},{5,6},{6,7},{8,9},{9,10},{10,11},{12,13},{... | collective-permute-start | bytes 1966088 | tf_op jit(solution)/shard_map/ppermute | solution.py:653
  54.4 11.4 %collective-permute-done.2.right_ref = bf16[512,640]{1,0:T(8,128)(2,1)} collective-permute-done((bf16[512,640]{1,0:T(8,128)(2,1)}, bf16[512,640]{1,0:T(8,128)(2,1)}, u32[]{:S(2)}, u32[]{:S(2)}) %collective-permute-start.2) | collective-permute-done | bytes 655392 | tf_op jit(solution)/shard_map/ppermute | solution.py:653
  72.7 8.3 %fusion.23 = f32[512,1536]{1,0:T(8,128)} fusion(bf16[512,2048]{1,0:T(8,128)(2,1)S(1)} %copy-done.17, bf16[1536,2048]{1,0:T(8,128)(2,1)} %param.26), kind=kOutput, calls=%fused_computation.60 | convolution fusion | flops 3221225472 | bytes 11534336 | tf_op jit(solution)/shard_map/td,fd->tf/dot_general | solution.py:812
  81.1 19.0 %collective-permute-done.4.back_ref = bf16[512,640]{1,0:T(8,128)(2,1)S(1)} collective-permute-done((bf16[512,640]{1,0:T(8,128)(2,1)S(1)}, bf16[512,640]{1,0:T(8,128)(2,1)S(1)}, u32[]{:S(2)}, u32[]{:S(2)}) %collective-permute-start.4) | collective-permute-done | bytes 655392 | tf_op jit(solution)/shard_map/ppermute | solution.py:663
  101.7 10.2 %all-gather.13.cloned.1.call-done = bf16[20480,256]{1,0:T(8,128)(2,1)} async-done(((bf16[2560,256]{1,0:T(8,128)(2,1)}), bf16[20480,256]{1,0:T(8,128)(2,1)}) %all-gather.13.cloned.1.call-update) | async-done | bytes 10485776 | tf_op jit(solution)/shard_map/all_gather | solution.py:807
  111.9 15.9 %shard_map.247 = (f32[512,2048]{1,0:T(8,128)}, bf16[512,2048]{1,0:T(8,128)(2,1)}) custom-call(bf16[512,640]{1,0:T(8,128)(2,1)} %copy-done.26, bf16[512,640]{1,0:T(8,128)(2,1)} %collective-permute-done.1.left_ref, bf16[512,640]{1,0:T(8,128)(2,1)} %collective-permute-done.2.right_ref, bf16[512,640]{1,0:T(8,128)(2,1)} %collective-permute-done.3.over_ref, ...), custom_call_target="tpu_custom_call" | custom-call | flops 5368709120 | bytes 20971520 | tf_op jit(solution)/shard_map/pallas_call | solution.py:338
  127.8 6.8 %fusion.24 = f32[512,1536]{1,0:T(8,128)S(1)} fusion(bf16[512,2048]{1,0:T(8,128)(2,1)} %get-tuple-element.126.refs_0_.refs_1_, bf16[2048,1536]{1,0:T(8,128)(2,1)} %param.24), kind=kOutput, calls=%fused_computation.61 | convolution fusion | flops 3221225472 | bytes 11534336 | tf_op jit(solution)/shard_map/dot_general | solution.py:822
  134.7 9.1 %multiply_convert_fusion = (bf16[512,1536]{1,0:T(8,128)(2,1)}, bf16[512,1536]{1,0:T(8,128)(2,1)S(1)}, bf16[512,1536]{1,0:T(8,128)(2,1)S(1)}) fusion(f32[512,1536]{1,0:T(8,128)S(1)} %fusion.24, f32[512,1536]{1,0:T(8,128)S(1)} %copy-done.53, bf16[512,2048]{1,0:T(8,128)(2,1)S(1)} %copy-done.50, bf16[2048,1536]{1,0:T(8,128)(2,1)} %param.25), kind=kOutput, calls=%fused_computation.19 | convolution fusion | flops 3240886272 | bytes 19398656 | tf_op jit(solution)/shard_map/dot_general | solution.py:823
  143.8 3.4 fusion.25
  147.3 3.7 add_convert_fusion.1.right_ref.left_ref.own_ref
  154.8 4.0 collective-permute-start.6
  158.8 3.6 collective-permute-start.8
  162.4 16.6 %shard_map.248 = bf16[2048,4608]{1,0:T(8,128)(2,1)} custom-call(bf16[512,2048]{1,0:T(8,128)(2,1)} %get-tuple-element.126.refs_0_.refs_1_, bf16[512,2048]{1,0:T(8,128)(2,1)} %get-tuple-element.126.refs_0_.refs_1_, bf16[512,2048]{1,0:T(8,128)(2,1)} %cotangent_ref.1, bf16[512,1536]{1,0:T(8,128)(2,1)} %copy-done.51, bf16[512,1536]{1,0:T(8,128)(2,1)} %copy-done.52, ...), custom_call_target="tpu_custom_call" | custom-call | flops 9663676416 | bytes 18874368 | tf_op jit(solution)/shard_map/pallas_call | solution.py:417
  179.0 2.2 collective-permute-done.8.far_ref
  181.3 2.6 shard_map.249
  183.9 4.2 %collective-permute-start.9 = (bf16[128,2048]{1,0:T(8,128)(2,1)}, bf16[128,2048]{1,0:T(8,128)(2,1)S(1)}, u32[]{:S(2)}, u32[]{:S(2)}) collective-permute-start(bf16[128,2048]{1,0:T(8,128)(2,1)} %get-tuple-element.135), channel_id=1, source_target_pairs={{0,1},{1,2},{2,3},{4,5},{5,6},{6,7},{8,9},{9,10},{10,11},{12,13},{... | collective-permute-start | bytes 1572872 | tf_op jit(solution)/shard_map/ppermute | solution.py:649
  189.8 8.5 %convolution_convert_fusion = bf16[512,2048]{1,0:T(8,128)(2,1)S(1)} fusion(bf16[512,1536]{1,0:T(8,128)(2,1)} %get-tuple-element.131.refs_5_, bf16[1536,2048]{1,0:T(8,128)(2,1)} %param.26), kind=kOutput, calls=%fused_computation.23 | convolution fusion | flops 3222274048 | bytes 9961472 | tf_op jit(solution)/shard_map/dot_general | solution.py:838
  199.0 4.6 %collective-permute-done.10.left_ref = bf16[128,2048]{1,0:T(8,128)(2,1)S(1)} collective-permute-done((bf16[128,2048]{1,0:T(8,128)(2,1)}, bf16[128,2048]{1,0:T(8,128)(2,1)S(1)}, u32[]{:S(2)}, u32[]{:S(2)}) %collective-permute-start.10) | collective-permute-done | bytes 524320 | tf_op jit(solution)/shard_map/ppermute | solution.py:649
  205.9 4.6 %collective-permute-start.11 = (bf16[128,2048]{1,0:T(8,128)(2,1)S(1)}, bf16[128,2048]{1,0:T(8,128)(2,1)S(1)}, u32[]{:S(2)}, u32[]{:S(2)}) collective-permute-start(bf16[128,2048]{1,0:T(8,128)(2,1)S(1)} %get-tuple-element.139.own_ref), channel_id=1, source_target_pairs={{0,1},{1,2},{2,3},{4,5},{5,6},{6,7},{8,9},{9,10},{10,11},{12,13},{... | collective-permute-start | bytes 1572872 | tf_op jit(solution)/shard_map/ppermute | solution.py:653
  210.5 7.5 %collective-permute-done.12.right_ref = bf16[128,2048]{1,0:T(8,128)(2,1)S(1)} collective-permute-done((bf16[128,2048]{1,0:T(8,128)(2,1)S(1)}, bf16[128,2048]{1,0:T(8,128)(2,1)S(1)}, u32[]{:S(2)}, u32[]{:S(2)}) %collective-permute-start.12) | collective-permute-done | bytes 524320 | tf_op jit(solution)/shard_map/ppermute | solution.py:653
  219.3 4.5 %collective-permute-start.16 = (bf16[320,2048]{1,0:T(8,128)(2,1)S(1)}, bf16[320,2048]{1,0:T(8,128)(2,1)S(1)}, u32[]{:S(2)}, u32[]{:S(2)}) collective-permute-start(bf16[320,2048]{1,0:T(8,128)(2,1)S(1)} %slice.17), channel_id=1, source_target_pairs={{0,1},{3,2},{4,5},{7,6},{8,9},{11,10},{12,13},{15,14},{16,17},{19,... | collective-permute-start | bytes 3932168 | tf_op jit(solution)/shard_map/ppermute | solution.py:670
  227.3 19.7 %collective-permute-done.14.back_ref = bf16[128,2048]{1,0:T(8,128)(2,1)S(1)} collective-permute-done((bf16[128,2048]{1,0:T(8,128)(2,1)S(1)}, bf16[128,2048]{1,0:T(8,128)(2,1)S(1)}, u32[]{:S(2)}, u32[]{:S(2)}) %collective-permute-start.14) | collective-permute-done | bytes 524320 | tf_op jit(solution)/shard_map/ppermute | solution.py:663
  250.7 7.1 %collective-permute-start.17 = (bf16[192,2048]{1,0:T(8,128)(2,1)S(1)}, bf16[192,2048]{1,0:T(8,128)(2,1)S(1)}, u32[]{:S(2)}, u32[]{:S(2)}) collective-permute-start(bf16[192,2048]{1,0:T(8,128)(2,1)S(1)} %slice.16), channel_id=1, source_target_pairs={{0,1},{3,2},{4,5},{7,6},{8,9},{11,10},{12,13},{15,14},{16,17},{19,... | collective-permute-start | bytes 2359304 | tf_op jit(solution)/shard_map/ppermute | solution.py:670
  257.9 5.6 %shard_map.252 = (bf16[512,640]{1,0:T(8,128)(2,1)S(1)}, f32[5,512,128]{2,1,0:T(8,128)S(1)}, f32[5,512,128]{2,1,0:T(8,128)S(1)}, f32[16,640]{1,0:T(8,128)S(1)}, f32[1,640]{1,0:T(1,128)S(1)}) custom-call(f32[512,640]{1,0:T(8,128)S(1)} %fusion.26.d_mixed_ref, f32[512,640]{1,0:T(8,128)S(1)} %copy-done.10, f32[512,640]{1,0:T(8,128)S(1)} %copy-done.8, ...), custom_call_target="tpu_custom_call" | custom-call | flops 1000 | bytes 1000 | tf_op jit(solution)/shard_map/pallas_call | solution.py:21
  263.6 9.2 %all-gather.6.backs_ref = f32[8,1,640]{2,1,0:T(1,128)S(1)} all-gather(f32[1,1,640]{2,1,0:T(1,128)S(1)} %bitcast.38), channel_id=5, replica_groups=mesh['seq'=8,'head'=4] {'seq'}, dimensions={0}, use_global_device_ids=true | all-gather | bytes 23040 | tf_op jit(solution)/shard_map/all_gather | solution.py:878
  275.7 5.9 %shard_map.253 = (bf16[512,1280]{1,0:T(8,128)(2,1)S(1)}, f32[512,640]{1,0:T(8,128)S(1)}, f32[8,640]{1,0:T(8,128)S(1)}, f32[8,640]{1,0:T(8,128)S(1)}, f32[32,640]{1,0:T(8,128)S(1)}) custom-call(f32[5,512,128]{2,1,0:T(8,128)S(1)} %get-tuple-element.149.local_ref, f32[5,512,128]{2,1,0:T(8,128)S(1)} %get-tuple-element.150.prod_ref, ...), custom_call_target="tpu_custom_call" | custom-call | flops 1000 | bytes 1000 | tf_op jit(solution)/shard_map/pallas_call | solution.py:21
  290.8 6.8 %collective-permute-start.22 = (bf16[128,2048]{1,0:T(8,128)(2,1)}, bf16[128,2048]{1,0:T(8,128)(2,1)}, u32[]{:S(2)}, u32[]{:S(2)}) collective-permute-start(bf16[128,2048]{1,0:T(8,128)(2,1)} %get-tuple-element.249), channel_id=1, source_target_pairs={{0,2},{3,1},{4,6},{7,5},{8,10},{11,9},{12,14},{15,13},{16,18},{19,... | collective-permute-start | bytes 1572872 | tf_op jit(solution)/shard_map/ppermute | solution.py:592
  303.2 11.6 %shard_map.255 = bf16[2048,2048]{1,0:T(8,128)(2,1)} custom-call(bf16[512,2048]{1,0:T(8,128)(2,1)} %copy-done.35, bf16[512,2048]{1,0:T(8,128)(2,1)} %copy-done.35, bf16[512,2048]{1,0:T(8,128)(2,1)} %copy-done.4, bf16[512,640]{1,0:T(8,128)(2,1)} %copy-done.27, bf16[512,640]{1,0:T(8,128)(2,1)} %copy-done.40, bf16[512,640]{1,0:T(8,128)(2,1)} %copy-done.26, ...), custom_call_target="tpu_custom_call" | custom-call | flops 4294967296 | bytes 8388608 | tf_op jit(solution)/shard_map/pallas_call | solution.py:417
  316.5 2.4 shard_map.256
  320.6 2.6 shard_map.257
  323.2 4.8 %collective-permute-start.25 = (bf16[128,2048]{1,0:T(8,128)(2,1)}, bf16[128,2048]{1,0:T(8,128)(2,1)S(1)}, u32[]{:S(2)}, u32[]{:S(2)}) collective-permute-start(bf16[128,2048]{1,0:T(8,128)(2,1)} %get-tuple-element.180), channel_id=1, source_target_pairs={{0,1},{1,2},{2,3},{4,5},{5,6},{6,7},{8,9},{9,10},{10,11},{12,13},{... | collective-permute-start | bytes 1572872 | tf_op jit(solution)/shard_map/ppermute | solution.py:649
  329.4 2.9 fusion.14
  333.5 6.2 %collective-permute-done.25.right_ref = bf16[128,2048]{1,0:T(8,128)(2,1)S(1)} collective-permute-done((bf16[128,2048]{1,0:T(8,128)(2,1)}, bf16[128,2048]{1,0:T(8,128)(2,1)S(1)}, u32[]{:S(2)}, u32[]{:S(2)}) %collective-permute-start.25) | collective-permute-done | bytes 524320 | tf_op jit(solution)/shard_map/ppermute | solution.py:649
  339.8 5.3 %collective-permute-done.26.left_ref = bf16[128,2048]{1,0:T(8,128)(2,1)} collective-permute-done((bf16[128,2048]{1,0:T(8,128)(2,1)}, bf16[128,2048]{1,0:T(8,128)(2,1)}, u32[]{:S(2)}, u32[]{:S(2)}) %collective-permute-start.26) | collective-permute-done | bytes 524320 | tf_op jit(solution)/shard_map/ppermute | solution.py:649
  345.1 3.9 shard_map.258
  350.4 4.6 %collective-permute-start.27 = (bf16[128,2048]{1,0:T(8,128)(2,1)}, bf16[128,2048]{1,0:T(8,128)(2,1)S(1)}, u32[]{:S(2)}, u32[]{:S(2)}) collective-permute-start(bf16[128,2048]{1,0:T(8,128)(2,1)} %get-tuple-element.183), channel_id=1, source_target_pairs={{0,1},{1,2},{2,3},{4,5},{5,6},{6,7},{8,9},{9,10},{10,11},{12,13},{... | collective-permute-start | bytes 1572872 | tf_op jit(solution)/shard_map/ppermute | solution.py:653
  355.0 5.2 %add_add_fusion.base_ref = f32[512,2048]{1,0:T(8,128)S(1)} fusion(f32[512,2048]{1,0:T(8,128)} %get-tuple-element.128.residual_ref, bf16[512,2048]{1,0:T(8,128)(2,1)} %copy-done.33, bf16[192,2048]{1,0:T(8,128)(2,1)} %copy-done.39, bf16[320,2048]{1,0:T(8,128)(2,1)} %copy-done.37, bf16[192,2048]{1,0:T(8,128)(2,1)} %collective-permute-done.24, ...), kind=kLoop, calls=%fused_computation.7 | loop fusion | flops 12582912 | bytes 14680064 | tf_op jit(solution)/shard_map/add | solution.py:947
  362.5 3.3 shard_map.259
  365.8 7.0 %collective-permute-done.28.right_ref = bf16[128,2048]{1,0:T(8,128)(2,1)S(1)} collective-permute-done((bf16[128,2048]{1,0:T(8,128)(2,1)}, bf16[128,2048]{1,0:T(8,128)(2,1)S(1)}, u32[]{:S(2)}, u32[]{:S(2)}) %collective-permute-start.28) | collective-permute-done | bytes 524320 | tf_op jit(solution)/shard_map/ppermute | solution.py:653
  378.7 10.2 %all-gather.7 = f32[8,2,2048]{2,1,0:T(2,128)S(1)} all-gather(f32[1,2,2048]{2,1,0:T(2,128)S(1)} %add_bitcast_fusion), channel_id=6, replica_groups=mesh['seq'=8,'head'=4] {'seq'}, dimensions={0}, use_global_device_ids=true | all-gather | bytes 147456 | tf_op jit(solution)/shard_map/all_gather | solution.py:951
  389.7 3.3 reduce-scatter.5.cloned.1.call-done.in_ref
  395.6 6.0 %collective-permute-done.31.back_ref = bf16[128,2048]{1,0:T(8,128)(2,1)} collective-permute-done((bf16[128,2048]{1,0:T(8,128)(2,1)}, bf16[128,2048]{1,0:T(8,128)(2,1)}, u32[]{:S(2)}, u32[]{:S(2)}) %collective-permute-start.31) | collective-permute-done | bytes 524320 | tf_op jit(solution)/shard_map/ppermute | solution.py:663
  405.2 3.8 shard_map.261
  (215 shorter events, 82.1 us)
Async XLA Ops:
  7.2 40.4 %all-gather.11.cloned.1.call-start = ((), (), s32[]{:S(2)}) async-start(), calls=%async_computation.4 | async-start | bytes 1638400 | tf_op jit(solution)/shard_map/all_gather | solution.py:755
  8.2 11.4 %collective-permute-start = (bf16[8,2048]{1,0:T(8,128)(2,1)S(1)}, bf16[8,2048]{1,0:T(8,128)(2,1)S(1)}, u32[]{:S(2)}, u32[]{:S(2)}) collective-permute-start(bf16[8,2048]{1,0:T(8,128)(2,1)S(1)} %slice.15), channel_id=1, source_target_pairs={{0,4},{4,8},{8,12},{12,16},{16,20},{20,24},{24,28},{1,5},{5,9},{9,... | collective-permute-start | bytes 98312 | tf_op jit(solution)/shard_map/ppermute | solution.py:752
  12.3 99.6 %all-gather.13.cloned.1.call-start = ((), (), s32[]{:S(2)}) async-start(), calls=%async_computation.5 | async-start | bytes 11796480 | tf_op jit(solution)/shard_map/all_gather | solution.py:807
  19.5 22.7 %copy-start.9 = (f32[512,640]{1,0:T(8,128)}, f32[512,640]{1,0:T(8,128)S(1)}, u32[]{:S(2)}) copy-start(f32[512,640]{1,0:T(8,128)S(1)} %fusion.22.gate_ref) | copy-start | bytes 3932164
  47.7 267.1 %reduce-scatter.3.cloned.1.call-start = ((), (), s32[]{:S(2)}) async-start(), calls=%async_computation.2 | async-start | bytes 21233664 | tf_op jit(solution)/shard_map/reduce_scatter | solution.py:836
  47.7 18.2 %collective-permute-start.2 = (bf16[512,640]{1,0:T(8,128)(2,1)}, bf16[512,640]{1,0:T(8,128)(2,1)}, u32[]{:S(2)}, u32[]{:S(2)}) collective-permute-start(bf16[512,640]{1,0:T(8,128)(2,1)} %copy-done.26), channel_id=1, source_target_pairs={{1,0},{2,1},{3,2},{5,4},{6,5},{7,6},{9,8},{10,9},{11,10},{13,12},{... | collective-permute-start | bytes 1966088 | tf_op jit(solution)/shard_map/ppermute | solution.py:653
  49.0 18.0 %collective-permute-start.1 = (bf16[512,640]{1,0:T(8,128)(2,1)}, bf16[512,640]{1,0:T(8,128)(2,1)}, u32[]{:S(2)}, u32[]{:S(2)}) collective-permute-start(bf16[512,640]{1,0:T(8,128)(2,1)} %copy-done.26), channel_id=1, source_target_pairs={{0,1},{1,2},{2,3},{4,5},{5,6},{6,7},{8,9},{9,10},{10,11},{12,13},{... | collective-permute-start | bytes 1966088 | tf_op jit(solution)/shard_map/ppermute | solution.py:653
  54.4 18.3 %copy-start.17 = (bf16[512,2048]{1,0:T(8,128)(2,1)S(1)}, bf16[512,2048]{1,0:T(8,128)(2,1)}, u32[]{:S(2)}) copy-start(bf16[512,2048]{1,0:T(8,128)(2,1)} %cotangent_ref.1) | copy-start | bytes 6291460
  68.5 31.6 %collective-permute-start.5 = (bf16[512,640]{1,0:T(8,128)(2,1)S(1)}, bf16[512,640]{1,0:T(8,128)(2,1)S(1)}, u32[]{:S(2)}, u32[]{:S(2)}) collective-permute-start(bf16[512,640]{1,0:T(8,128)(2,1)S(1)} %get-tuple-element.254), channel_id=1, source_target_pairs={{1,3},{2,0},{5,7},{6,4},{9,11},{10,8},{13,15},{14,12},{17,19},{18,... | collective-permute-start | bytes 1966088 | tf_op jit(solution)/shard_map/ppermute | solution.py:664
  69.8 32.0 %collective-permute-start.3 = (bf16[512,640]{1,0:T(8,128)(2,1)S(1)}, bf16[512,640]{1,0:T(8,128)(2,1)}, u32[]{:S(2)}, u32[]{:S(2)}) collective-permute-start(bf16[512,640]{1,0:T(8,128)(2,1)S(1)} %get-tuple-element.254), channel_id=1, source_target_pairs={{1,2},{2,1},{5,6},{6,5},{9,10},{10,9},{13,14},{14,13},{17,18},{18,... | collective-permute-start | bytes 1966088 | tf_op jit(solution)/shard_map/ppermute | solution.py:662
  71.3 28.8 %collective-permute-start.4 = (bf16[512,640]{1,0:T(8,128)(2,1)S(1)}, bf16[512,640]{1,0:T(8,128)(2,1)S(1)}, u32[]{:S(2)}, u32[]{:S(2)}) collective-permute-start(bf16[512,640]{1,0:T(8,128)(2,1)S(1)} %get-tuple-element.253), channel_id=1, source_target_pairs={{1,0},{2,3},{5,4},{6,7},{9,8},{10,11},{13,12},{14,15},{17,16},{18,... | collective-permute-start | bytes 1966088 | tf_op jit(solution)/shard_map/ppermute | solution.py:663
  127.8 19.4 %slice-start.2 = ((s8[6291456]{0:T(1024)(128)(4,1)}), s8[4194304]{0:T(1024)(128)(4,1)S(1)}, s32[]{:S(2)}) async-start(s8[6291456]{0:T(1024)(128)(4,1)} %bitcast.45), calls=%async_computation.8 | async-start | bytes 8388608
  153.3 27.9 %collective-permute-start.7 = (bf16[128,2048]{1,0:T(8,128)(2,1)}, bf16[128,2048]{1,0:T(8,128)(2,1)}, u32[]{:S(2)}, u32[]{:S(2)}) collective-permute-start(bf16[128,2048]{1,0:T(8,128)(2,1)} %get-tuple-element.252), channel_id=1, source_target_pairs={{3,2},{2,1},{7,6},{6,5},{11,10},{10,9},{15,14},{14,13},{19,18},{18... | collective-permute-start | bytes 1572872 | tf_op jit(solution)/shard_map/ppermute | solution.py:591
  154.8 26.4 %collective-permute-start.6 = (bf16[128,2048]{1,0:T(8,128)(2,1)}, bf16[128,2048]{1,0:T(8,128)(2,1)}, u32[]{:S(2)}, u32[]{:S(2)}) collective-permute-start(bf16[128,2048]{1,0:T(8,128)(2,1)} %get-tuple-element.252), channel_id=1, source_target_pairs={{0,1},{1,2},{4,5},{5,6},{8,9},{9,10},{12,13},{13,14},{16,17},{17,1... | collective-permute-start | bytes 1572872 | tf_op jit(solution)/shard_map/ppermute | solution.py:590
  158.8 22.4 %collective-permute-start.8 = (bf16[128,2048]{1,0:T(8,128)(2,1)}, bf16[128,2048]{1,0:T(8,128)(2,1)}, u32[]{:S(2)}, u32[]{:S(2)}) collective-permute-start(bf16[128,2048]{1,0:T(8,128)(2,1)} %get-tuple-element.251), channel_id=1, source_target_pairs={{0,2},{3,1},{4,6},{7,5},{8,10},{11,9},{12,14},{15,13},{16,18},{19,... | collective-permute-start | bytes 1572872 | tf_op jit(solution)/shard_map/ppermute | solution.py:592
  181.2 211.7 %reduce-scatter.5.cloned.1.call-start = ((), (), s32[]{:S(2)}) async-start(), calls=%async_computation.3 | async-start | bytes 9437184 | tf_op jit(solution)/shard_map/reduce_scatter | solution.py:936
  183.9 15.1 %collective-permute-start.9 = (bf16[128,2048]{1,0:T(8,128)(2,1)}, bf16[128,2048]{1,0:T(8,128)(2,1)S(1)}, u32[]{:S(2)}, u32[]{:S(2)}) collective-permute-start(bf16[128,2048]{1,0:T(8,128)(2,1)} %get-tuple-element.135), channel_id=1, source_target_pairs={{0,1},{1,2},{2,3},{4,5},{5,6},{6,7},{8,9},{9,10},{10,11},{12,13},{... | collective-permute-start | bytes 1572872 | tf_op jit(solution)/shard_map/ppermute | solution.py:649
  188.2 15.3 %collective-permute-start.10 = (bf16[128,2048]{1,0:T(8,128)(2,1)}, bf16[128,2048]{1,0:T(8,128)(2,1)S(1)}, u32[]{:S(2)}, u32[]{:S(2)}) collective-permute-start(bf16[128,2048]{1,0:T(8,128)(2,1)} %get-tuple-element.136), channel_id=1, source_target_pairs={{1,0},{2,1},{3,2},{5,4},{6,5},{7,6},{9,8},{10,9},{11,10},{13,12},{... | collective-permute-start | bytes 1572872 | tf_op jit(solution)/shard_map/ppermute | solution.py:649
  198.3 83.3 %copy-start.33 = (bf16[512,2048]{1,0:T(8,128)(2,1)}, bf16[512,2048]{1,0:T(8,128)(2,1)S(1)}, u32[]{:S(2)}) copy-start(bf16[512,2048]{1,0:T(8,128)(2,1)S(1)} %convolution_convert_fusion) | copy-start | bytes 6291460
  204.6 22.6 %copy-start.23 = (f32[128,2048]{1,0:T(8,128)}, f32[128,2048]{1,0:T(8,128)S(1)}, u32[]{:S(2)}) copy-start(f32[128,2048]{1,0:T(8,128)S(1)} %get-tuple-element.182.d_resid_ref) | copy-start | bytes 3145732
  204.6 13.4 %collective-permute-start.12 = (bf16[128,2048]{1,0:T(8,128)(2,1)S(1)}, bf16[128,2048]{1,0:T(8,128)(2,1)S(1)}, u32[]{:S(2)}, u32[]{:S(2)}) collective-permute-start(bf16[128,2048]{1,0:T(8,128)(2,1)S(1)} %get-tuple-element.139.own_ref), channel_id=1, source_target_pairs={{1,0},{2,1},{3,2},{5,4},{6,5},{7,6},{9,8},{10,9},{11,10},{13,12},{... | collective-permute-start | bytes 1572872 | tf_op jit(solution)/shard_map/ppermute | solution.py:653
  205.9 13.3 %collective-permute-start.11 = (bf16[128,2048]{1,0:T(8,128)(2,1)S(1)}, bf16[128,2048]{1,0:T(8,128)(2,1)S(1)}, u32[]{:S(2)}, u32[]{:S(2)}) collective-permute-start(bf16[128,2048]{1,0:T(8,128)(2,1)S(1)} %get-tuple-element.139.own_ref), channel_id=1, source_target_pairs={{0,1},{1,2},{2,3},{4,5},{5,6},{6,7},{8,9},{9,10},{10,11},{12,13},{... | collective-permute-start | bytes 1572872 | tf_op jit(solution)/shard_map/ppermute | solution.py:653
  219.3 30.0 %collective-permute-start.16 = (bf16[320,2048]{1,0:T(8,128)(2,1)S(1)}, bf16[320,2048]{1,0:T(8,128)(2,1)S(1)}, u32[]{:S(2)}, u32[]{:S(2)}) collective-permute-start(bf16[320,2048]{1,0:T(8,128)(2,1)S(1)} %slice.17), channel_id=1, source_target_pairs={{0,1},{3,2},{4,5},{7,6},{8,9},{11,10},{12,13},{15,14},{16,17},{19,... | collective-permute-start | bytes 3932168 | tf_op jit(solution)/shard_map/ppermute | solution.py:670
  223.9 23.1 %collective-permute-start.14 = (bf16[128,2048]{1,0:T(8,128)(2,1)S(1)}, bf16[128,2048]{1,0:T(8,128)(2,1)S(1)}, u32[]{:S(2)}, u32[]{:S(2)}) collective-permute-start(bf16[128,2048]{1,0:T(8,128)(2,1)S(1)} %get-tuple-element.257), channel_id=1, source_target_pairs={{1,0},{2,3},{5,4},{6,7},{9,8},{10,11},{13,12},{14,15},{17,16},{18,... | collective-permute-start | bytes 1572872 | tf_op jit(solution)/shard_map/ppermute | solution.py:663
  225.2 21.8 %collective-permute-start.15 = (bf16[128,2048]{1,0:T(8,128)(2,1)S(1)}, bf16[128,2048]{1,0:T(8,128)(2,1)S(1)}, u32[]{:S(2)}, u32[]{:S(2)}) collective-permute-start(bf16[128,2048]{1,0:T(8,128)(2,1)S(1)} %get-tuple-element.258), channel_id=1, source_target_pairs={{1,3},{2,0},{5,7},{6,4},{9,11},{10,8},{13,15},{14,12},{17,19},{18,... | collective-permute-start | bytes 1572872 | tf_op jit(solution)/shard_map/ppermute | solution.py:664
  226.5 20.5 %collective-permute-start.13 = (bf16[128,2048]{1,0:T(8,128)(2,1)S(1)}, bf16[128,2048]{1,0:T(8,128)(2,1)S(1)}, u32[]{:S(2)}, u32[]{:S(2)}) collective-permute-start(bf16[128,2048]{1,0:T(8,128)(2,1)S(1)} %get-tuple-element.258), channel_id=1, source_target_pairs={{1,2},{2,1},{5,6},{6,5},{9,10},{10,9},{13,14},{14,13},{17,18},{18,... | collective-permute-start | bytes 1572872 | tf_op jit(solution)/shard_map/ppermute | solution.py:662
  227.2 45.5 %copy-start.36 = (bf16[192,2048]{1,0:T(8,128)(2,1)}, bf16[192,2048]{1,0:T(8,128)(2,1)S(1)}, u32[]{:S(2)}) copy-start(bf16[192,2048]{1,0:T(8,128)(2,1)S(1)} %slice.16) | copy-start | bytes 2359300
  227.2 20.1 %copy-start.43 = (bf16[640,2048]{1,0:T(8,128)(2,1)S(1)}, bf16[640,2048]{1,0:T(8,128)(2,1)}, u32[]{:S(2)}) copy-start(bf16[640,2048]{1,0:T(8,128)(2,1)} %param.22) | copy-start | bytes 7864324
  249.9 31.7 %collective-permute-start.18 = (bf16[320,2048]{1,0:T(8,128)(2,1)S(1)}, bf16[320,2048]{1,0:T(8,128)(2,1)S(1)}, u32[]{:S(2)}, u32[]{:S(2)}) collective-permute-start(bf16[320,2048]{1,0:T(8,128)(2,1)S(1)} %fusion.11), channel_id=1, source_target_pairs={{1,2},{2,1},{5,6},{6,5},{9,10},{10,9},{13,14},{14,13},{17,18},{18,... | collective-permute-start | bytes 3932168 | tf_op jit(solution)/shard_map/ppermute | solution.py:670
  250.7 22.0 %collective-permute-start.17 = (bf16[192,2048]{1,0:T(8,128)(2,1)S(1)}, bf16[192,2048]{1,0:T(8,128)(2,1)S(1)}, u32[]{:S(2)}, u32[]{:S(2)}) collective-permute-start(bf16[192,2048]{1,0:T(8,128)(2,1)S(1)} %slice.16), channel_id=1, source_target_pairs={{0,1},{3,2},{4,5},{7,6},{8,9},{11,10},{12,13},{15,14},{16,17},{19,... | collective-permute-start | bytes 2359304 | tf_op jit(solution)/shard_map/ppermute | solution.py:670
  263.5 21.0 %copy-start.27 = (bf16[512,640]{1,0:T(8,128)(2,1)}, bf16[512,640]{1,0:T(8,128)(2,1)S(1)}, u32[]{:S(2)}) copy-start(bf16[512,640]{1,0:T(8,128)(2,1)S(1)} %get-tuple-element.148.refs_3_) | copy-start | bytes 1966084
  273.9 45.0 %collective-permute-start.24 = (bf16[192,2048]{1,0:T(8,128)(2,1)}, bf16[192,2048]{1,0:T(8,128)(2,1)}, u32[]{:S(2)}, u32[]{:S(2)}) collective-permute-start(bf16[192,2048]{1,0:T(8,128)(2,1)} %fusion.13), channel_id=1, source_target_pairs={{1,2},{2,1},{5,6},{6,5},{9,10},{10,9},{13,14},{14,13},{17,18},{18,... | collective-permute-start | bytes 2359304 | tf_op jit(solution)/shard_map/ppermute | solution.py:670
  283.1 4.6 %collective-permute-start.19 = (f32[8,640]{1,0:T(8,128)S(1)}, f32[8,640]{1,0:T(8,128)S(1)}, u32[]{:S(2)}, u32[]{:S(2)}) collective-permute-start(f32[8,640]{1,0:T(8,128)S(1)} %get-tuple-element.164), channel_id=1, source_target_pairs={{4,0},{8,4},{12,8},{16,12},{20,16},{24,20},{28,24},{5,1},{9,5},{13... | collective-permute-start | bytes 61448 | tf_op jit(solution)/shard_map/ppermute | solution.py:918
  286.4 34.2 %collective-permute-start.23 = (bf16[320,2048]{1,0:T(8,128)(2,1)}, bf16[320,2048]{1,0:T(8,128)(2,1)}, u32[]{:S(2)}, u32[]{:S(2)}) collective-permute-start(bf16[320,2048]{1,0:T(8,128)(2,1)} %fusion.12), channel_id=1, source_target_pairs={{2,3},{1,0},{6,7},{5,4},{10,11},{9,8},{14,15},{13,12},{18,19},{17,... | collective-permute-start | bytes 3932168 | tf_op jit(solution)/shard_map/ppermute | solution.py:670
  290.8 28.1 %collective-permute-start.22 = (bf16[128,2048]{1,0:T(8,128)(2,1)}, bf16[128,2048]{1,0:T(8,128)(2,1)}, u32[]{:S(2)}, u32[]{:S(2)}) collective-permute-start(bf16[128,2048]{1,0:T(8,128)(2,1)} %get-tuple-element.249), channel_id=1, source_target_pairs={{0,2},{3,1},{4,6},{7,5},{8,10},{11,9},{12,14},{15,13},{16,18},{19,... | collective-permute-start | bytes 1572872 | tf_op jit(solution)/shard_map/ppermute | solution.py:592
  297.6 21.3 %collective-permute-start.21 = (bf16[128,2048]{1,0:T(8,128)(2,1)}, bf16[128,2048]{1,0:T(8,128)(2,1)}, u32[]{:S(2)}, u32[]{:S(2)}) collective-permute-start(bf16[128,2048]{1,0:T(8,128)(2,1)} %get-tuple-element.250), channel_id=1, source_target_pairs={{3,2},{2,1},{7,6},{6,5},{11,10},{10,9},{15,14},{14,13},{19,18},{18... | collective-permute-start | bytes 1572872 | tf_op jit(solution)/shard_map/ppermute | solution.py:591
  299.1 21.5 %collective-permute-start.20 = (bf16[128,2048]{1,0:T(8,128)(2,1)}, bf16[128,2048]{1,0:T(8,128)(2,1)}, u32[]{:S(2)}, u32[]{:S(2)}) collective-permute-start(bf16[128,2048]{1,0:T(8,128)(2,1)} %get-tuple-element.250), channel_id=1, source_target_pairs={{0,1},{1,2},{4,5},{5,6},{8,9},{9,10},{12,13},{13,14},{16,17},{17,1... | collective-permute-start | bytes 1572872 | tf_op jit(solution)/shard_map/ppermute | solution.py:590
  323.2 16.5 %collective-permute-start.25 = (bf16[128,2048]{1,0:T(8,128)(2,1)}, bf16[128,2048]{1,0:T(8,128)(2,1)S(1)}, u32[]{:S(2)}, u32[]{:S(2)}) collective-permute-start(bf16[128,2048]{1,0:T(8,128)(2,1)} %get-tuple-element.180), channel_id=1, source_target_pairs={{0,1},{1,2},{2,3},{4,5},{5,6},{6,7},{8,9},{9,10},{10,11},{12,13},{... | collective-permute-start | bytes 1572872 | tf_op jit(solution)/shard_map/ppermute | solution.py:649
  328.1 17.0 %collective-permute-start.26 = (bf16[128,2048]{1,0:T(8,128)(2,1)}, bf16[128,2048]{1,0:T(8,128)(2,1)}, u32[]{:S(2)}, u32[]{:S(2)}) collective-permute-start(bf16[128,2048]{1,0:T(8,128)(2,1)} %get-tuple-element.181), channel_id=1, source_target_pairs={{1,0},{2,1},{3,2},{5,4},{6,5},{7,6},{9,8},{10,9},{11,10},{13,12},{... | collective-permute-start | bytes 1572872 | tf_op jit(solution)/shard_map/ppermute | solution.py:649
  332.3 30.3 %collective-permute-start.29 = (bf16[192,2048]{1,0:T(8,128)(2,1)}, bf16[192,2048]{1,0:T(8,128)(2,1)}, u32[]{:S(2)}, u32[]{:S(2)}) collective-permute-start(bf16[192,2048]{1,0:T(8,128)(2,1)} %fusion.14), channel_id=1, source_target_pairs={{2,3},{1,0},{6,7},{5,4},{10,11},{9,8},{14,15},{13,12},{18,19},{17,... | collective-permute-start | bytes 2359304 | tf_op jit(solution)/shard_map/ppermute | solution.py:670
  349.0 23.8 %collective-permute-start.28 = (bf16[128,2048]{1,0:T(8,128)(2,1)}, bf16[128,2048]{1,0:T(8,128)(2,1)S(1)}, u32[]{:S(2)}, u32[]{:S(2)}) collective-permute-start(bf16[128,2048]{1,0:T(8,128)(2,1)} %get-tuple-element.183), channel_id=1, source_target_pairs={{1,0},{2,1},{3,2},{5,4},{6,5},{7,6},{9,8},{10,9},{11,10},{13,12},{... | collective-permute-start | bytes 1572872 | tf_op jit(solution)/shard_map/ppermute | solution.py:653
  350.4 22.4 %collective-permute-start.27 = (bf16[128,2048]{1,0:T(8,128)(2,1)}, bf16[128,2048]{1,0:T(8,128)(2,1)S(1)}, u32[]{:S(2)}, u32[]{:S(2)}) collective-permute-start(bf16[128,2048]{1,0:T(8,128)(2,1)} %get-tuple-element.183), channel_id=1, source_target_pairs={{0,1},{1,2},{2,3},{4,5},{5,6},{6,7},{8,9},{9,10},{10,11},{12,13},{... | collective-permute-start | bytes 1572872 | tf_op jit(solution)/shard_map/ppermute | solution.py:653
  360.3 17.1 %collective-permute-start.34 = (f32[2,2048]{1,0:T(2,128)S(1)}, f32[2,2048]{1,0:T(2,128)S(1)}, u32[]{:S(2)}, u32[]{:S(2)}) collective-permute-start(f32[2,2048]{1,0:T(2,128)S(1)} %pad_maximum_fusion), channel_id=1, source_target_pairs={{0,2},{1,3},{2,0},{3,1},{4,6},{5,7},{6,4},{7,5},{8,10},{9,11},{10,... | collective-permute-start | bytes 49160 | tf_op jit(solution)/shard_map/ppermute | solution.py:561
  360.4 18.3 %collective-permute-start.35 = (f32[2,2048]{1,0:T(2,128)S(1)}, f32[2,2048]{1,0:T(2,128)S(1)}, u32[]{:S(2)}, u32[]{:S(2)}) collective-permute-start(f32[2,2048]{1,0:T(2,128)S(1)} %pad_maximum_fusion), channel_id=1, source_target_pairs={{0,3},{1,0},{2,1},{3,2},{4,7},{5,4},{6,5},{7,6},{8,11},{9,8},{10,9... | collective-permute-start | bytes 49160 | tf_op jit(solution)/shard_map/ppermute | solution.py:561
  362.5 16.2 %collective-permute-start.33 = (f32[2,2048]{1,0:T(2,128)S(1)}, f32[2,2048]{1,0:T(2,128)S(1)}, u32[]{:S(2)}, u32[]{:S(2)}) collective-permute-start(f32[2,2048]{1,0:T(2,128)S(1)} %pad_maximum_fusion), channel_id=1, source_target_pairs={{0,1},{1,2},{2,3},{3,0},{4,5},{5,6},{6,7},{7,4},{8,9},{9,10},{10,1... | collective-permute-start | bytes 49160 | tf_op jit(solution)/shard_map/ppermute | solution.py:561
  374.7 26.9 %collective-permute-start.32 = (bf16[128,2048]{1,0:T(8,128)(2,1)}, bf16[128,2048]{1,0:T(8,128)(2,1)}, u32[]{:S(2)}, u32[]{:S(2)}) collective-permute-start(bf16[128,2048]{1,0:T(8,128)(2,1)} %get-tuple-element.256), channel_id=1, source_target_pairs={{1,3},{2,0},{5,7},{6,4},{9,11},{10,8},{13,15},{14,12},{17,19},{18,... | collective-permute-start | bytes 1572872 | tf_op jit(solution)/shard_map/ppermute | solution.py:664
  375.9 25.7 %collective-permute-start.30 = (bf16[128,2048]{1,0:T(8,128)(2,1)}, bf16[128,2048]{1,0:T(8,128)(2,1)}, u32[]{:S(2)}, u32[]{:S(2)}) collective-permute-start(bf16[128,2048]{1,0:T(8,128)(2,1)} %get-tuple-element.256), channel_id=1, source_target_pairs={{1,2},{2,1},{5,6},{6,5},{9,10},{10,9},{13,14},{14,13},{17,18},{18,... | collective-permute-start | bytes 1572872 | tf_op jit(solution)/shard_map/ppermute | solution.py:662
  377.4 24.2 %collective-permute-start.31 = (bf16[128,2048]{1,0:T(8,128)(2,1)}, bf16[128,2048]{1,0:T(8,128)(2,1)}, u32[]{:S(2)}, u32[]{:S(2)}) collective-permute-start(bf16[128,2048]{1,0:T(8,128)(2,1)} %get-tuple-element.255), channel_id=1, source_target_pairs={{1,0},{2,3},{5,4},{6,7},{9,8},{10,11},{13,12},{14,15},{17,16},{18,... | collective-permute-start | bytes 1572872 | tf_op jit(solution)/shard_map/ppermute | solution.py:663
  (50 other events, 300.0 us)
Sparse Core Ops, SparseCore 0:
  12.4 35.1 all-gather.10
  49.5 62.3 all-gather.12
  181.4 127.2 reduce-scatter.2
  320.7 72.1 reduce-scatter.4
